TPU v7x, 32 devices: a whole 2x2x4 slice. The times are simulated.
32 devices in a mesh: dp: 4 (over z), seq: 2 (over y), mp: 4 (over x, core).
Axes of the slice: x: 2, y: 2, z: 4, core: 2. Of those that a mesh axis runs over, the one named last changes fastest.
Arguments:
- hidden_in: bfloat16 [4, 1024, 768], P('dp', 'seq', 'mp'), may hold values from -6 to 6
- cotangent: bfloat16 [4, 1024, 768], P('dp', 'seq', 'mp'), may hold values from -6 to 6
- attention_gain: float32 [768], replicated, may hold values from 0.1 to 1.9
- feedforward_gain: float32 [768], replicated, may hold values from 0.1 to 1.9
- qkv_weight: bfloat16 [768, 3, 768], P(None, None, 'mp'), may hold values from -0.21875 to 0.21875
- attention_out: bfloat16 [768, 768], P('mp'), may hold values from -0.75 to 0.75
- geglu_in: bfloat16 [768, 2, 1152], P(None, None, 'mp'), may hold values from -0.21875 to 0.21875
- geglu_out: bfloat16 [1152, 768], P('mp'), may hold values from -0.1875 to 0.1875
Outputs:
- layer_out: float32 [4, 1024, 768], P('dp', 'seq', 'mp')
- grad_input: float32 [4, 1024, 768], P('dp', 'seq', 'mp')
- grad_qkv: float32 [768, 3, 768], P(None, None, 'mp')
- grad_attention_out: float32 [768, 768], P('mp')
- grad_geglu_in: float32 [768, 2, 1152], P(None, None, 'mp')
- grad_geglu_out: float32 [1152, 768], P('mp')
- grad_attention_gain: float32 [768], P('mp')
- grad_feedforward_gain: float32 [768], P('mp')
All inputs are finite; a program needn't handle non-finite values.
Results may differ from a plain program's by a relative error of at most 0.018.
Values may be sent and summed in bfloat16 or wider, within the bound.
No kernel may reach another device: no remote copies, remote signals or barrier semaphores. Data moves between devices by JAX's collectives and lax.ppermute only.
A program may use at most 64 MiB of HBM per device.

v0:
```python
import math

import jax
import jax.numpy as jnp
from jax import lax
from jax.sharding import PartitionSpec as P

HEAD = 64
HALF = 64


def with_halo(block, sides, width):
    for axis, dim in sides:
        count = lax.axis_size(axis)
        forward = [(i, i + 1) for i in range(count - 1)]
        backward = [(target, source) for source, target in forward]
        low = lax.ppermute(
            lax.slice_in_dim(block, block.shape[dim] - width, None, axis=dim), axis, forward
        )
        high = lax.ppermute(lax.slice_in_dim(block, 0, width, axis=dim), axis, backward)
        block = jnp.concatenate([low, block, high], axis=dim)
    return block


def normalize(rows):
    center = rows - jnp.mean(rows, axis=-1, keepdims=True)
    inverse = lax.rsqrt(jnp.mean(center * center, axis=-1, keepdims=True) + 1e-05)
    return (center * inverse, inverse)


def frequencies(positions):
    inverse_freq = jnp.exp(
        jnp.arange(HEAD // 2).astype(jnp.float32) * (-2.0 * math.log(10000.0) / HEAD)
    )
    angles = positions[:, None] * inverse_freq[None, :]
    angles = jnp.concatenate([angles, angles], axis=-1)
    return (jnp.cos(angles), jnp.sin(angles))


def rotate(tensor, cosine, sine):
    halfway = HEAD // 2
    turned = jnp.concatenate([-tensor[..., halfway:], tensor[..., :halfway]], axis=-1)
    return tensor * cosine[:, None, :] + turned * sine[:, None, :]


def gelu_exact(value):
    return 0.5 * value * (1.0 + lax.erf(value * 0.7071067811865476))


def gelu_slope(value):
    return (
        0.5 * (1.0 + lax.erf(value * 0.7071067811865476))
        + value * jnp.exp(-0.5 * value * value) * 0.3989422804014327
    )


def windows(wide, tile):
    count = (wide.shape[1] - tile) // tile
    shape = (wide.shape[0], count, tile) + wide.shape[2:]
    lower = wide[:, : count * tile].reshape(shape)
    upper = wide[:, tile:].reshape(shape)
    return jnp.concatenate([lower, upper], axis=2)


def unwindow(grads, tile):
    rest = grads.shape[3:]
    shape = (grads.shape[0], grads.shape[1] * tile) + rest
    lower = grads[:, :, :tile].reshape(shape)
    upper = grads[:, :, tile:].reshape(shape)
    others = ((0, 0),) * len(rest)
    return jnp.pad(lower, ((0, 0), (0, tile)) + others) + jnp.pad(
        upper, ((0, 0), (tile, 0)) + others
    )


def band_mask(base, count, tile, total_length):
    query_off = jnp.arange(tile, dtype=jnp.int32)
    key_off = jnp.arange(2 * tile, dtype=jnp.int32) - HALF
    near = jnp.abs(query_off[:, None] - key_off[None, :]) <= HALF
    key_pos = (
        base
        - HALF
        + jnp.arange(count, dtype=jnp.int32)[:, None] * tile
        + jnp.arange(2 * tile, dtype=jnp.int32)[None, :]
    )
    inside = (key_pos >= 0) & (key_pos < total_length)
    return near[None] & inside[:, None, :]


def attend(queries, keys_wide, values_wide, allowed):
    batch, length, heads, size = queries.shape
    tile = 2 * HALF
    count = length // tile
    query_tiles = queries.reshape(batch, count, tile, heads, size)
    key_tiles = windows(keys_wide, tile)
    value_tiles = windows(values_wide, tile)
    scores = jnp.einsum(
        "snqhd,snkhd->snhqk", query_tiles, key_tiles, preferred_element_type=jnp.float32
    ) * HEAD ** (-0.5)
    scores = jnp.where(allowed[None, :, None], scores, -1e30)
    top = jnp.max(scores, axis=-1, keepdims=True)
    log_total = top + jnp.log(jnp.sum(jnp.exp(scores - top), axis=-1, keepdims=True))
    weights = jnp.exp(scores - log_total).astype(jnp.bfloat16)
    mixed = jnp.einsum(
        "snhqk,snkhd->snqhd", weights, value_tiles, preferred_element_type=jnp.float32
    ).astype(jnp.bfloat16)
    return (mixed.reshape(batch, length, heads, size), log_total)


def attend_back(queries, keys_wide, values_wide, allowed, log_total, mixed, grad_mixed):
    batch, length, heads, size = queries.shape
    tile = 2 * HALF
    count = length // tile
    query_tiles = queries.reshape(batch, count, tile, heads, size)
    key_tiles = windows(keys_wide, tile)
    value_tiles = windows(values_wide, tile)
    grad_tiles = grad_mixed.reshape(batch, count, tile, heads, size)
    again = jnp.einsum(
        "snqhd,snkhd->snhqk", query_tiles, key_tiles, preferred_element_type=jnp.float32
    ) * HEAD ** (-0.5)
    again = jnp.where(allowed[None, :, None], again, -1e30)
    probs = jnp.exp(again - log_total)
    delta = jnp.sum(grad_mixed.astype(jnp.float32) * mixed.astype(jnp.float32), axis=-1)
    delta = jnp.transpose(delta.reshape(batch, count, tile, heads), (0, 1, 3, 2))
    grad_value_tiles = jnp.einsum(
        "snhqk,snqhd->snkhd",
        probs.astype(jnp.bfloat16),
        grad_tiles,
        preferred_element_type=jnp.float32,
    )
    grad_probs = jnp.einsum(
        "snqhd,snkhd->snhqk", grad_tiles, value_tiles, preferred_element_type=jnp.float32
    )
    grad_scores = (probs * (grad_probs - delta[..., None]) * HEAD ** (-0.5)).astype(jnp.bfloat16)
    grad_queries = jnp.einsum(
        "snhqk,snkhd->snqhd", grad_scores, key_tiles, preferred_element_type=jnp.float32
    )
    grad_key_tiles = jnp.einsum(
        "snhqk,snqhd->snkhd", grad_scores, query_tiles, preferred_element_type=jnp.float32
    )
    return (
        grad_queries.reshape(batch, length, heads, size),
        unwindow(grad_key_tiles, tile),
        unwindow(grad_value_tiles, tile),
    )


def edge_rims(grad_packed, length):
    return jnp.concatenate([grad_packed[:, :HALF], grad_packed[:, HALF + length :]], axis=1)


def fold_rims(grad_packed, returned, length):
    lower_add = jnp.pad(returned[:, :HALF], ((0, 0), (0, length - HALF), (0, 0)))
    upper_add = jnp.pad(returned[:, 3 * HALF :], ((0, 0), (length - HALF, 0), (0, 0)))
    return grad_packed[:, HALF : HALF + length] + lower_add + upper_add


def body(
    hidden_in,
    cotangent,
    attention_gain,
    feedforward_gain,
    qkv_weight,
    attention_out,
    geglu_in,
    geglu_out,
):
    batch, length, share = hidden_in.shape
    width = share * lax.axis_size("mp")
    offset = lax.axis_index("mp") * share
    columns = qkv_weight.shape[2]
    heads = columns // HEAD
    span = length + 2 * HALF
    inputs_full, upstream_full = (
        lax.all_gather(hidden_in, "mp", axis=2, tiled=True),
        lax.all_gather(cotangent, "mp", axis=2, tiled=True),
    )
    normed_one, inverse_one = normalize(inputs_full.astype(jnp.float32))
    fed_one = (normed_one * attention_gain).astype(jnp.bfloat16)
    projected = jnp.einsum("std,dch->stch", fed_one, qkv_weight, preferred_element_type=jnp.float32)
    block_index = lax.axis_index("seq")
    total_length = length * lax.axis_size("seq")
    query_pos = block_index * length + jnp.arange(length, dtype=jnp.int32)
    cosine, sine = frequencies(query_pos.astype(jnp.float32))
    queries = rotate(projected[:, :, 0].reshape(batch, length, heads, HEAD), cosine, sine).astype(
        jnp.bfloat16
    )
    keys_own = rotate(projected[:, :, 1].reshape(batch, length, heads, HEAD), cosine, sine).astype(
        jnp.bfloat16
    )
    values_own = projected[:, :, 2].astype(jnp.bfloat16)
    packed = jnp.concatenate([keys_own.reshape(batch, length, columns), values_own], axis=2)
    widened = with_halo(packed, (("seq", 1),), HALF)
    keys_wide = widened[:, :, :columns].reshape(batch, span, heads, HEAD)
    values_wide = widened[:, :, columns:].reshape(batch, span, heads, HEAD)
    allowed = band_mask(block_index * length, length // (2 * HALF), 2 * HALF, total_length)
    mixed, log_total = attend(queries, keys_wide, values_wide, allowed)
    joined = mixed.reshape(batch, length, columns)
    attn_terms = jnp.einsum(
        "sqh,hd->sqd", joined, attention_out, preferred_element_type=jnp.float32
    )
    middle = hidden_in.astype(jnp.float32) + lax.psum_scatter(
        attn_terms, "mp", scatter_dimension=2, tiled=True
    )
    middle_full = lax.all_gather(middle, "mp", axis=2, tiled=True)
    normed_two, inverse_two = normalize(middle_full)
    fed_two = (normed_two * feedforward_gain).astype(jnp.bfloat16)
    lifted = jnp.einsum("std,dcf->stcf", fed_two, geglu_in, preferred_element_type=jnp.float32)
    linear = lifted[:, :, 0]
    gating = lifted[:, :, 1]
    activated = gelu_exact(linear)
    product = (activated * gating).astype(jnp.bfloat16)
    mlp_terms = jnp.einsum("stf,fd->std", product, geglu_out, preferred_element_type=jnp.float32)
    layer_out = middle + lax.psum_scatter(
        mlp_terms.astype(jnp.bfloat16), "mp", scatter_dimension=2, tiled=True
    ).astype(jnp.float32)
    grad_geglu_out = jnp.einsum(
        "stf,std->fd", product, upstream_full, preferred_element_type=jnp.float32
    )
    grad_product = jnp.einsum(
        "std,fd->stf", upstream_full, geglu_out, preferred_element_type=jnp.float32
    )
    grad_linear = grad_product * gating * gelu_slope(linear)
    grad_gating = grad_product * activated
    grad_lifted = jnp.stack([grad_linear, grad_gating], axis=2).astype(jnp.bfloat16)
    grad_geglu_in = jnp.einsum(
        "std,stcf->dcf", fed_two, grad_lifted, preferred_element_type=jnp.float32
    )
    fed_terms = jnp.einsum(
        "stcf,dcf->std", grad_lifted, geglu_in, preferred_element_type=jnp.float32
    )
    grad_fed_two = lax.psum_scatter(fed_terms, "mp", scatter_dimension=2, tiled=True)
    normed_two_own = lax.dynamic_slice_in_dim(normed_two, offset, share, 2)
    gain_two_own = lax.dynamic_slice_in_dim(feedforward_gain, offset, share, 0)
    grad_ff_gain = jnp.sum(grad_fed_two * normed_two_own, axis=(0, 1))
    dhat_two = grad_fed_two * gain_two_own
    first_two, second_two = lax.psum(
        (
            jnp.sum(dhat_two, axis=-1, keepdims=True),
            jnp.sum(dhat_two * normed_two_own, axis=-1, keepdims=True),
        ),
        "mp",
    )
    grad_middle = cotangent.astype(jnp.float32) + inverse_two * (
        dhat_two - first_two / width - normed_two_own * (second_two / width)
    )
    grad_middle_full = lax.all_gather(grad_middle.astype(jnp.bfloat16), "mp", axis=2, tiled=True)
    grad_attention_out = jnp.einsum(
        "sqh,sqd->hd", joined, grad_middle_full, preferred_element_type=jnp.float32
    )
    grad_mixed = jnp.einsum(
        "sqd,hd->sqh", grad_middle_full, attention_out, preferred_element_type=jnp.float32
    ).astype(jnp.bfloat16)
    grad_mixed = grad_mixed.reshape(batch, length, heads, HEAD)
    grad_queries, grad_keys_wide, grad_values_wide = attend_back(
        queries, keys_wide, values_wide, allowed, log_total, mixed, grad_mixed
    )
    grad_packed = jnp.concatenate(
        [
            grad_keys_wide.reshape(batch, span, columns),
            grad_values_wide.reshape(batch, span, columns),
        ],
        axis=2,
    )
    returned = with_halo(
        edge_rims(grad_packed, length).astype(jnp.bfloat16), (("seq", 1),), HALF
    ).astype(jnp.float32)
    grad_own = fold_rims(grad_packed, returned, length)
    grad_keys = rotate(grad_own[:, :, :columns].reshape(batch, length, heads, HEAD), cosine, -sine)
    grad_queries = rotate(grad_queries, cosine, -sine)
    grad_values = grad_own[:, :, columns:].reshape(batch, length, heads, HEAD)
    grad_projected = (
        jnp.stack([grad_queries, grad_keys, grad_values], axis=2)
        .reshape(batch, length, 3, columns)
        .astype(jnp.bfloat16)
    )
    grad_qkv = jnp.einsum(
        "std,stch->dch", fed_one, grad_projected, preferred_element_type=jnp.float32
    )
    one_terms = jnp.einsum(
        "stch,dch->std", grad_projected, qkv_weight, preferred_element_type=jnp.float32
    )
    grad_fed_one = lax.psum_scatter(
        one_terms.astype(jnp.bfloat16), "mp", scatter_dimension=2, tiled=True
    ).astype(jnp.float32)
    normed_one_own = lax.dynamic_slice_in_dim(normed_one, offset, share, 2)
    gain_one_own = lax.dynamic_slice_in_dim(attention_gain, offset, share, 0)
    grad_attn_gain = jnp.sum(grad_fed_one * normed_one_own, axis=(0, 1))
    dhat_one = grad_fed_one * gain_one_own
    first_one, second_one = lax.psum(
        (
            jnp.sum(dhat_one, axis=-1, keepdims=True),
            jnp.sum(dhat_one * normed_one_own, axis=-1, keepdims=True),
        ),
        "mp",
    )
    grad_input = grad_middle + inverse_one * (
        dhat_one - first_one / width - normed_one_own * (second_one / width)
    )
    local_grads = (
        grad_qkv,
        grad_attention_out,
        grad_geglu_in,
        grad_geglu_out,
        grad_attn_gain,
        grad_ff_gain,
    )
    summed = lax.psum(
        (
            local_grads[0],
            local_grads[1],
            local_grads[2],
            local_grads[3],
            local_grads[4],
            local_grads[5],
        ),
        ("dp", "seq"),
    )
    return (layer_out, grad_input, summed[0], summed[1], summed[2], summed[3], summed[4], summed[5])


def solution(mesh):
    in_specs = (
        P("dp", "seq", "mp"),
        P("dp", "seq", "mp"),
        P(),
        P(),
        P(None, None, "mp"),
        P("mp", None),
        P(None, None, "mp"),
        P("mp", None),
    )
    out_specs = (
        P("dp", "seq", "mp"),
        P("dp", "seq", "mp"),
        P(None, None, "mp"),
        P("mp", None),
        P(None, None, "mp"),
        P("mp", None),
        P("mp"),
        P("mp"),
    )
    return jax.shard_map(body, mesh=mesh, in_specs=in_specs, out_specs=out_specs, check_vma=False)
```

profile of v0, /device:TPU:0, one launch (start us, length us, event | category | flops | bytes accessed | tf_op | source)
XLA Modules:
  0.0 433.2 jit_solution(13001490404904794870)
XLA Ops:
  7.3 10.4 %all_gather.12 = bf16[1,512,768]{1,2,0:T(8,128)(2,1)S(1)} all-gather(bf16[1,512,192]{1,2,0:T(8,128)(2,1)} %param.8), channel_id=1, replica_groups=mesh['dp'=4,'seq'=2,'mp'=4] {'mp'}, dimensions={2}, use_global_device_ids=true | all-gather | bytes 983040 | tf_op jit(solution)/shard_map/all_gather | solution.py:175
  22.8 3.4 collective-permute-start
  37.7 2.7 copy.56
  42.3 43.4 %all-reduce.16.cloned.1.call-done = f32[1,512,768]{1,0,2:T(1,128)} async-done(((f32[1,512,768]{1,0,2:T(1,128)}), f32[1,512,768]{1,0,2:T(1,128)}) %all-reduce.16.cloned.1.call-update) | async-done | bytes 1572880
  87.9 8.6 %all_gather.14 = bf16[1,512,768]{1,2,0:T(8,128)(2,1)} all-gather(bf16[1,512,192]{1,2,0:T(8,128)(2,1)S(1)} %copy-done.12), channel_id=1, replica_groups=mesh['dp'=4,'seq'=2,'mp'=4] {'mp'}, dimensions={2}, use_global_device_ids=true | all-gather | bytes 983040 | tf_op jit(solution)/shard_map/all_gather | solution.py:176
  96.5 11.2 %all-gather.2.cloned.1.call-done = f32[1,512,768]{1,0,2:T(1,128)} async-done(((f32[1,512,192]{1,0,2:T(1,128)}), f32[1,512,768]{1,0,2:T(1,128)}) %all-gather.2.cloned.1.call-update) | async-done | bytes 1572880 | tf_op jit(solution)/shard_map/all_gather | solution.py:205
  107.7 2.4 reduce_sum.111
  117.8 4.8 %copy.60 = f32[1,512,768]{1,0,2:T(1,128)} copy(f32[1,512,768]{2,1,0:T(8,128)} %convolution_bitcast_fusion) | data formatting | bytes 3145728 | tf_op jit(solution)/shard_map/stcf,dcf->std/dot_general | solution.py:229
  123.6 2.9 fusion.6
  126.6 4.8 %copy.86 = bf16[1,512,768]{1,0,2:T(2,128)(2,1)} copy(bf16[1,512,768]{2,1,0:T(8,128)(2,1)} %fusion.6) | data formatting | bytes 1572864
  131.3 2.5 copy.151
  133.9 31.7 %all-reduce.18.cloned.1.call-done = f32[1,512,768]{1,0,2:T(1,128)} async-done(((f32[1,512,768]{1,0,2:T(1,128)}), f32[1,512,768]{1,0,2:T(1,128)}) %all-reduce.18.cloned.1.call-update) | async-done | bytes 1572880
  167.8 6.0 %all-reduce.11 = (f32[1,512,1]{1,2,0:T(1,128)S(1)}, f32[1,512,1]{1,2,0:T(1,128)S(1)}) all-reduce(f32[1,512,1]{1,2,0:T(1,128)S(1)} %bitcast.303, f32[1,512,1]{1,2,0:T(1,128)S(1)} %bitcast.304), channel_id=1, replica_groups=mesh['dp'=4,'seq'=2,'mp'=4] {'mp'}, use_global_device_ids=true, to_apply=%region_12.13 | all-reduce | flops 1024 | bytes 8192 | tf_op jit(solution)/shard_map/psum | solution.py:237
  175.0 8.3 %all_gather.15 = bf16[1,512,768]{1,2,0:T(8,128)(2,1)S(1)} all-gather(bf16[1,512,192]{1,2,0:T(8,128)(2,1)S(1)} %fusion.98), channel_id=1, replica_groups=mesh['dp'=4,'seq'=2,'mp'=4] {'mp'}, dimensions={2}, use_global_device_ids=true | all-gather | bytes 983040 | tf_op jit(solution)/shard_map/all_gather | solution.py:247
  193.4 3.4 collective-permute-start.2
  199.4 4.1 collective-permute-done.3
  207.9 4.8 %copy.88 = bf16[1,512,768]{1,0,2:T(2,128)(2,1)} copy(bf16[1,512,768]{2,1,0:T(8,128)(2,1)} %fusion.5) | data formatting | bytes 1572864
  212.6 2.5 copy.150
  215.2 2.9 fusion.16
  227.1 10.6 %reduce-scatter.9.cloned.1.call-done = bf16[192,512]{1,0:T(8,128)(2,1)} async-done(((bf16[768,512]{1,0:T(8,128)(2,1)}), bf16[192,512]{1,0:T(8,128)(2,1)}) %reduce-scatter.9.cloned.1.call-update) | async-done | bytes 196624
  240.0 22.6 %all-reduce.8 = (f32[192]{0:T(256)}, f32[192]{0:T(256)}) all-reduce(f32[192]{0:T(256)S(1)} %get-tuple-element.34, f32[192]{0:T(256)S(1)} %get-tuple-element.32), channel_id=1, replica_groups=mesh['dp'=4,'seq'=2,'mp'=4] {'dp','seq'}, use_global_device_ids=true, to_apply=%region_24.25 | all-reduce | flops 384 | bytes 3072 | tf_op jit(solution)/shard_map/psum | solution.py:308
  262.6 6.0 %all-reduce.10 = (f32[1,512,1]{1,2,0:T(1,128)S(1)}, f32[1,512,1]{1,2,0:T(1,128)S(1)}) all-reduce(f32[1,512,1]{1,2,0:T(1,128)S(1)} %bitcast.301, f32[1,512,1]{1,2,0:T(1,128)S(1)} %bitcast.302), channel_id=1, replica_groups=mesh['dp'=4,'seq'=2,'mp'=4] {'mp'}, use_global_device_ids=true, to_apply=%region_18.19 | all-reduce | flops 1024 | bytes 8192 | tf_op jit(solution)/shard_map/psum | solution.py:290
  270.7 149.2 %all-reduce.20.cloned.1.call-done = (f32[768,3,192]{0,2,1:T(8,128)}, f32[192,768]{1,0:T(8,128)}, f32[768,2,288]{0,2,1:T(8,128)}, f32[288,768]{1,0:T(8,128)}) async-done(((f32[768,3,192]{0,2,1:T(8,128)}, f32[192,768]{1,0:T(8,128)}, f32[768,2,288]{0,2,1:T(8,128)}, f32[288,768]{1,0:T(8,128)}), (f32[768,3,192]{0,2,1:T(8,128)}, f32[192,768]{1,0:T(8,128)}, f32[768,2,288]{0,2,1:T(8,128)}, ...) | async-done | bytes 5013520 | tf_op jit(solution)/shard_map/psum | solution.py:308
  419.9 2.9 copy.158
  (227 shorter events, 65.4 us)
Async XLA Ops:
  7.2 10.9 %copy-start = (bf16[768,3,192]{0,2,1:T(8,128)(2,1)S(1)}, bf16[768,3,192]{0,2,1:T(8,128)(2,1)}, u32[]{:S(2)}) copy-start(bf16[768,3,192]{0,2,1:T(8,128)(2,1)} %param.12) | copy-start | bytes 2654212
  7.2 10.9 %copy-start.47 = (f32[768]{0:T(1024)S(1)}, f32[768]{0:T(1024)}, u32[]{:S(2)}) copy-start(f32[768]{0:T(1024)} %param.10) | copy-start | bytes 9220
  7.2 78.5 %all-reduce.16.cloned.1.call-start = ((), (), s32[]{:S(2)}) async-start(), calls=%async_computation.5 | async-start | bytes 3145728
  22.8 9.8 %collective-permute-start = (bf16[1,64,384]{1,2,0:T(8,128)(2,1)}, bf16[1,64,384]{1,2,0:T(8,128)(2,1)S(1)}, u32[]{:S(2)}, u32[]{:S(2)}) collective-permute-start(bf16[1,64,384]{1,2,0:T(8,128)(2,1)} %get-tuple-element.71), channel_id=1, source_target_pairs={{0,4},{1,5},{2,6},{3,7},{8,12},{9,13},{10,14},{11,15},{16,20},{17,... | collective-permute-start | bytes 147464 | tf_op jit(solution)/shard_map/ppermute | solution.py:17
  26.2 6.8 %collective-permute-start.1 = (bf16[1,64,384]{1,2,0:T(8,128)(2,1)S(1)}, bf16[1,64,384]{1,2,0:T(8,128)(2,1)}, u32[]{:S(2)}, u32[]{:S(2)}) collective-permute-start(bf16[1,64,384]{1,2,0:T(8,128)(2,1)S(1)} %get-tuple-element.72), channel_id=1, source_target_pairs={{4,0},{5,1},{6,2},{7,3},{12,8},{13,9},{14,10},{15,11},{20,16},{21,... | collective-permute-start | bytes 147464 | tf_op jit(solution)/shard_map/ppermute | solution.py:20
  40.4 45.3 %copy-start.35 = (bf16[1,512,192]{1,2,0:T(8,128)(2,1)S(1)}, bf16[1,512,192]{1,2,0:T(8,128)(2,1)}, u32[]{:S(2)}) copy-start(bf16[1,512,192]{1,2,0:T(8,128)(2,1)} %param.8) | copy-start | bytes 589828
  40.4 47.5 %copy-start.12 = (bf16[1,512,192]{1,2,0:T(8,128)(2,1)S(1)}, bf16[1,512,192]{1,2,0:T(8,128)(2,1)}, u32[]{:S(2)}) copy-start(bf16[1,512,192]{1,2,0:T(8,128)(2,1)} %param.9) | copy-start | bytes 589828
  40.5 67.3 %all-gather.2.cloned.1.call-start = ((), (), s32[]{:S(2)}) async-start(), calls=%async_computation.2 | async-start | bytes 1966080 | tf_op jit(solution)/shard_map/all_gather | solution.py:205
  87.9 77.7 %all-reduce.18.cloned.1.call-start = ((), (), s32[]{:S(2)}) async-start(), calls=%async_computation.6 | async-start | bytes 3145728
  107.7 2.4 copy-start.3
  122.6 102.3 %reduce-scatter.7.cloned.1.call-start = ((), (), s32[]{:S(2)}) async-start(), calls=%async_computation.3 | async-start | bytes 983040
  133.8 40.0 %copy-start.13 = (bf16[1,512,192]{1,2,0:T(8,128)(2,1)S(1)}, bf16[1,512,192]{1,2,0:T(8,128)(2,1)}, u32[]{:S(2)}) copy-start(bf16[1,512,192]{1,2,0:T(8,128)(2,1)} %param.9) | copy-start | bytes 589828
  133.9 103.9 %reduce-scatter.9.cloned.1.call-start = ((), (), s32[]{:S(2)}) async-start(), calls=%async_computation.4 | async-start | bytes 983040
  173.8 10.4 %copy-start.21 = (bf16[192,768]{1,0:T(8,128)(2,1)S(1)}, bf16[192,768]{1,0:T(8,128)(2,1)}, u32[]{:S(2)}) copy-start(bf16[192,768]{1,0:T(8,128)(2,1)} %param.13) | copy-start | bytes 884740
  185.3 3.8 copy-start.26
  193.4 5.9 %collective-permute-start.2 = (bf16[1,64,384]{1,2,0:T(8,128)(2,1)S(1)}, bf16[1,64,384]{1,2,0:T(8,128)(2,1)S(1)}, u32[]{:S(2)}, u32[]{:S(2)}) collective-permute-start(bf16[1,64,384]{1,2,0:T(8,128)(2,1)S(1)} %get-tuple-element.53), channel_id=1, source_target_pairs={{0,4},{1,5},{2,6},{3,7},{8,12},{9,13},{10,14},{11,15},{16,20},{17,... | collective-permute-start | bytes 147464 | tf_op jit(solution)/shard_map/ppermute | solution.py:17
  196.8 6.7 %collective-permute-start.3 = (bf16[1,64,384]{1,2,0:T(8,128)(2,1)S(1)}, bf16[1,64,384]{1,2,0:T(8,128)(2,1)S(1)}, u32[]{:S(2)}, u32[]{:S(2)}) collective-permute-start(bf16[1,64,384]{1,2,0:T(8,128)(2,1)S(1)} %get-tuple-element.54), channel_id=1, source_target_pairs={{4,0},{5,1},{6,2},{7,3},{12,8},{13,9},{14,10},{15,11},{20,16},{21,... | collective-permute-start | bytes 147464 | tf_op jit(solution)/shard_map/ppermute | solution.py:20
  215.1 204.8 %all-reduce.20.cloned.1.call-start = ((), (), s32[]{:S(2)}) async-start(), calls=%async_computation.7 | async-start | bytes 10027008 | tf_op jit(solution)/shard_map/psum | solution.py:308
  215.2 2.9 copy-start.43
  215.2 2.9 copy-start.45
  224.9 43.8 %copy-start.8 = (f32[1,512,192]{1,0,2:T(1,128)S(1)}, f32[1,512,192]{1,0,2:T(1,128)}, u32[]{:S(2)}) copy-start(f32[1,512,192]{1,0,2:T(1,128)} %copy-done.7) | copy-start | bytes 1179652
  224.9 43.8 %copy-start.14 = (bf16[1,512,192]{1,2,0:T(8,128)(2,1)S(1)}, bf16[1,512,192]{1,2,0:T(8,128)(2,1)}, u32[]{:S(2)}) copy-start(bf16[1,512,192]{1,2,0:T(8,128)(2,1)} %param.9) | copy-start | bytes 589828
  419.9 3.0 copy-start.40
  419.9 3.8 copy-start.11
  (36 other events, 43.5 us)
Sparse Core Ops, SparseCore 0:
  40.6 45.0 all-reduce.15
  88.0 19.6 all-gather.1
  122.7 42.8 all-reduce.17
  168.0 23.2 reduce-scatter.6
  215.3 22.4 reduce-scatter.8
  242.1 177.7 all-reduce.19
where the time goes:
time: 434 us; the launch traced here: 433 us
  waiting for transfers between devices  251 us (58%)
  blocking collectives  61.9 us (14%)
  local copies, waits for them, and re-layouts  47.5 us (11%)
  other arithmetic  25.6 us (6%)
  matrix products  21.8 us (5%)
  between operations  15.6 us (4%)
  starting transfers between devices  9.63 us (2%)
    psum x1, waiting for transfers between devices, body(): lax.psum((local_grads[0], local_grads[1], local_grads[2], local_grads[3],...  149 us
    unnamed x10, waiting for transfers between devices  85.8 us
    unnamed x117, local copies, waits for them, and re-layouts  34.8 us
    psum x1, blocking collectives, body(): lax.psum((local_grads[0], local_grads[1], local_grads[2], local_grads[3],...  22.6 us
    all_gather x1, waiting for transfers between devices, body(): middle_full = lax.all_gather(middle, 'mp', axis=2, tiled=True)  11.2 us
    all_gather x1, blocking collectives, body(): lax.all_gather(hidden_in, 'mp', axis=2, tiled=True)  10.4 us
  transfers between devices with their start and end apart: 10, of which 8 were waited for; matrix products, arithmetic and copies ran while one was open for 13% of the time, Pallas kernels for 0%

commit v1 on v0

v1 whole, which is shorter than its diff:
```python
import functools
import math

import jax
import jax.numpy as jnp
from jax import lax
from jax.experimental import pallas as pl
from jax.experimental.pallas import tpu as pltpu
from jax.sharding import PartitionSpec as P

HEAD = 64
HALF = 64
TILE = 2 * HALF
STEP = 64
F32 = jnp.float32
BF16 = jnp.bfloat16


def call(kernel, outs, scratch, *args):
    return pl.pallas_call(
        kernel,
        out_shape=tuple(jax.ShapeDtypeStruct(s, t) for s, t in outs),
        scratch_shapes=[pltpu.VMEM(s, t) for s, t in scratch],
        compiler_params=pltpu.CompilerParams(vmem_limit_bytes=56 * 1024 * 1024),
    )(*args)


def nn(a, b):
    return lax.dot_general(a, b, (((1,), (0,)), ((), ())), preferred_element_type=F32)


def tn(a, b):
    return lax.dot_general(a, b, (((0,), (0,)), ((), ())), preferred_element_type=F32)


def nt(a, b):
    return lax.dot_general(a, b, (((1,), (1,)), ((), ())), preferred_element_type=F32)


def row_loop(rows, step, fn, init):
    def one(i, carry):
        return fn(pl.multiple_of(i * step, step), carry)

    return lax.fori_loop(0, rows // step, one, init)


def fold(x):
    return jnp.sum(x.reshape(x.shape[0] // 8, 8, x.shape[1]), axis=0)


def allowed_of(first, tile, total):
    shape = (2 * TILE, TILE)
    key = lax.broadcasted_iota(jnp.int32, shape, 0)
    query = lax.broadcasted_iota(jnp.int32, shape, 1)
    gap = key - query
    position = key + (first + tile * TILE - HALF)
    return (gap >= 0) & (gap <= TILE) & (position >= 0) & (position < total)


def gather_rows(pieces, target, lanes):
    me = lax.axis_index("mp")
    share = pieces[0].shape[0]
    for k, piece in enumerate(pieces):
        start = pl.multiple_of(jnp.bitwise_xor(me, k) * share, share)
        target[pl.ds(start, share), lanes] = piece[...]


def split_half(source, keep, send, index):
    rows = keep.shape[0]

    def one(r, carry):
        mine = pl.multiple_of(index * rows + r, 16)
        other = pl.multiple_of((1 - index) * rows + r, 16)
        keep[pl.ds(r, 16), :] = source[pl.ds(mine, 16), :]
        send[pl.ds(r, 16), :] = source[pl.ds(other, 16), :].astype(send.dtype)
        return carry

    row_loop(rows, 16, one, 0)


def split_shards(source, keep, send, core):
    share = keep.shape[1]
    for x in range(2):
        mine = pl.multiple_of((2 * x + core) * share, share)
        other = pl.multiple_of((2 * x + 1 - core) * share, share)
        keep[x] = source[pl.ds(mine, share), :]
        send[x] = source[pl.ds(other, share), :].astype(send.dtype)


def attention_kernel(
    p0, p1, p2, p3, h0, h1, h2, h3, gain, w, wo, cos, sin,
    xall, stats, fed, q, kw, vw, totals, mixed, keep, send,
    proj, terms,
):
    width, tokens = xall.shape
    length = q.shape[1]
    columns = q.shape[0]
    heads = columns // HEAD
    core = lax.axis_index("mp") % 2
    first = lax.axis_index("seq") * length
    total = lax.axis_size("seq") * length
    gather_rows((p0, p1, p2, p3), xall, slice(0, length))
    gather_rows((h0, h1, h2, h3), xall, slice(length, tokens))

    def add(r, acc):
        return acc + fold(xall[pl.ds(r, STEP), :].astype(F32))

    zero = jnp.zeros((8, tokens), F32)
    mean = jnp.sum(row_loop(width, STEP, add, zero), axis=0, keepdims=True) / width

    def add_square(r, acc):
        center = xall[pl.ds(r, STEP), :].astype(F32) - mean
        return acc + fold(center * center)

    var = jnp.sum(row_loop(width, STEP, add_square, zero), axis=0, keepdims=True) / width
    inverse = lax.rsqrt(var + 1e-05)
    stats[0:1, :] = mean
    stats[1:2, :] = inverse
    stats[2:8, :] = jnp.zeros((6, tokens), F32)

    def feed(r, carry):
        normed = (xall[pl.ds(r, STEP), :].astype(F32) - mean) * inverse
        fed[pl.ds(r, STEP), :] = (normed * gain[pl.ds(r, STEP), :]).astype(BF16)
        return carry

    row_loop(width, STEP, feed, 0)
    proj[...] = nn(w[...], fed[...])
    half = HEAD // 2

    def rope(row, lanes):
        a = proj[pl.ds(row, half), lanes]
        b = proj[pl.ds(row + half, half), lanes]
        c = cos[:, lanes]
        s = sin[:, lanes]
        return a * c - b * s, b * c + a * s

    def one_head(h, carry):
        row = pl.multiple_of(h * HEAD, HEAD)
        own = slice(0, length)
        every = slice(0, tokens)
        upper, lower = rope(row, own)
        q[pl.ds(row, half), :] = upper.astype(BF16)
        q[pl.ds(row + half, half), :] = lower.astype(BF16)
        upper, lower = rope(columns + row, every)
        kw[pl.ds(row, half), :] = pltpu.roll(upper, HALF, 1).astype(BF16)
        kw[pl.ds(row + half, half), :] = pltpu.roll(lower, HALF, 1).astype(BF16)
        value = proj[pl.ds(2 * columns + row, HEAD), :]
        vw[pl.ds(row, HEAD), :] = pltpu.roll(value, HALF, 1).astype(BF16)
        for j in range(length // TILE):
            wide = slice(j * TILE, (j + 2) * TILE)
            mine = slice(j * TILE, (j + 1) * TILE)
            scores = tn(kw[pl.ds(row, HEAD), wide], q[pl.ds(row, HEAD), mine]) * HEAD**-0.5
            scores = jnp.where(allowed_of(first, j, total), scores, -1e30)
            top = jnp.max(scores, axis=0, keepdims=True)
            log_total = top + jnp.log(jnp.sum(jnp.exp(scores - top), axis=0, keepdims=True))
            weights = jnp.exp(scores - log_total).astype(BF16)
            totals[h, 0:1, mine] = log_total
            mixed[pl.ds(row, HEAD), mine] = nn(vw[pl.ds(row, HEAD), wide], weights).astype(BF16)
        return carry

    lax.fori_loop(0, heads, one_head, 0)
    terms[...] = tn(wo[...], mixed[...])
    split_half(terms, keep, send, core)


def geglu_kernel(
    xall, mine, other, u0, u1, u2, u3, gain, win, gout,
    middle_own, normed, inverse_out, fed, upstream, product, lifted_grad, keep, send,
    middle, lifted, grad_product, terms,
):
    width, length = normed.shape
    share = middle_own.shape[0]
    units = product.shape[0]
    rows = mine.shape[0]
    me = lax.axis_index("mp")
    core = me % 2
    gather_rows((u0, u1, u2, u3), upstream, slice(0, length))
    own = slice(0, length)

    def add(r, acc):
        for part, index in ((mine, core), (other, 1 - core)):
            at = pl.multiple_of(index * rows + r, STEP)
            value = xall[pl.ds(at, STEP), own].astype(F32) + part[pl.ds(r, STEP), :].astype(F32)
            middle[pl.ds(at, STEP), :] = value
            acc = acc + fold(value)
        return acc

    zero = jnp.zeros((8, length), F32)
    mean = jnp.sum(row_loop(rows, STEP, add, zero), axis=0, keepdims=True) / width

    def add_square(r, acc):
        center = middle[pl.ds(r, STEP), :] - mean
        return acc + fold(center * center)

    var = jnp.sum(row_loop(width, STEP, add_square, zero), axis=0, keepdims=True) / width
    inverse = lax.rsqrt(var + 1e-05)
    inverse_out[...] = jnp.broadcast_to(inverse, inverse_out.shape)

    def feed(r, carry):
        value = (middle[pl.ds(r, STEP), :] - mean) * inverse
        normed[pl.ds(r, STEP), :] = value
        fed[pl.ds(r, STEP), :] = (value * gain[pl.ds(r, STEP), :]).astype(BF16)
        return carry

    row_loop(width, STEP, feed, 0)
    middle_own[...] = middle[pl.ds(pl.multiple_of(me * share, share), share), :]
    lifted[...] = nn(win[...], fed[...])
    grad_product[...] = nn(gout[...], upstream[...])

    def unit(r, carry):
        at = pl.ds(r, 32)
        gate = pl.ds(pl.multiple_of(units + r, 32), 32)
        linear = lifted[at, :]
        gating = lifted[gate, :]
        grad = grad_product[at, :]
        area = 0.5 * (1.0 + lax.erf(linear * 0.7071067811865476))
        activated = linear * area
        slope = area + linear * jnp.exp(-0.5 * linear * linear) * 0.3989422804014327
        product[at, :] = (activated * gating).astype(BF16)
        lifted_grad[at, :] = (grad * gating * slope).astype(BF16)
        lifted_grad[gate, :] = (grad * activated).astype(BF16)
        return carry

    row_loop(units, 32, unit, 0)
    terms[...] = tn(win[...], lifted_grad[...])
    split_half(terms, keep, send, core)


def geglu_weights_kernel(product, lifted_grad, fed, upstream, gout, *rest, cuts):
    outs, (terms, stack) = rest[:-2], rest[-2:]
    core = lax.axis_index("mp") % 2
    terms[...] = tn(gout[...], product[...])
    split_shards(terms, outs[0], outs[1], core)
    count = lifted_grad.shape[0]
    units = product.shape[0]
    stack[0:count, :] = nt(lifted_grad[...], fed[...])
    stack[count : count + units, :] = nt(product[...], upstream[...])
    if stack.shape[0] > count + units:
        stack[count + units :, :] = jnp.zeros((stack.shape[0] - count - units, stack.shape[1]), F32)
    emit_units(stack, outs[2:], cuts)


def emit_units(stack, outs, cuts):
    if cuts is None:
        outs[0][...] = stack[...]
        return
    seq = lax.axis_index("seq")
    start = 0
    for i, rows in enumerate(cuts):
        split_half(stack.at[pl.ds(start, rows), :], outs[2 * i], outs[2 * i + 1], seq)
        start += rows


def attention_back_kernel(
    mine, other, normed, inverse, gain, upstream, wo, q, kw, vw, totals, mixed, cos, sin, fed, *rest,
    cuts,
):
    outs, (full, low, mixed_grad, dk, dv, stack) = rest[:-6], rest[-6:]
    middle_grad_own, gain_grad, proj_grad = outs[:3]
    width, length = normed.shape
    columns = q.shape[0]
    heads = columns // HEAD
    tokens = kw.shape[1]
    rows = mine.shape[0]
    share = middle_grad_own.shape[0]
    me = lax.axis_index("mp")
    core = me % 2
    first = lax.axis_index("seq") * length
    total = lax.axis_size("seq") * length
    inv = inverse[0:1, :]

    def add(r, acc):
        a, b = acc
        for part, index in ((mine, core), (other, 1 - core)):
            at = pl.multiple_of(index * rows + r, STEP)
            grad = part[pl.ds(r, STEP), :].astype(F32)
            full[pl.ds(at, STEP), :] = grad
            hat = grad * gain[pl.ds(at, STEP), :]
            a = a + fold(hat)
            b = b + fold(hat * normed[pl.ds(at, STEP), :])
        return a, b

    zero = jnp.zeros((8, length), F32)
    a, b = row_loop(rows, STEP, add, (zero, zero))
    one = jnp.sum(a, axis=0, keepdims=True) / width
    two = jnp.sum(b, axis=0, keepdims=True) / width
    start = pl.multiple_of(me * share, share)
    weighted = full[pl.ds(start, share), :] * normed[pl.ds(start, share), :]
    lanes = weighted[:, 0:128]
    for j in range(1, length // 128):
        lanes = lanes + weighted[:, j * 128 : (j + 1) * 128]
    gain_grad[...] = lanes

    def back(r, carry):
        at = pl.ds(r, STEP)
        hat = full[at, :] * gain[at, :]
        value = upstream[at, :].astype(F32) + inv * (hat - one - normed[at, :] * two)
        full[at, :] = value
        low[at, :] = value.astype(BF16)
        return carry

    row_loop(width, STEP, back, 0)
    middle_grad_own[...] = full[pl.ds(start, share), :]
    mixed_grad[...] = nn(wo[...], low[...]).astype(BF16)
    dk[...] = jnp.zeros(dk.shape, F32)
    dv[...] = jnp.zeros(dv.shape, F32)
    half = HEAD // 2
    every = slice(0, tokens)

    def unrope(a, b, lanes):
        c = cos[:, lanes]
        s = sin[:, lanes]
        return a * c + b * s, b * c - a * s

    def one_head(h, carry):
        row = pl.multiple_of(h * HEAD, HEAD)
        head = pl.ds(row, HEAD)
        for j in range(length // TILE):
            wide = slice(j * TILE, (j + 2) * TILE)
            here = slice(j * TILE, (j + 1) * TILE)
            keys = kw[head, wide]
            query = q[head, here]
            grad = mixed_grad[head, here]
            scores = tn(keys, query) * HEAD**-0.5
            scores = jnp.where(allowed_of(first, j, total), scores, -1e30)
            probs = jnp.exp(scores - totals[h, 0:1, here])
            both = grad.astype(F32) * mixed[head, here].astype(F32)
            delta = jnp.sum(both, axis=0, keepdims=True)
            dv[head, wide] += nt(grad, probs.astype(BF16))
            grad_probs = tn(vw[head, wide], grad)
            grad_scores = (probs * (grad_probs - delta) * HEAD**-0.5).astype(BF16)
            dk[head, wide] += nt(query, grad_scores)
            dq = nn(keys, grad_scores)
            upper, lower = unrope(dq[:half], dq[half:], here)
            proj_grad[pl.ds(row, half), here] = upper.astype(BF16)
            proj_grad[pl.ds(row + half, half), here] = lower.astype(BF16)
        proj_grad[head, length:tokens] = jnp.zeros((HEAD, tokens - length), BF16)
        keys_grad = pltpu.roll(dk[head, :], tokens - HALF, 1)
        upper, lower = unrope(keys_grad[:half], keys_grad[half:], every)
        at = pl.multiple_of(columns + row, HEAD)
        proj_grad[pl.ds(at, half), :] = upper.astype(BF16)
        proj_grad[pl.ds(at + half, half), :] = lower.astype(BF16)
        at = pl.multiple_of(2 * columns + row, HEAD)
        proj_grad[pl.ds(at, HEAD), :] = pltpu.roll(dv[head, :], tokens - HALF, 1).astype(BF16)
        return carry

    lax.fori_loop(0, heads, one_head, 0)
    stack[0:columns, :] = nt(proj_grad[2 * columns : 3 * columns, :], fed[...])
    stack[columns : 2 * columns, :] = nt(mixed[...], low[...])
    stack[2 * columns : 4 * columns, :] = nt(proj_grad[0 : 2 * columns, :], fed[...])
    emit_units(stack, outs[3:], cuts)


def input_terms_kernel(proj_grad, w, gain, xall, stats, keep, send, sums, terms):
    width, tokens = terms.shape
    core = lax.axis_index("mp") % 2
    terms[...] = tn(w[...], proj_grad[...])
    mean = stats[0:1, :]
    inverse = stats[1:2, :]

    def add(r, acc):
        a, b = acc
        at = pl.ds(r, STEP)
        hat = terms[at, :] * gain[at, :]
        normed = (xall[at, :].astype(F32) - mean) * inverse
        return a + fold(hat), b + fold(hat * normed)

    zero = jnp.zeros((8, tokens), F32)
    a, b = row_loop(width, STEP, add, (zero, zero))
    sums[0:1, :] = jnp.sum(a, axis=0, keepdims=True) / width
    sums[1:2, :] = jnp.sum(b, axis=0, keepdims=True) / width
    sums[2:8, :] = jnp.zeros((6, tokens), F32)
    split_shards(terms, keep, send, core)


def quarters_kernel(keep, got, own, *sends):
    rows = own.shape[0]
    me = lax.axis_index("dp")
    for k, out in enumerate((own,) + sends):
        at = pl.ds(pl.multiple_of(jnp.bitwise_xor(me, k) * rows, 16), rows)
        out[...] = (keep[at, :] + got[at, :].astype(F32)).astype(out.dtype)


def join_kernel(*refs):
    pieces, out = refs[:-1], refs[-1]
    rows = pieces[0].shape[0]
    me = lax.axis_index("dp")
    for k, piece in enumerate(pieces):
        out[pl.ds(pl.multiple_of(jnp.bitwise_xor(me, k) * rows, 16), rows), :] = piece[...]


def place_kernel(*refs, cuts, outs):
    count = len(cuts)
    halves, targets, stack = refs[: 2 * count], refs[2 * count : -1], refs[-1]
    seq = lax.axis_index("seq")
    start = 0
    for i, rows in enumerate(cuts):
        size = rows // 2
        mine = pl.ds(pl.multiple_of(start + seq * size, 16), size)
        other = pl.ds(pl.multiple_of(start + (1 - seq) * size, 16), size)
        stack[mine, :] = halves[2 * i][...].astype(F32)
        stack[other, :] = halves[2 * i + 1][...].astype(F32)
        start += rows
    for target, spans in zip(targets, outs):
        at = 0
        for begin, size in spans:
            target[at : at + size, :] = stack[begin : begin + size, :]
            at += size


def flip(x, axis, bit):
    count = lax.axis_size(axis)
    return lax.ppermute(x, axis, [(i, i ^ bit) for i in range(count)])


def gather_mp(shard):
    across = flip(shard, "mp", 2)
    return shard, flip(shard, "mp", 1), across, flip(across, "mp", 1)


def sum_halves(keep, send):
    half = (keep + flip(send, "mp", 1).astype(F32)).astype(BF16)
    total = (half.astype(F32) + flip(half, "mp", 2).astype(F32)).astype(BF16)
    return total, flip(total, "mp", 1)


def scatter_shards(keep, send):
    x = lax.axis_index("mp") // 2
    half = keep + flip(send, "mp", 1).astype(F32)
    away = jnp.where(x == 0, half[1], half[0]).astype(BF16)
    return jnp.where(x == 0, half[0], half[1]) + flip(away, "mp", 2).astype(F32)


def reduce_unit(keep, send):
    rows, width = keep.shape
    count = lax.axis_size("dp")
    part = rows // count
    got = flip(send, "seq", 1)
    outs = [((part, width), F32)] + [((part, width), BF16)] * (count - 1)
    quarters = call(quarters_kernel, outs, [], keep, got)
    total = quarters[0]
    for k in range(1, count):
        total = total + flip(quarters[k], "dp", k).astype(F32)
    total = total.astype(BF16)
    pieces = [total] + [flip(total, "dp", k) for k in range(1, count)]
    (half,) = call(join_kernel, [((rows, width), BF16)], [], *pieces)
    return half, flip(half, "seq", 1)


def reduce_stack(parts, cuts, spans, width):
    sizes = [(sum(size for _, size in span), width) for span in spans]
    if cuts is None:
        total = lax.psum(parts[0], ("dp", "seq"))
        return [jnp.concatenate([total[b : b + n] for b, n in span]) for span in spans]
    halves = []
    for i in range(len(cuts)):
        halves.extend(reduce_unit(parts[2 * i], parts[2 * i + 1]))
    kernel = functools.partial(place_kernel, cuts=cuts, outs=spans)
    return call(
        kernel, [(size, F32) for size in sizes], [((sum(cuts), width), F32)], *halves
    )


def unit_shapes(cuts, rows, width):
    if cuts is None:
        return [((rows, width), F32)]
    shapes = []
    for size in cuts:
        shapes += [((size // 2, width), F32), ((size // 2, width), BF16)]
    return shapes


def body(
    hidden_in,
    cotangent,
    attention_gain,
    feedforward_gain,
    qkv_weight,
    attention_out,
    geglu_in,
    geglu_out,
):
    length, share = hidden_in.shape[1:]
    width = qkv_weight.shape[0]
    columns = qkv_weight.shape[2]
    units = geglu_out.shape[0]
    heads = columns // HEAD
    tokens = length + TILE
    half = width // 2
    dp, seqs = lax.axis_size("dp"), lax.axis_size("seq")
    staged = seqs == 2 and dp & (dp - 1) == 0
    grain = 2 * dp * 16
    x_own = hidden_in[0].T
    u_own = cotangent[0].T
    w = jnp.transpose(qkv_weight, (1, 2, 0)).reshape(3 * columns, width)
    win = jnp.transpose(geglu_in, (1, 2, 0)).reshape(2 * units, width)
    gain_one = attention_gain[:, None]
    gain_two = feedforward_gain[:, None]

    forward = [(i, i + 1) for i in range(seqs - 1)]
    backward = [(i + 1, i) for i in range(seqs - 1)]
    before = lax.ppermute(x_own[:, length - HALF :], "seq", forward)
    after = lax.ppermute(x_own[:, :HALF], "seq", backward)
    halo = jnp.concatenate([after, before], axis=1)
    x_parts = gather_mp(x_own)
    h_parts = gather_mp(halo)
    u_parts = gather_mp(u_own)

    base = (lax.axis_index("seq") * length).astype(jnp.int32)
    spot = jnp.arange(tokens, dtype=jnp.int32)
    spot = jnp.where(spot < length + HALF, spot, spot - tokens) + base
    rates = jnp.exp(jnp.arange(HEAD // 2).astype(F32) * (-2.0 * math.log(10000.0) / HEAD))
    angles = rates[:, None] * spot.astype(F32)[None, :]
    cos, sin = jnp.cos(angles), jnp.sin(angles)

    xall, stats, fed, q, kw, vw, totals, mixed, keep, send = call(
        attention_kernel,
        [
            ((width, tokens), BF16),
            ((8, tokens), F32),
            ((width, tokens), BF16),
            ((columns, length), BF16),
            ((columns, tokens), BF16),
            ((columns, tokens), BF16),
            ((heads, 8, length), F32),
            ((columns, length), BF16),
            ((half, length), F32),
            ((half, length), BF16),
        ],
        [((3 * columns, tokens), F32), ((width, length), F32)],
        *x_parts, *h_parts, gain_one, w, attention_out, cos, sin,
    )
    mine, other = sum_halves(keep, send)
    middle_own, normed, inverse, fed_two, upstream, product, lifted_grad, keep, send = call(
        geglu_kernel,
        [
            ((share, length), F32),
            ((width, length), F32),
            ((8, length), F32),
            ((width, length), BF16),
            ((width, length), BF16),
            ((units, length), BF16),
            ((2 * units, length), BF16),
            ((half, length), F32),
            ((half, length), BF16),
        ],
        [
            ((width, length), F32),
            ((2 * units, length), F32),
            ((units, length), F32),
            ((width, length), F32),
        ],
        xall, mine, other, *u_parts, gain_two, win, geglu_out,
    )
    mine, other = sum_halves(keep, send)

    rows = 3 * units
    padded = -(-rows // grain) * grain if staged else rows
    large = -(-padded // (2 * grain)) * grain
    geglu_cuts = (large, padded - large) if staged else None
    shard_shapes = [((2, share, length), F32), ((2, share, length), BF16)]
    outs = call(
        functools.partial(geglu_weights_kernel, cuts=geglu_cuts),
        shard_shapes + unit_shapes(geglu_cuts, padded, width),
        [((width, length), F32), ((padded, width), F32)],
        product, lifted_grad, fed_two, upstream, geglu_out,
    )
    layer_out = middle_own + scatter_shards(outs[0], outs[1])
    grad_in, grad_out = reduce_stack(
        outs[2:], geglu_cuts, (((0, 2 * units),), ((2 * units, units),)), width
    )

    back_cuts = (2 * columns, 2 * columns) if staged and 2 * columns % grain == 0 else None
    outs = call(
        functools.partial(attention_back_kernel, cuts=back_cuts),
        [((share, length), F32), ((share, 128), F32), ((3 * columns, tokens), BF16)]
        + unit_shapes(back_cuts, 4 * columns, width),
        [
            ((width, length), F32),
            ((width, length), BF16),
            ((columns, length), BF16),
            ((columns, tokens), F32),
            ((columns, tokens), F32),
            ((4 * columns, width), F32),
        ],
        mine, other, normed, inverse, gain_two, upstream, attention_out,
        q, kw, vw, totals, mixed, cos, sin, fed,
    )
    middle_grad, gain_two_lanes, proj_grad = outs[:3]
    grad_qkv, grad_attention_out = reduce_stack(
        outs[3:],
        back_cuts,
        (((2 * columns, 2 * columns), (0, columns)), ((columns, columns),)),
        width,
    )

    keep, send, sums = call(
        input_terms_kernel,
        [((2, share, tokens), F32), ((2, share, tokens), BF16), ((8, tokens), F32)],
        [((width, tokens), F32)],
        proj_grad, w, gain_one, xall, stats,
    )
    grad_one = scatter_shards(keep, send)
    sums = sums + flip(sums, "mp", 1)
    sums = sums + flip(sums, "mp", 2)
    offset = lax.axis_index("mp") * share
    x_all_own = lax.dynamic_slice_in_dim(xall, offset, share, 0).astype(F32)
    normed_own = (x_all_own - stats[0:1]) * stats[1:2]
    gain_one_grad = jnp.sum(grad_one * normed_own, axis=1)
    gain_two_grad = jnp.sum(gain_two_lanes, axis=1)
    gains = lax.psum(jnp.stack([gain_one_grad, gain_two_grad]), ("dp", "seq"))
    both = jnp.concatenate([grad_one, sums], axis=0)
    low_add = lax.ppermute(both[:, length : length + HALF], "seq", forward)
    high_add = lax.ppermute(both[:, length + HALF :], "seq", backward)
    both = jnp.concatenate(
        [
            both[:, :HALF] + low_add,
            both[:, HALF : length - HALF],
            both[:, length - HALF : length] + high_add,
        ],
        axis=1,
    )
    hat = both[:share] * lax.dynamic_slice_in_dim(gain_one, offset, share, 0)
    grad_input = middle_grad + stats[1:2, :length] * (
        hat - both[share : share + 1] - normed_own[:, :length] * both[share + 1 : share + 2]
    )
    return (
        layer_out.T[None],
        grad_input.T[None],
        jnp.transpose(grad_qkv.reshape(3, columns, width), (2, 0, 1)),
        grad_attention_out,
        jnp.transpose(grad_in.reshape(2, units, width), (2, 0, 1)),
        grad_out,
        gains[0],
        gains[1],
    )


def solution(mesh):
    in_specs = (
        P("dp", "seq", "mp"),
        P("dp", "seq", "mp"),
        P(),
        P(),
        P(None, None, "mp"),
        P("mp", None),
        P(None, None, "mp"),
        P("mp", None),
    )
    out_specs = (
        P("dp", "seq", "mp"),
        P("dp", "seq", "mp"),
        P(None, None, "mp"),
        P("mp", None),
        P(None, None, "mp"),
        P("mp", None),
        P("mp"),
        P("mp"),
    )
    return jax.shard_map(body, mesh=mesh, in_specs=in_specs, out_specs=out_specs, check_vma=False)
```

time: 434 us -> 232 us (0.53)
  waiting for transfers between devices: 251 us -> 63.8 us
  Pallas kernels: 0 us -> 63 us
  starting transfers between devices: 9.63 us -> 62.7 us
  blocking collectives: 61.9 us -> 19.9 us
  local copies, waits for them, and re-layouts: 47.5 us -> 11.6 us
  matrix products: 21.8 us -> 0 us
  other arithmetic: 25.6 us -> 8.97 us
  between operations: 15.6 us -> 1.32 us
    psum x1 -> x0, waiting for transfers between devices: 149 us -> none  [body(): lax.psum((local_grads[0], local_grads[1], local_grads[2], local_grads[3],...]
    unnamed x10 -> x0, waiting for transfers between devices: 85.8 us -> none
    pallas_call x0 -> x15, Pallas kernels: none -> 63 us  [call(): pl.pallas_call(kernel, out_shape=tuple((jax.ShapeDtypeStruct(s, t) for s,...]
    ppermute x4 -> x57, waiting for transfers between devices: 4.88 us -> 63.8 us  [the longest x53 55.3 us: flip(): return lax.ppermute(x, axis, [(i, i ^ bit) for i in range(count)])]
    ppermute x4 -> x57, starting transfers between devices: 9.38 us -> 62.7 us  [the longest x53 54.3 us: flip(): return lax.ppermute(x, axis, [(i, i ^ bit) for i in range(count)])]
    unnamed x117 -> x104, local copies, waits for them, and re-layouts: 34.8 us -> 5.25 us
    all_gather x3 -> x0, blocking collectives: 27.3 us -> none  [the longest x1 10.4 us: body(): lax.all_gather(hidden_in, 'mp', axis=2, tiled=True)]
    dot_general x16 -> x0, matrix products: 19.2 us -> none  [the longest x1 2.92 us: body(): jnp.einsum('stf,std->fd', product, upstream_full, preferred_element_type=...]
  transfers between devices with their start and end apart: 10 -> 57, of which waited for: 8 -> 20; matrix products, arithmetic and copies ran while one was open for 13% -> 4% of each run, Pallas kernels for 0% -> 19%
where the time goes in v1:
time: 232 us; the launch traced here: 231 us
  waiting for transfers between devices  63.8 us (28%)
  Pallas kernels  63 us (27%)
  starting transfers between devices  62.7 us (27%)
  blocking collectives  19.9 us (9%)
  local copies, waits for them, and re-layouts  11.6 us (5%)
  other arithmetic  8.97 us (4%)
    pallas_call x15, Pallas kernels, call(): pl.pallas_call(kernel, out_shape=tuple((jax.ShapeDtypeStruct(s, t) for s,...  63 us
    ppermute x53, waiting for transfers between devices, flip(): return lax.ppermute(x, axis, [(i, i ^ bit) for i in range(count)])  55.3 us
    ppermute x53, starting transfers between devices, flip(): return lax.ppermute(x, axis, [(i, i ^ bit) for i in range(count)])  54.3 us
    psum x1, blocking collectives, body(): gains = lax.psum(jnp.stack([gain_one_grad, gain_two_grad]), ('dp', 'seq'))  19.9 us
    unnamed x104, local copies, waits for them, and re-layouts  5.25 us
    ppermute x1, waiting for transfers between devices, body(): high_add = lax.ppermute(both[:, length + HALF:], 'seq', backward)  5.11 us
  transfers between devices with their start and end apart: 57, of which 20 were waited for; matrix products, arithmetic and copies ran while one was open for 4% of the time, Pallas kernels for 19%

profile of v1, /device:TPU:0, one launch (start us, length us, event | category | flops | bytes accessed | tf_op | source)
XLA Modules:
  0.0 231.3 jit_solution(701710569946947116)
XLA Ops:
  0.6 3.0 %collective-permute-start.1 = (bf16[192,512]{1,0:T(8,128)(2,1)}, bf16[192,512]{1,0:T(8,128)(2,1)S(1)}, u32[]{:S(2)}, u32[]{:S(2)}) collective-permute-start(bf16[192,512]{1,0:T(8,128)(2,1)} %bitcast.49), channel_id=1, source_target_pairs={{0,2},{1,3},{2,0},{3,1},{4,6},{5,7},{6,4},{7,5},{8,10},{9,11},{10,... | collective-permute-start | bytes 589832 | tf_op jit(solution)/shard_map/ppermute | solution.py:413
  5.9 4.5 %collective-permute-start.4 = (bf16[192,64]{1,0:T(8,128)(2,1)S(1)}, bf16[192,64]{1,0:T(8,128)(2,1)S(1)}, u32[]{:S(2)}, u32[]{:S(2)}) collective-permute-start(bf16[192,64]{1,0:T(8,128)(2,1)S(1)} %get-tuple-element.128), channel_id=1, source_target_pairs={{0,4},{1,5},{2,6},{3,7},{8,12},{9,13},{10,14},{11,15},{16,20},{17,... | collective-permute-start | bytes 73736 | tf_op jit(solution)/shard_map/ppermute | solution.py:502
  12.4 4.0 %collective-permute-done.6.h2 = bf16[192,128]{1,0:T(8,128)(2,1)S(1)} collective-permute-done((bf16[192,128]{1,0:T(8,128)(2,1)S(1)}, bf16[192,128]{1,0:T(8,128)(2,1)S(1)}, u32[]{:S(2)}, u32[]{:S(2)}) %collective-permute-start.6) | collective-permute-done | bytes 49184 | tf_op jit(solution)/shard_map/ppermute | solution.py:413
  20.4 10.9 %shard_map.143 = (bf16[768,640]{1,0:T(8,128)(2,1)}, f32[8,640]{1,0:T(8,128)}, bf16[768,640]{1,0:T(8,128)(2,1)}, bf16[192,512]{1,0:T(8,128)(2,1)}, bf16[192,640]{...) custom-call(bf16[192,512]{1,0:T(8,128)(2,1)} %bitcast.52, ...), custom_call_target="tpu_custom_call" | custom-call | tf_op jit(solution)/shard_map/pallas_call | solution.py:20
  36.6 10.0 %collective-permute-done.9 = bf16[384,512]{1,0:T(8,128)(2,1)S(1)} collective-permute-done((bf16[384,512]{1,0:T(8,128)(2,1)S(1)}, bf16[384,512]{1,0:T(8,128)(2,1)S(1)}, u32[]{:S(2)}, u32[]{:S(2)}) %collective-permute-start.9) | collective-permute-done | bytes 393248 | tf_op jit(solution)/shard_map/ppermute | solution.py:413
  47.2 2.7 %collective-permute-done.12.u2 = bf16[192,512]{1,0:T(8,128)(2,1)S(1)} collective-permute-done((bf16[192,512]{1,0:T(8,128)(2,1)S(1)}, bf16[192,512]{1,0:T(8,128)(2,1)S(1)}, u32[]{:S(2)}, u32[]{:S(2)}) %collective-permute-start.12) | collective-permute-done | bytes 196640 | tf_op jit(solution)/shard_map/ppermute | solution.py:413
  52.2 8.5 %shard_map.144 = (f32[192,512]{1,0:T(8,128)}, f32[768,512]{1,0:T(8,128)}, f32[8,512]{1,0:T(8,128)}, bf16[768,512]{1,0:T(8,128)(2,1)}, bf16[768,512]{1,0:T(8,128)...) custom-call(bf16[768,640]{1,0:T(8,128)(2,1)} %get-tuple-element.63.x, ...), custom_call_target="tpu_custom_call" | custom-call | tf_op jit(solution)/shard_map/pallas_call | solution.py:20
  64.3 5.2 %shard_map.145 = (f32[2,192,512]{2,1,0:T(8,128)}, bf16[2,192,512]{2,1,0:T(8,128)(2,1)}, f32[256,768]{1,0:T(8,128)}, bf16[256,768]{1,0:T(8,128)(2,1)}, f32[192,768]{1,0:T(8,128)}, /*index=5*/bf16[192,768]{1,0:T(8,128)(2,1)}) custom-call(bf16[288,512]{1,0:T(8,128)(2,1)} %get-tuple-element.67.product, bf16[576,512]{1,0:T(8,128)(2,1)} %get-tuple-element.68.lifted_grad, ...), custom_call_target="tpu_custom_call" | custom-call | tf_op jit(solution)/shard_map/pallas_call | solution.py:20
  71.9 3.2 %collective-permute-done.17 = bf16[384,512]{1,0:T(8,128)(2,1)S(1)} collective-permute-done((bf16[384,512]{1,0:T(8,128)(2,1)S(1)}, bf16[384,512]{1,0:T(8,128)(2,1)S(1)}, u32[]{:S(2)}, u32[]{:S(2)}) %collective-permute-start.17) | collective-permute-done | bytes 393248 | tf_op jit(solution)/shard_map/ppermute | solution.py:413
  76.9 3.0 %collective-permute-done.49.got = bf16[192,768]{1,0:T(8,128)(2,1)S(1)} collective-permute-done((bf16[192,768]{1,0:T(8,128)(2,1)}, bf16[192,768]{1,0:T(8,128)(2,1)S(1)}, u32[]{:S(2)}, u32[]{:S(2)}) %collective-permute-start.49) | collective-permute-done | bytes 294944 | tf_op jit(solution)/shard_map/ppermute | solution.py:413
  93.8 11.9 %shard_map.146 = (f32[192,512]{1,0:T(8,128)}, f32[192,128]{1,0:T(8,128)}, bf16[576,640]{1,0:T(8,128)(2,1)}, f32[192,768]{1,0:T(8,128)}, bf16[192,768]{1,0:T(8,12...) custom-call(bf16[384,512]{1,0:T(8,128)(2,1)} %copy-done, bf16[384,512]{1,0:T(8,128)(2,1)} %copy-done.4, ...), custom_call_target="tpu_custom_call" | custom-call | tf_op jit(solution)/shard_map/pallas_call | solution.py:20
  105.8 2.7 %collective-permute-start.43 = (bf16[64,768]{1,0:T(8,128)(2,1)S(1)}, bf16[64,768]{1,0:T(8,128)(2,1)S(1)}, u32[]{:S(2)}, u32[]{:S(2)}) collective-permute-start(bf16[64,768]{1,0:T(8,128)(2,1)S(1)} %copy-done.51), channel_id=1, source_target_pairs={{0,16},{8,24},{16,0},{24,8},{1,17},{9,25},{17,1},{25,9},{2,18},{10... | collective-permute-start | bytes 294920 | tf_op jit(solution)/shard_map/ppermute | solution.py:413
  110.6 4.8 %collective-permute-done.43 = bf16[64,768]{1,0:T(8,128)(2,1)S(1)} collective-permute-done((bf16[64,768]{1,0:T(8,128)(2,1)S(1)}, bf16[64,768]{1,0:T(8,128)(2,1)S(1)}, u32[]{:S(2)}, u32[]{:S(2)}) %collective-permute-start.43) | collective-permute-done | bytes 98336 | tf_op jit(solution)/shard_map/ppermute | solution.py:413
  116.2 3.4 %collective-permute-start.54 = (bf16[48,768]{1,0:T(8,128)(2,1)S(1)}, bf16[48,768]{1,0:T(8,128)(2,1)S(1)}, u32[]{:S(2)}, u32[]{:S(2)}) collective-permute-start(bf16[48,768]{1,0:T(8,128)(2,1)S(1)} %add_convert_fusion.5.refs_0_), channel_id=1, source_target_pairs={{0,16},{8,24},{16,0},{24,8},{1,17},{9,25},{17,1},{25,9},{2,18},{10... | collective-permute-start | bytes 221192 | tf_op jit(solution)/shard_map/ppermute | solution.py:413
  119.7 2.7 %collective-permute-start.55 = (bf16[48,768]{1,0:T(8,128)(2,1)S(1)}, bf16[48,768]{1,0:T(8,128)(2,1)S(1)}, u32[]{:S(2)}, u32[]{:S(2)}) collective-permute-start(bf16[48,768]{1,0:T(8,128)(2,1)S(1)} %add_convert_fusion.5.refs_0_), channel_id=1, source_target_pairs={{0,24},{8,16},{16,8},{24,0},{1,25},{9,17},{17,9},{25,1},{2,26},{10... | collective-permute-start | bytes 221192 | tf_op jit(solution)/shard_map/ppermute | solution.py:413
  128.9 5.4 %shard_map.147 = (f32[2,192,640]{2,1,0:T(8,128)}, bf16[2,192,640]{2,1,0:T(8,128)(2,1)}, f32[8,640]{1,0:T(8,128)}) custom-call(bf16[576,640]{1,0:T(8,128)(2,1)} %get-tuple-element.85.proj_grad, bf16[576,768]{1,0:T(8,128)(2,1)} %bitcast.47, f32[768,1]{1,0:T(8,128)} %broadcast_in_dim.18.gain, bf16[768,640]{1,0:T(8,128)(2,1)} %get-tuple-element.63.xall, ...), custom_call_target="tpu_custom_call" | custom-call | tf_op jit(solution)/shard_map/pallas_call | solution.py:20
  144.5 5.7 %collective-permute-done.27 = bf16[48,768]{1,0:T(8,128)(2,1)S(1)} collective-permute-done((bf16[48,768]{1,0:T(8,128)(2,1)}, bf16[48,768]{1,0:T(8,128)(2,1)S(1)}, u32[]{:S(2)}, u32[]{:S(2)}) %collective-permute-start.27) | collective-permute-done | bytes 73760 | tf_op jit(solution)/shard_map/ppermute | solution.py:413
  174.3 3.1 %collective-permute-done.56.refs_3_ = bf16[192,768]{1,0:T(8,128)(2,1)S(1)} collective-permute-done((bf16[192,768]{1,0:T(8,128)(2,1)}, bf16[192,768]{1,0:T(8,128)(2,1)S(1)}, u32[]{:S(2)}, u32[]{:S(2)}) %collective-permute-start.56) | collective-permute-done | bytes 294944 | tf_op jit(solution)/shard_map/ppermute | solution.py:413
  178.8 7.0 %collective-permute-done.48.refs_1_ = bf16[256,768]{1,0:T(8,128)(2,1)S(1)} collective-permute-done((bf16[256,768]{1,0:T(8,128)(2,1)}, bf16[256,768]{1,0:T(8,128)(2,1)S(1)}, u32[]{:S(2)}, u32[]{:S(2)}) %collective-permute-start.48) | collective-permute-done | bytes 393248 | tf_op jit(solution)/shard_map/ppermute | solution.py:413
  186.6 3.1 %shard_map.157 = (f32[576,768]{1,0:T(8,128)}, f32[288,768]{1,0:T(8,128)}) custom-call(bf16[256,768]{1,0:T(8,128)(2,1)} %shard_map.154.refs_0_, bf16[256,768]{1,0:T(8,128)(2,1)} %copy-done.9, bf16[192,768]{1,0:T(8,128)(2,1)} %shard_map.156.refs_2_, bf16[192,768]{1,0:T(8,128)(2,1)} %copy-done.18), custom_call_target="tpu_custom_call" | custom-call | tf_op jit(solution)/shard_map/pallas_call | solution.py:20
  191.9 3.2 %collective-permute-done.32.refs_1_ = bf16[192,768]{1,0:T(8,128)(2,1)S(1)} collective-permute-done((bf16[192,768]{1,0:T(8,128)(2,1)}, bf16[192,768]{1,0:T(8,128)(2,1)S(1)}, u32[]{:S(2)}, u32[]{:S(2)}) %collective-permute-start.32) | collective-permute-done | bytes 294944 | tf_op jit(solution)/shard_map/ppermute | solution.py:413
  195.8 2.9 %shard_map.152 = (f32[576,768]{1,0:T(8,128)}, f32[192,768]{1,0:T(8,128)}) custom-call(bf16[192,768]{1,0:T(8,128)(2,1)} %shard_map.149.refs_0_, bf16[192,768]{1,0:T(8,128)(2,1)} %copy-done.19, bf16[192,768]{1,0:T(8,128)(2,1)} %shard_map.151.refs_2_, bf16[192,768]{1,0:T(8,128)(2,1)} %copy-done.17), custom_call_target="tpu_custom_call" | custom-call | tf_op jit(solution)/shard_map/pallas_call | solution.py:20
  199.9 19.9 %psum.7 = f32[2,192]{1,0:T(2,128)S(1)} all-reduce(f32[2,192]{1,0:T(2,128)S(1)} %pad_maximum_fusion.5), channel_id=1, replica_groups=mesh['dp'=4,'seq'=2,'mp'=4] {'dp','seq'}, use_global_device_ids=true, to_apply=%region_2.3 | all-reduce | flops 384 | bytes 3072 | tf_op jit(solution)/shard_map/psum | solution.py:611
  224.9 5.1 %collective-permute-done.24 = f32[200,64]{1,0:T(8,128)S(1)} collective-permute-done((f32[200,64]{1,0:T(8,128)S(1)}, f32[200,64]{1,0:T(8,128)S(1)}, u32[]{:S(2)}, u32[]{:S(2)}) %collective-permute-start.24) | collective-permute-done | bytes 51232 | tf_op jit(solution)/shard_map/ppermute | solution.py:614
  (246 shorter events, 93.9 us)
Async XLA Ops:
  0.6 15.8 %collective-permute-start.1 = (bf16[192,512]{1,0:T(8,128)(2,1)}, bf16[192,512]{1,0:T(8,128)(2,1)S(1)}, u32[]{:S(2)}, u32[]{:S(2)}) collective-permute-start(bf16[192,512]{1,0:T(8,128)(2,1)} %bitcast.49), channel_id=1, source_target_pairs={{0,2},{1,3},{2,0},{3,1},{4,6},{5,7},{6,4},{7,5},{8,10},{9,11},{10,... | collective-permute-start | bytes 589832 | tf_op jit(solution)/shard_map/ppermute | solution.py:413
  3.7 15.9 %collective-permute-start = (bf16[192,512]{1,0:T(8,128)(2,1)}, bf16[192,512]{1,0:T(8,128)(2,1)S(1)}, u32[]{:S(2)}, u32[]{:S(2)}) collective-permute-start(bf16[192,512]{1,0:T(8,128)(2,1)} %bitcast.50), channel_id=1, source_target_pairs={{0,1},{1,0},{2,3},{3,2},{4,5},{5,4},{6,7},{7,6},{8,9},{9,8},{10,11... | collective-permute-start | bytes 589832 | tf_op jit(solution)/shard_map/ppermute | solution.py:413
  34.5 12.1 %collective-permute-start.9 = (bf16[384,512]{1,0:T(8,128)(2,1)S(1)}, bf16[384,512]{1,0:T(8,128)(2,1)S(1)}, u32[]{:S(2)}, u32[]{:S(2)}) collective-permute-start(bf16[384,512]{1,0:T(8,128)(2,1)S(1)} %add_convert_fusion.3), channel_id=1, source_target_pairs={{0,2},{1,3},{2,0},{3,1},{4,6},{5,7},{6,4},{7,5},{8,10},{9,11},{10,... | collective-permute-start | bytes 1179656 | tf_op jit(solution)/shard_map/ppermute | solution.py:413
  34.7 15.3 %collective-permute-start.12 = (bf16[192,512]{1,0:T(8,128)(2,1)S(1)}, bf16[192,512]{1,0:T(8,128)(2,1)S(1)}, u32[]{:S(2)}, u32[]{:S(2)}) collective-permute-start(bf16[192,512]{1,0:T(8,128)(2,1)S(1)} %bitcast.54), channel_id=1, source_target_pairs={{0,2},{1,3},{2,0},{3,1},{4,6},{5,7},{6,4},{7,5},{8,10},{9,11},{10,... | collective-permute-start | bytes 589832 | tf_op jit(solution)/shard_map/ppermute | solution.py:413
  71.9 15.7 %collective-permute-start.41 = (bf16[256,768]{1,0:T(8,128)(2,1)}, bf16[256,768]{1,0:T(8,128)(2,1)S(1)}, u32[]{:S(2)}, u32[]{:S(2)}) collective-permute-start(bf16[256,768]{1,0:T(8,128)(2,1)} %get-tuple-element.104), channel_id=1, source_target_pairs={{0,4},{4,0},{1,5},{5,1},{2,6},{6,2},{3,7},{7,3},{8,12},{12,8},{9,1... | collective-permute-start | bytes 1179656 | tf_op jit(solution)/shard_map/ppermute | solution.py:413
  75.3 17.7 %collective-permute-start.18 = (bf16[384,512]{1,0:T(8,128)(2,1)S(1)}, bf16[384,512]{1,0:T(8,128)(2,1)S(1)}, u32[]{:S(2)}, u32[]{:S(2)}) collective-permute-start(bf16[384,512]{1,0:T(8,128)(2,1)S(1)} %add_convert_fusion.mine), channel_id=1, source_target_pairs={{0,1},{1,0},{2,3},{3,2},{4,5},{5,4},{6,7},{7,6},{8,9},{9,8},{10,11... | collective-permute-start | bytes 1179656 | tf_op jit(solution)/shard_map/ppermute | solution.py:413
  82.6 23.1 %collective-permute-start.50 = (bf16[48,768]{1,0:T(8,128)(2,1)}, bf16[48,768]{1,0:T(8,128)(2,1)S(1)}, u32[]{:S(2)}, u32[]{:S(2)}) collective-permute-start(bf16[48,768]{1,0:T(8,128)(2,1)} %get-tuple-element.112), channel_id=1, source_target_pairs={{0,8},{8,0},{16,24},{24,16},{1,9},{9,1},{17,25},{25,17},{2,10},{10... | collective-permute-start | bytes 221192 | tf_op jit(solution)/shard_map/ppermute | solution.py:413
  84.4 24.0 %collective-permute-start.51 = (bf16[48,768]{1,0:T(8,128)(2,1)}, bf16[48,768]{1,0:T(8,128)(2,1)S(1)}, u32[]{:S(2)}, u32[]{:S(2)}) collective-permute-start(bf16[48,768]{1,0:T(8,128)(2,1)} %get-tuple-element.113), channel_id=1, source_target_pairs={{0,16},{8,24},{16,0},{24,8},{1,17},{9,25},{17,1},{25,9},{2,18},{10... | collective-permute-start | bytes 221192 | tf_op jit(solution)/shard_map/ppermute | solution.py:413
  87.0 21.4 %collective-permute-start.52 = (bf16[48,768]{1,0:T(8,128)(2,1)}, bf16[48,768]{1,0:T(8,128)(2,1)S(1)}, u32[]{:S(2)}, u32[]{:S(2)}) collective-permute-start(bf16[48,768]{1,0:T(8,128)(2,1)} %get-tuple-element.114), channel_id=1, source_target_pairs={{0,24},{8,16},{16,8},{24,0},{1,25},{9,17},{17,9},{25,1},{2,26},{10... | collective-permute-start | bytes 221192 | tf_op jit(solution)/shard_map/ppermute | solution.py:413
  90.4 19.9 %collective-permute-start.42 = (bf16[64,768]{1,0:T(8,128)(2,1)}, bf16[64,768]{1,0:T(8,128)(2,1)S(1)}, u32[]{:S(2)}, u32[]{:S(2)}) collective-permute-start(bf16[64,768]{1,0:T(8,128)(2,1)} %get-tuple-element.106), channel_id=1, source_target_pairs={{0,8},{8,0},{16,24},{24,16},{1,9},{9,1},{17,25},{25,17},{2,10},{10... | collective-permute-start | bytes 294920 | tf_op jit(solution)/shard_map/ppermute | solution.py:413
  93.0 31.3 %collective-permute-start.14 = (bf16[2,192,512]{2,1,0:T(8,128)(2,1)S(1)}, bf16[2,192,512]{2,1,0:T(8,128)(2,1)S(1)}, u32[]{:S(2)}, u32[]{:S(2)}) collective-permute-start(bf16[2,192,512]{2,1,0:T(8,128)(2,1)S(1)} %copy-done.49), channel_id=1, source_target_pairs={{0,1},{1,0},{2,3},{3,2},{4,5},{5,4},{6,7},{7,6},{8,9},{9,8},{10,11... | collective-permute-start | bytes 1179656 | tf_op jit(solution)/shard_map/ppermute | solution.py:413
  110.3 16.1 %collective-permute-start.25 = (bf16[192,768]{1,0:T(8,128)(2,1)}, bf16[192,768]{1,0:T(8,128)(2,1)S(1)}, u32[]{:S(2)}, u32[]{:S(2)}) collective-permute-start(bf16[192,768]{1,0:T(8,128)(2,1)} %get-tuple-element.90), channel_id=1, source_target_pairs={{0,4},{4,0},{1,5},{5,1},{2,6},{6,2},{3,7},{7,3},{8,12},{12,8},{9,1... | collective-permute-start | bytes 884744 | tf_op jit(solution)/shard_map/ppermute | solution.py:413
  119.7 16.6 %collective-permute-start.55 = (bf16[48,768]{1,0:T(8,128)(2,1)S(1)}, bf16[48,768]{1,0:T(8,128)(2,1)S(1)}, u32[]{:S(2)}, u32[]{:S(2)}) collective-permute-start(bf16[48,768]{1,0:T(8,128)(2,1)S(1)} %add_convert_fusion.5.refs_0_), channel_id=1, source_target_pairs={{0,24},{8,16},{16,8},{24,0},{1,25},{9,17},{17,9},{25,1},{2,26},{10... | collective-permute-start | bytes 221192 | tf_op jit(solution)/shard_map/ppermute | solution.py:413
  124.3 12.9 %collective-permute-start.45 = (bf16[64,768]{1,0:T(8,128)(2,1)S(1)}, bf16[64,768]{1,0:T(8,128)(2,1)S(1)}, u32[]{:S(2)}, u32[]{:S(2)}) collective-permute-start(bf16[64,768]{1,0:T(8,128)(2,1)S(1)} %add_convert_fusion.4.refs_0_), channel_id=1, source_target_pairs={{0,8},{8,0},{16,24},{24,16},{1,9},{9,1},{17,25},{25,17},{2,10},{10... | collective-permute-start | bytes 294920 | tf_op jit(solution)/shard_map/ppermute | solution.py:413
  124.3 12.8 %collective-permute-start.34 = (bf16[48,768]{1,0:T(8,128)(2,1)}, bf16[48,768]{1,0:T(8,128)(2,1)S(1)}, u32[]{:S(2)}, u32[]{:S(2)}) collective-permute-start(bf16[48,768]{1,0:T(8,128)(2,1)} %get-tuple-element.98), channel_id=1, source_target_pairs={{0,8},{8,0},{16,24},{24,16},{1,9},{9,1},{17,25},{25,17},{2,10},{10... | collective-permute-start | bytes 221192 | tf_op jit(solution)/shard_map/ppermute | solution.py:413
  126.3 12.1 %collective-permute-start.35 = (bf16[48,768]{1,0:T(8,128)(2,1)}, bf16[48,768]{1,0:T(8,128)(2,1)S(1)}, u32[]{:S(2)}, u32[]{:S(2)}) collective-permute-start(bf16[48,768]{1,0:T(8,128)(2,1)} %get-tuple-element.99), channel_id=1, source_target_pairs={{0,16},{8,24},{16,0},{24,8},{1,17},{9,25},{17,1},{25,9},{2,18},{10... | collective-permute-start | bytes 221192 | tf_op jit(solution)/shard_map/ppermute | solution.py:413
  126.4 14.0 %collective-permute-start.36 = (bf16[48,768]{1,0:T(8,128)(2,1)}, bf16[48,768]{1,0:T(8,128)(2,1)S(1)}, u32[]{:S(2)}, u32[]{:S(2)}) collective-permute-start(bf16[48,768]{1,0:T(8,128)(2,1)} %get-tuple-element.100), channel_id=1, source_target_pairs={{0,24},{8,16},{16,8},{24,0},{1,25},{9,17},{17,9},{25,1},{2,26},{10... | collective-permute-start | bytes 221192 | tf_op jit(solution)/shard_map/ppermute | solution.py:413
  137.2 35.7 %collective-permute-start.19 = (bf16[2,192,640]{2,1,0:T(8,128)(2,1)}, bf16[2,192,640]{2,1,0:T(8,128)(2,1)S(1)}, u32[]{:S(2)}, u32[]{:S(2)}) collective-permute-start(bf16[2,192,640]{2,1,0:T(8,128)(2,1)} %get-tuple-element.87), channel_id=1, source_target_pairs={{0,1},{1,0},{2,3},{3,2},{4,5},{5,4},{6,7},{7,6},{8,9},{9,8},{10,11... | collective-permute-start | bytes 1474568 | tf_op jit(solution)/shard_map/ppermute | solution.py:413
  155.9 13.2 %collective-permute-start.30 = (bf16[48,768]{1,0:T(8,128)(2,1)S(1)}, bf16[48,768]{1,0:T(8,128)(2,1)S(1)}, u32[]{:S(2)}, u32[]{:S(2)}) collective-permute-start(bf16[48,768]{1,0:T(8,128)(2,1)S(1)} %add_convert_fusion.7.refs_0_), channel_id=1, source_target_pairs={{0,16},{8,24},{16,0},{24,8},{1,17},{9,25},{17,1},{25,9},{2,18},{10... | collective-permute-start | bytes 221192 | tf_op jit(solution)/shard_map/ppermute | solution.py:413
  169.1 16.8 %collective-permute-start.48 = (bf16[256,768]{1,0:T(8,128)(2,1)}, bf16[256,768]{1,0:T(8,128)(2,1)S(1)}, u32[]{:S(2)}, u32[]{:S(2)}) collective-permute-start(bf16[256,768]{1,0:T(8,128)(2,1)} %shard_map.154.refs_0_), channel_id=1, source_target_pairs={{0,4},{4,0},{1,5},{5,1},{2,6},{6,2},{3,7},{7,3},{8,12},{12,8},{9,1... | collective-permute-start | bytes 1179656 | tf_op jit(solution)/shard_map/ppermute | solution.py:413
  169.4 22.6 %collective-permute-start.40 = (bf16[192,768]{1,0:T(8,128)(2,1)}, bf16[192,768]{1,0:T(8,128)(2,1)S(1)}, u32[]{:S(2)}, u32[]{:S(2)}) collective-permute-start(bf16[192,768]{1,0:T(8,128)(2,1)} %shard_map.151.refs_2_), channel_id=1, source_target_pairs={{0,4},{4,0},{1,5},{5,1},{2,6},{6,2},{3,7},{7,3},{8,12},{12,8},{9,1... | collective-permute-start | bytes 884744 | tf_op jit(solution)/shard_map/ppermute | solution.py:413
  172.9 22.2 %collective-permute-start.32 = (bf16[192,768]{1,0:T(8,128)(2,1)}, bf16[192,768]{1,0:T(8,128)(2,1)S(1)}, u32[]{:S(2)}, u32[]{:S(2)}) collective-permute-start(bf16[192,768]{1,0:T(8,128)(2,1)} %shard_map.149.refs_0_), channel_id=1, source_target_pairs={{0,4},{4,0},{1,5},{5,1},{2,6},{6,2},{3,7},{7,3},{8,12},{12,8},{9,1... | collective-permute-start | bytes 884744 | tf_op jit(solution)/shard_map/ppermute | solution.py:413
  173.7 16.2 %collective-permute-start.22 = (f32[8,640]{1,0:T(8,128)S(1)}, f32[8,640]{1,0:T(8,128)S(1)}, u32[]{:S(2)}, u32[]{:S(2)}) collective-permute-start(f32[8,640]{1,0:T(8,128)S(1)} %add.111), channel_id=1, source_target_pairs={{0,2},{1,3},{2,0},{3,1},{4,6},{5,7},{6,4},{7,5},{8,10},{9,11},{10,... | collective-permute-start | bytes 61448 | tf_op jit(solution)/shard_map/ppermute | solution.py:413
  177.4 21.3 %collective-permute-start.20 = (bf16[192,640]{1,0:T(8,128)(2,1)S(1)}, bf16[192,640]{1,0:T(8,128)(2,1)S(1)}, u32[]{:S(2)}, u32[]{:S(2)}) collective-permute-start(bf16[192,640]{1,0:T(8,128)(2,1)S(1)} %fusion.8), channel_id=1, source_target_pairs={{0,2},{1,3},{2,0},{3,1},{4,6},{5,7},{6,4},{7,5},{8,10},{9,11},{10,... | collective-permute-start | bytes 737288 | tf_op jit(solution)/shard_map/ppermute | solution.py:413
  (85 other events, 771.7 us)

commit v2 on v1

--- a/solution.py
+++ b/solution.py
@@ -16,12 +16,19 @@
 BF16 = jnp.bfloat16
 
 
+def room(shape, dtype):
+    lanes = -(-shape[-1] // 128) * 128
+    return math.prod(shape[:-1]) * lanes * jnp.dtype(dtype).itemsize
+
+
 def call(kernel, outs, scratch, *args):
+    arrays = list(outs) + list(scratch) + [(a.shape, a.dtype) for a in args]
+    grant = sum(room(s, t) for s, t in arrays) + 4 * 1024 * 1024
     return pl.pallas_call(
         kernel,
         out_shape=tuple(jax.ShapeDtypeStruct(s, t) for s, t in outs),
         scratch_shapes=[pltpu.VMEM(s, t) for s, t in scratch],
-        compiler_params=pltpu.CompilerParams(vmem_limit_bytes=56 * 1024 * 1024),
+        compiler_params=pltpu.CompilerParams(vmem_limit_bytes=grant),
     )(*args)
 
 
@@ -120,7 +127,7 @@
 
     def feed(r, carry):
         normed = (xall[pl.ds(r, STEP), :].astype(F32) - mean) * inverse
-        fed[pl.ds(r, STEP), :] = (normed * gain[pl.ds(r, STEP), :]).astype(BF16)
+        fed[pl.ds(r, STEP), :] = (normed * gain[pl.ds(r, STEP), 0:1]).astype(BF16)
         return carry
 
     row_loop(width, STEP, feed, 0)
@@ -199,7 +206,7 @@
     def feed(r, carry):
         value = (middle[pl.ds(r, STEP), :] - mean) * inverse
         normed[pl.ds(r, STEP), :] = value
-        fed[pl.ds(r, STEP), :] = (value * gain[pl.ds(r, STEP), :]).astype(BF16)
+        fed[pl.ds(r, STEP), :] = (value * gain[pl.ds(r, STEP), 1:2]).astype(BF16)
         return carry
 
     row_loop(width, STEP, feed, 0)
@@ -244,10 +251,10 @@
     if cuts is None:
         outs[0][...] = stack[...]
         return
-    seq = lax.axis_index("seq")
     start = 0
-    for i, rows in enumerate(cuts):
-        split_half(stack.at[pl.ds(start, rows), :], outs[2 * i], outs[2 * i + 1], seq)
+    for i, (rows, order) in enumerate(cuts):
+        index = lax.axis_index(order[0]) % 2
+        split_half(stack.at[pl.ds(start, rows), :], outs[2 * i], outs[2 * i + 1], index)
         start += rows
 
 
@@ -275,7 +282,7 @@
             at = pl.multiple_of(index * rows + r, STEP)
             grad = part[pl.ds(r, STEP), :].astype(F32)
             full[pl.ds(at, STEP), :] = grad
-            hat = grad * gain[pl.ds(at, STEP), :]
+            hat = grad * gain[pl.ds(at, STEP), 1:2]
             a = a + fold(hat)
             b = b + fold(hat * normed[pl.ds(at, STEP), :])
         return a, b
@@ -293,7 +300,7 @@
 
     def back(r, carry):
         at = pl.ds(r, STEP)
-        hat = full[at, :] * gain[at, :]
+        hat = full[at, :] * gain[at, 1:2]
         value = upstream[at, :].astype(F32) + inv * (hat - one - normed[at, :] * two)
         full[at, :] = value
         low[at, :] = value.astype(BF16)
@@ -361,7 +368,7 @@
     def add(r, acc):
         a, b = acc
         at = pl.ds(r, STEP)
-        hat = terms[at, :] * gain[at, :]
+        hat = terms[at, :] * gain[at, 0:1]
         normed = (xall[at, :].astype(F32) - mean) * inverse
         return a + fold(hat), b + fold(hat * normed)
 
@@ -373,33 +380,33 @@
     split_shards(terms, keep, send, core)
 
 
-def quarters_kernel(keep, got, own, *sends):
-    rows = own.shape[0]
-    me = lax.axis_index("dp")
-    for k, out in enumerate((own,) + sends):
-        at = pl.ds(pl.multiple_of(jnp.bitwise_xor(me, k) * rows, 16), rows)
-        out[...] = (keep[at, :] + got[at, :].astype(F32)).astype(out.dtype)
-
-
-def join_kernel(*refs):
-    pieces, out = refs[:-1], refs[-1]
-    rows = pieces[0].shape[0]
-    me = lax.axis_index("dp")
-    for k, piece in enumerate(pieces):
-        out[pl.ds(pl.multiple_of(jnp.bitwise_xor(me, k) * rows, 16), rows), :] = piece[...]
+def halves_kernel(keep, got, out_keep, out_send, *, axis):
+    rows = out_keep.shape[0]
+    index = lax.axis_index(axis) % 2
+
+    def one(r, carry):
+        mine = pl.ds(pl.multiple_of(index * rows + r, 16), 16)
+        other = pl.ds(pl.multiple_of((1 - index) * rows + r, 16), 16)
+        at = pl.ds(r, 16)
+        out_keep[at, :] = keep[mine, :] + got[mine, :].astype(F32)
+        out_send[at, :] = (keep[other, :] + got[other, :].astype(F32)).astype(BF16)
+        return carry
+
+    row_loop(rows, 16, one, 0)
 
 
 def place_kernel(*refs, cuts, outs):
     count = len(cuts)
-    halves, targets, stack = refs[: 2 * count], refs[2 * count : -1], refs[-1]
-    seq = lax.axis_index("seq")
+    pieces, targets, stack = refs[: 4 * count], refs[4 * count : -1], refs[-1]
     start = 0
-    for i, rows in enumerate(cuts):
-        size = rows // 2
-        mine = pl.ds(pl.multiple_of(start + seq * size, 16), size)
-        other = pl.ds(pl.multiple_of(start + (1 - seq) * size, 16), size)
-        stack[mine, :] = halves[2 * i][...].astype(F32)
-        stack[other, :] = halves[2 * i + 1][...].astype(F32)
+    for i, (rows, order) in enumerate(cuts):
+        size = rows // 4
+        one, two = (lax.axis_index(axis) % 2 for axis in order)
+        for k in range(4):
+            far = one if k < 2 else 1 - one
+            near = two if k % 2 == 0 else 1 - two
+            at = pl.multiple_of(start + (2 * far + near) * size, 16)
+            stack[pl.ds(at, size), :] = pieces[4 * i + k][...].astype(F32)
         start += rows
     for target, spans in zip(targets, outs):
         at = 0
@@ -431,20 +438,45 @@
     return jnp.where(x == 0, half[0], half[1]) + flip(away, "mp", 2).astype(F32)
 
 
-def reduce_unit(keep, send):
+def to_neighbours(low, high):
+    count = lax.axis_size("seq")
+    if count == 2:
+        last = lax.axis_index("seq") == 1
+        got = flip(jnp.where(last, low, high), "seq", 1)
+        zero = jnp.zeros_like(got)
+        return jnp.where(last, zero, got), jnp.where(last, got, zero)
+    after = lax.ppermute(low, "seq", [(i + 1, i) for i in range(count - 1)])
+    before = lax.ppermute(high, "seq", [(i, i + 1) for i in range(count - 1)])
+    return after, before
+
+
+def staged():
+    return lax.axis_size("seq") == 2 and lax.axis_size("dp") == 4
+
+
+def sum_blocks(x):
+    if not staged():
+        return lax.psum(x, ("dp", "seq"))
+    x = x + flip(x, "seq", 1)
+    x = x + flip(x, "dp", 1)
+    return x + flip(x, "dp", 2)
+
+
+def reduce_unit(keep, send, order):
+    one, two = order
     rows, width = keep.shape
-    count = lax.axis_size("dp")
-    part = rows // count
-    got = flip(send, "seq", 1)
-    outs = [((part, width), F32)] + [((part, width), BF16)] * (count - 1)
-    quarters = call(quarters_kernel, outs, [], keep, got)
-    total = quarters[0]
-    for k in range(1, count):
-        total = total + flip(quarters[k], "dp", k).astype(F32)
-    total = total.astype(BF16)
-    pieces = [total] + [flip(total, "dp", k) for k in range(1, count)]
-    (half,) = call(join_kernel, [((rows, width), BF16)], [], *pieces)
-    return half, flip(half, "seq", 1)
+    got = flip(send, one, 1)
+    keep, send = call(
+        functools.partial(halves_kernel, axis=two),
+        [((rows // 2, width), F32), ((rows // 2, width), BF16)],
+        [],
+        keep,
+        got,
+    )
+    part = (keep + flip(send, two, 1).astype(F32)).astype(BF16)
+    total = (part.astype(F32) + flip(part, "dp", 2).astype(F32)).astype(BF16)
+    beside = flip(total, two, 1)
+    return total, beside, flip(total, one, 1), flip(beside, one, 1)
 
 
 def reduce_stack(parts, cuts, spans, width):
@@ -452,20 +484,19 @@
     if cuts is None:
         total = lax.psum(parts[0], ("dp", "seq"))
         return [jnp.concatenate([total[b : b + n] for b, n in span]) for span in spans]
-    halves = []
-    for i in range(len(cuts)):
-        halves.extend(reduce_unit(parts[2 * i], parts[2 * i + 1]))
+    pieces = []
+    for i, (_, order) in enumerate(cuts):
+        pieces.extend(reduce_unit(parts[2 * i], parts[2 * i + 1], order))
     kernel = functools.partial(place_kernel, cuts=cuts, outs=spans)
-    return call(
-        kernel, [(size, F32) for size in sizes], [((sum(cuts), width), F32)], *halves
-    )
+    scratch = [((sum(rows for rows, _ in cuts), width), F32)]
+    return call(kernel, [(size, F32) for size in sizes], scratch, *pieces)
 
 
 def unit_shapes(cuts, rows, width):
     if cuts is None:
         return [((rows, width), F32)]
     shapes = []
-    for size in cuts:
+    for size, _ in cuts:
         shapes += [((size // 2, width), F32), ((size // 2, width), BF16)]
     return shapes
 
@@ -487,22 +518,17 @@
     heads = columns // HEAD
     tokens = length + TILE
     half = width // 2
-    dp, seqs = lax.axis_size("dp"), lax.axis_size("seq")
-    staged = seqs == 2 and dp & (dp - 1) == 0
-    grain = 2 * dp * 16
+    orders = (("seq", "dp"), ("dp", "seq"))
+    grain = 4 * 16
     x_own = hidden_in[0].T
     u_own = cotangent[0].T
     w = jnp.transpose(qkv_weight, (1, 2, 0)).reshape(3 * columns, width)
     win = jnp.transpose(geglu_in, (1, 2, 0)).reshape(2 * units, width)
-    gain_one = attention_gain[:, None]
-    gain_two = feedforward_gain[:, None]
-
-    forward = [(i, i + 1) for i in range(seqs - 1)]
-    backward = [(i + 1, i) for i in range(seqs - 1)]
-    before = lax.ppermute(x_own[:, length - HALF :], "seq", forward)
-    after = lax.ppermute(x_own[:, :HALF], "seq", backward)
+    gains = jnp.stack([attention_gain, feedforward_gain], axis=1)
+
+    x_parts = gather_mp(x_own)
+    after, before = to_neighbours(x_own[:, :HALF], x_own[:, length - HALF :])
     halo = jnp.concatenate([after, before], axis=1)
-    x_parts = gather_mp(x_own)
     h_parts = gather_mp(halo)
     u_parts = gather_mp(u_own)
 
@@ -528,7 +554,7 @@
             ((half, length), BF16),
         ],
         [((3 * columns, tokens), F32), ((width, length), F32)],
-        *x_parts, *h_parts, gain_one, w, attention_out, cos, sin,
+        *x_parts, *h_parts, gains, w, attention_out, cos, sin,
     )
     mine, other = sum_halves(keep, send)
     middle_own, normed, inverse, fed_two, upstream, product, lifted_grad, keep, send = call(
@@ -550,14 +576,13 @@
             ((units, length), F32),
             ((width, length), F32),
         ],
-        xall, mine, other, *u_parts, gain_two, win, geglu_out,
+        xall, mine, other, *u_parts, gains, win, geglu_out,
     )
     mine, other = sum_halves(keep, send)
 
     rows = 3 * units
-    padded = -(-rows // grain) * grain if staged else rows
-    large = -(-padded // (2 * grain)) * grain
-    geglu_cuts = (large, padded - large) if staged else None
+    padded = -(-rows // (2 * grain)) * (2 * grain) if staged() else rows
+    geglu_cuts = tuple((padded // 2, order) for order in orders) if staged() else None
     shard_shapes = [((2, share, length), F32), ((2, share, length), BF16)]
     outs = call(
         functools.partial(geglu_weights_kernel, cuts=geglu_cuts),
@@ -570,7 +595,9 @@
         outs[2:], geglu_cuts, (((0, 2 * units),), ((2 * units, units),)), width
     )
 
-    back_cuts = (2 * columns, 2 * columns) if staged and 2 * columns % grain == 0 else None
+    back_cuts = None
+    if staged() and 2 * columns % grain == 0:
+        back_cuts = tuple((2 * columns, order) for order in orders)
     outs = call(
         functools.partial(attention_back_kernel, cuts=back_cuts),
         [((share, length), F32), ((share, 128), F32), ((3 * columns, tokens), BF16)]
@@ -583,7 +610,7 @@
             ((columns, tokens), F32),
             ((4 * columns, width), F32),
         ],
-        mine, other, normed, inverse, gain_two, upstream, attention_out,
+        mine, other, normed, inverse, gains, upstream, attention_out,
         q, kw, vw, totals, mixed, cos, sin, fed,
     )
     middle_grad, gain_two_lanes, proj_grad = outs[:3]
@@ -598,7 +625,7 @@
         input_terms_kernel,
         [((2, share, tokens), F32), ((2, share, tokens), BF16), ((8, tokens), F32)],
         [((width, tokens), F32)],
-        proj_grad, w, gain_one, xall, stats,
+        proj_grad, w, gains, xall, stats,
     )
     grad_one = scatter_shards(keep, send)
     sums = sums + flip(sums, "mp", 1)
@@ -608,10 +635,9 @@
     normed_own = (x_all_own - stats[0:1]) * stats[1:2]
     gain_one_grad = jnp.sum(grad_one * normed_own, axis=1)
     gain_two_grad = jnp.sum(gain_two_lanes, axis=1)
-    gains = lax.psum(jnp.stack([gain_one_grad, gain_two_grad]), ("dp", "seq"))
+    gains = sum_blocks(jnp.stack([gain_one_grad, gain_two_grad]))
     both = jnp.concatenate([grad_one, sums], axis=0)
-    low_add = lax.ppermute(both[:, length : length + HALF], "seq", forward)
-    high_add = lax.ppermute(both[:, length + HALF :], "seq", backward)
+    high_add, low_add = to_neighbours(both[:, length + HALF :], both[:, length : length + HALF])
     both = jnp.concatenate(
         [
             both[:, :HALF] + low_add,
@@ -620,7 +646,7 @@
         ],
         axis=1,
     )
-    hat = both[:share] * lax.dynamic_slice_in_dim(gain_one, offset, share, 0)
+    hat = both[:share] * lax.dynamic_slice_in_dim(attention_gain, offset, share, 0)[:, None]
     grad_input = middle_grad + stats[1:2, :length] * (
         hat - both[share : share + 1] - normed_own[:, :length] * both[share + 1 : share + 2]
     )

time: 232 us -> 164 us (0.71)
  Pallas kernels: 63 us -> 31.9 us
  starting transfers between devices: 62.7 us -> 40.4 us
  blocking collectives: 19.9 us -> 0 us
  other arithmetic: 8.97 us -> 13 us
    pallas_call x15 -> x11, Pallas kernels: 63 us -> 31.9 us  [call(): pl.pallas_call(kernel, out_shape=tuple((jax.ShapeDtypeStruct(s, t) for s,...]
    psum x1 -> x0, blocking collectives: 19.9 us -> none  [body(): gains = lax.psum(jnp.stack([gain_one_grad, gain_two_grad]), ('dp', 'seq'))]
    ppermute x53 -> x50, starting transfers between devices: 54.3 us -> 40.4 us  [flip(): return lax.ppermute(x, axis, [(i, i ^ bit) for i in range(count)])]
    ppermute x4 -> x0, waiting for transfers between devices: 8.48 us -> none  [the longest x1 5.11 us: body(): high_add = lax.ppermute(both[:, length + HALF:], 'seq', backward)]
    ppermute x4 -> x0, starting transfers between devices: 8.42 us -> none  [the longest x1 4.55 us: body(): before = lax.ppermute(x_own[:, length - HALF:], 'seq', forward)]
    ppermute x53 -> x50, waiting for transfers between devices: 55.3 us -> 63.2 us  [flip(): return lax.ppermute(x, axis, [(i, i ^ bit) for i in range(count)])]
    broadcast_in_dim x2 -> x0, local copies, waits for them, and re-layouts: 2.52 us -> none  [the longest x1 1.6 us: body(): gain_one = attention_gain[:, None]]
    unnamed x104 -> x84, local copies, waits for them, and re-layouts: 5.25 us -> 7.6 us
  transfers between devices with their start and end apart: 57 -> 50, of which waited for: 20 -> 17; matrix products, arithmetic and copies ran while one was open for 4% -> 12% of each run, Pallas kernels for 19% -> 12%
where the time goes in v2:
time: 164 us
  waiting for transfers between devices  63.2 us (39%)
  starting transfers between devices  40.4 us (25%)
  Pallas kernels  31.9 us (19%)
  local copies, waits for them, and re-layouts  13.8 us (8%)
  other arithmetic  13 us (8%)
    ppermute x50, waiting for transfers between devices, flip(): return lax.ppermute(x, axis, [(i, i ^ bit) for i in range(count)])  63.2 us
    ppermute x50, starting transfers between devices, flip(): return lax.ppermute(x, axis, [(i, i ^ bit) for i in range(count)])  40.4 us
    pallas_call x11, Pallas kernels, call(): pl.pallas_call(kernel, out_shape=tuple((jax.ShapeDtypeStruct(s, t) for s,...  31.9 us
    unnamed x84, local copies, waits for them, and re-layouts  7.6 us
  transfers between devices with their start and end apart: 50, of which 17 were waited for; matrix products, arithmetic and copies ran while one was open for 12% of the time, Pallas kernels for 12%

profile of v2, /device:TPU:0, one launch (start us, length us, event | category | flops | bytes accessed | tf_op | source)
XLA Modules:
  0.0 163.6 jit_solution(3603604150838797290)
XLA Ops:
  0.6 3.0 %collective-permute-start.1 = (bf16[192,512]{1,0:T(8,128)(2,1)}, bf16[192,512]{1,0:T(8,128)(2,1)S(1)}, u32[]{:S(2)}, u32[]{:S(2)}) collective-permute-start(bf16[192,512]{1,0:T(8,128)(2,1)} %bitcast.49), channel_id=1, source_target_pairs={{0,2},{1,3},{2,0},{3,1},{4,6},{5,7},{6,4},{7,5},{8,10},{9,11},{10,... | collective-permute-start | bytes 589832 | tf_op jit(solution)/shard_map/ppermute | solution.py:420
  6.2 2.6 %collective-permute-done.3 = bf16[192,64]{1,0:T(8,128)(2,1)S(1)} collective-permute-done((bf16[192,64]{1,0:T(8,128)(2,1)S(1)}, bf16[192,64]{1,0:T(8,128)(2,1)S(1)}, u32[]{:S(2)}, u32[]{:S(2)}) %collective-permute-start.3) | collective-permute-done | bytes 24608 | tf_op jit(solution)/shard_map/ppermute | solution.py:420
  17.4 7.2 %shard_map.143 = (bf16[768,640]{1,0:T(8,128)(2,1)S(1)}, f32[8,640]{1,0:T(8,128)S(1)}, bf16[768,640]{1,0:T(8,128)(2,1)S(1)}, bf16[192,512]{1,0:T(8,128)(2,1)S(1)}...) custom-call(bf16[192,512]{1,0:T(8,128)(2,1)S(1)} %bitcast.52, ...), custom_call_target="tpu_custom_call" | custom-call | tf_op jit(solution)/shard_map/pallas_call | solution.py:27
  27.5 1.7 %collective-permute-start.11 = (bf16[192,512]{1,0:T(8,128)(2,1)S(1)}, bf16[192,512]{1,0:T(8,128)(2,1)S(1)}, u32[]{:S(2)}, u32[]{:S(2)}) collective-permute-start(bf16[192,512]{1,0:T(8,128)(2,1)S(1)} %bitcast.53), channel_id=1, source_target_pairs={{0,2},{1,3},{2,0},{3,1},{4,6},{5,7},{6,4},{7,5},{8,10},{9,11},{10,... | collective-permute-start | bytes 589832 | tf_op jit(solution)/shard_map/ppermute | solution.py:420
  29.2 10.0 %collective-permute-done.8 = bf16[384,512]{1,0:T(8,128)(2,1)S(1)} collective-permute-done((bf16[384,512]{1,0:T(8,128)(2,1)S(1)}, bf16[384,512]{1,0:T(8,128)(2,1)S(1)}, u32[]{:S(2)}, u32[]{:S(2)}) %collective-permute-start.8) | collective-permute-done | bytes 393248 | tf_op jit(solution)/shard_map/ppermute | solution.py:420
  39.8 2.7 %collective-permute-done.11.u2 = bf16[192,512]{1,0:T(8,128)(2,1)S(1)} collective-permute-done((bf16[192,512]{1,0:T(8,128)(2,1)S(1)}, bf16[192,512]{1,0:T(8,128)(2,1)S(1)}, u32[]{:S(2)}, u32[]{:S(2)}) %collective-permute-start.11) | collective-permute-done | bytes 196640 | tf_op jit(solution)/shard_map/ppermute | solution.py:420
  44.0 3.8 %shard_map.144 = (f32[192,512]{1,0:T(8,128)S(1)}, f32[768,512]{1,0:T(8,128)S(1)}, f32[8,512]{1,0:T(8,128)S(1)}, bf16[768,512]{1,0:T(8,128)(2,1)S(1)}, bf16[768,5...) custom-call(bf16[768,640]{1,0:T(8,128)(2,1)S(1)} %get-tuple-element., ...), custom_call_target="tpu_custom_call" | custom-call | tf_op jit(solution)/shard_map/pallas_call | solution.py:27
  48.1 2.8 %shard_map.145 = (f32[2,192,512]{2,1,0:T(8,128)S(1)}, bf16[2,192,512]{2,1,0:T(8,128)(2,1)}, f32[224,768]{1,0:T(8,128)S(1)}, bf16[224,768]{1,0:T(8,128)(2,1)}, f3...) custom-call(bf16[288,512]{1,0:T(8,128)(2,1)S(1)} %get-tuple-element.59.product, ...), custom_call_target="tpu_custom_call" | custom-call | tf_op jit(solution)/shard_map/pallas_call | solution.py:27
  74.4 2.7 %collective-permute-start.43 = (bf16[112,768]{1,0:T(8,128)(2,1)S(1)}, bf16[112,768]{1,0:T(8,128)(2,1)S(1)}, u32[]{:S(2)}, u32[]{:S(2)}) collective-permute-start(bf16[112,768]{1,0:T(8,128)(2,1)S(1)} %add_convert_fusion.5), channel_id=1, source_target_pairs={{0,16},{8,24},{16,0},{24,8},{1,17},{9,25},{17,1},{25,9},{2,18},{10... | collective-permute-start | bytes 516104 | tf_op jit(solution)/shard_map/ppermute | solution.py:420
  77.1 8.3 %shard_map.146 = (f32[192,512]{1,0:T(8,128)S(1)}, f32[192,128]{1,0:T(8,128)S(1)}, bf16[576,640]{1,0:T(8,128)(2,1)S(1)}, f32[192,768]{1,0:T(8,128)S(1)}, bf16[192...) custom-call(bf16[384,512]{1,0:T(8,128)(2,1)S(1)} %add_convert_fusion.mine, ...), custom_call_target="tpu_custom_call" | custom-call | tf_op jit(solution)/shard_map/pallas_call | solution.py:27
  87.0 3.1 %shard_map.147 = (f32[2,192,640]{2,1,0:T(8,128)S(1)}, bf16[2,192,640]{2,1,0:T(8,128)(2,1)}, f32[8,640]{1,0:T(8,128)S(1)}) custom-call(bf16[576,640]{1,0:T(8,128)(2,1)S(1)} %get-tuple-element.77.proj_grad, bf16[576,768]{1,0:T(8,128)(2,1)S(1)} %bitcast.47, f32[768,2]{1,0:T(8,128)S(1)} %copy.18.gain, bf16[768,640]{1,0:T(8,128)(2,1)S(1)} %get-tuple-element.55.xall, ...), custom_call_target="tpu_custom_call" | custom-call | tf_op jit(solution)/shard_map/pallas_call | solution.py:27
  90.2 7.9 %collective-permute-done.29.got = bf16[192,768]{1,0:T(8,128)(2,1)S(1)} collective-permute-done((bf16[192,768]{1,0:T(8,128)(2,1)S(1)}, bf16[192,768]{1,0:T(8,128)(2,1)S(1)}, u32[]{:S(2)}, u32[]{:S(2)}) %collective-permute-start.29) | collective-permute-done | bytes 294944 | tf_op jit(solution)/shard_map/ppermute | solution.py:420
  103.1 3.5 %collective-permute-done.30 = bf16[96,768]{1,0:T(8,128)(2,1)} collective-permute-done((bf16[96,768]{1,0:T(8,128)(2,1)}, bf16[96,768]{1,0:T(8,128)(2,1)}, u32[]{:S(2)}, u32[]{:S(2)}) %collective-permute-start.30) | collective-permute-done | bytes 147488 | tf_op jit(solution)/shard_map/ppermute | solution.py:420
  107.6 4.5 %collective-permute-done.24 = bf16[96,768]{1,0:T(8,128)(2,1)S(1)} collective-permute-done((bf16[96,768]{1,0:T(8,128)(2,1)S(1)}, bf16[96,768]{1,0:T(8,128)(2,1)S(1)}, u32[]{:S(2)}, u32[]{:S(2)}) %collective-permute-start.24) | collective-permute-done | bytes 147488 | tf_op jit(solution)/shard_map/ppermute | solution.py:420
  112.2 3.0 %collective-permute-start.25 = (bf16[96,768]{1,0:T(8,128)(2,1)S(1)}, bf16[96,768]{1,0:T(8,128)(2,1)S(1)}, u32[]{:S(2)}, u32[]{:S(2)}) collective-permute-start(bf16[96,768]{1,0:T(8,128)(2,1)S(1)} %add_convert_fusion.11), channel_id=1, source_target_pairs={{0,16},{8,24},{16,0},{24,8},{1,17},{9,25},{17,1},{25,9},{2,18},{10... | collective-permute-start | bytes 442376 | tf_op jit(solution)/shard_map/ppermute | solution.py:420
  116.4 7.8 %collective-permute-done.31 = bf16[96,768]{1,0:T(8,128)(2,1)S(1)} collective-permute-done((bf16[96,768]{1,0:T(8,128)(2,1)S(1)}, bf16[96,768]{1,0:T(8,128)(2,1)S(1)}, u32[]{:S(2)}, u32[]{:S(2)}) %collective-permute-start.31) | collective-permute-done | bytes 147488 | tf_op jit(solution)/shard_map/ppermute | solution.py:420
  127.9 5.6 %collective-permute-done.38.refs_1_ = bf16[112,768]{1,0:T(8,128)(2,1)S(1)} collective-permute-done((bf16[112,768]{1,0:T(8,128)(2,1)S(1)}, bf16[112,768]{1,0:T(8,128)(2,1)S(1)}, u32[]{:S(2)}, u32[]{:S(2)}) %collective-permute-start.38) | collective-permute-done | bytes 172064 | tf_op jit(solution)/shard_map/ppermute | solution.py:420
  137.6 1.7 %collective-permute-start.26 = (bf16[96,768]{1,0:T(8,128)(2,1)S(1)}, bf16[96,768]{1,0:T(8,128)(2,1)S(1)}, u32[]{:S(2)}, u32[]{:S(2)}) collective-permute-start(bf16[96,768]{1,0:T(8,128)(2,1)S(1)} %add_convert_fusion.10.refs_0_), channel_id=1, source_target_pairs={{0,8},{8,0},{16,24},{24,16},{1,9},{9,1},{17,25},{25,17},{2,10},{10... | collective-permute-start | bytes 442376 | tf_op jit(solution)/shard_map/ppermute | solution.py:420
  139.9 1.8 %fusion.6 = f32[1,512,192]{1,2,0:T(8,128)} fusion(f32[192,512]{1,0:T(8,128)S(1)} %copy-done.20, bf16[192,512]{1,0:T(8,128)(2,1)} %collective-permute-done.14, f32[2,192,512]{2,1,0:T(8,128)S(1)} %copy-done.37, pred[]{:T(512)S(6)} %eq.5), kind=kLoop, calls=%fused_computation.28 | loop fusion | flops 393216 | bytes 1769473 | tf_op jit(solution)/shard_map/broadcast_in_dim | solution.py:654
  141.7 1.8 %shard_map.153 = (f32[576,768]{1,0:T(8,128)}, f32[288,768]{1,0:T(8,128)}) custom-call(bf16[112,768]{1,0:T(8,128)(2,1)S(1)} %add_convert_fusion.6.refs_0_, bf16[112,768]{1,0:T(8,128)(2,1)S(1)} %collective-permute-done.38.refs_1_, bf16[112,768]{1,0:T(8,128)(2,1)S(1)} %collective-permute-done.39.refs_2_, bf16[112,768]{1,0:T(8,128)(2,1)S(1)} %collective-permute-done.40.refs_3_, ...), custom_call_target="tpu_custom_call" | custom-call | tf_op jit(solution)/shard_map/pallas_call | solution.py:27
  145.4 1.7 %collective-permute-start.34 = (bf16[96,768]{1,0:T(8,128)(2,1)S(1)}, bf16[96,768]{1,0:T(8,128)(2,1)S(1)}, u32[]{:S(2)}, u32[]{:S(2)}) collective-permute-start(bf16[96,768]{1,0:T(8,128)(2,1)S(1)} %collective-permute-done.32.refs_5_), channel_id=1, source_target_pairs={{0,8},{8,0},{16,24},{24,16},{1,9},{9,1},{17,25},{25,17},{2,10},{10... | collective-permute-start | bytes 442376 | tf_op jit(solution)/shard_map/ppermute | solution.py:420
  148.5 2.8 %collective-permute-done.48 = f32[2,192]{1,0:T(2,128)S(1)} collective-permute-done((f32[2,192]{1,0:T(2,128)S(1)}, f32[2,192]{1,0:T(2,128)S(1)}, u32[]{:S(2)}, u32[]{:S(2)}) %collective-permute-start.48) | collective-permute-done | bytes 1568 | tf_op jit(solution)/shard_map/ppermute | solution.py:420
  151.5 4.4 %collective-permute-done.49 = f32[2,192]{1,0:T(2,128)S(1)} collective-permute-done((f32[2,192]{1,0:T(2,128)S(1)}, f32[2,192]{1,0:T(2,128)S(1)}, u32[]{:S(2)}, u32[]{:S(2)}) %collective-permute-start.49) | collective-permute-done | bytes 1568 | tf_op jit(solution)/shard_map/ppermute | solution.py:420
  158.0 2.5 %collective-permute-done.22 = f32[200,64]{1,0:T(8,128)S(1)} collective-permute-done((f32[200,64]{1,0:T(8,128)S(1)}, f32[200,64]{1,0:T(8,128)S(1)}, u32[]{:S(2)}, u32[]{:S(2)}) %collective-permute-start.22) | collective-permute-done | bytes 51232 | tf_op jit(solution)/shard_map/ppermute | solution.py:420
  (216 shorter events, 65.3 us)
Async XLA Ops:
  3.7 10.6 %collective-permute-start = (bf16[192,512]{1,0:T(8,128)(2,1)}, bf16[192,512]{1,0:T(8,128)(2,1)S(1)}, u32[]{:S(2)}, u32[]{:S(2)}) collective-permute-start(bf16[192,512]{1,0:T(8,128)(2,1)} %bitcast.50), channel_id=1, source_target_pairs={{0,1},{1,0},{2,3},{3,2},{4,5},{5,4},{6,7},{7,6},{8,9},{9,8},{10,11... | collective-permute-start | bytes 589832 | tf_op jit(solution)/shard_map/ppermute | solution.py:420
  27.1 12.1 %collective-permute-start.8 = (bf16[384,512]{1,0:T(8,128)(2,1)S(1)}, bf16[384,512]{1,0:T(8,128)(2,1)S(1)}, u32[]{:S(2)}, u32[]{:S(2)}) collective-permute-start(bf16[384,512]{1,0:T(8,128)(2,1)S(1)} %add_convert_fusion.3), channel_id=1, source_target_pairs={{0,2},{1,3},{2,0},{3,1},{4,6},{5,7},{6,4},{7,5},{8,10},{9,11},{10,... | collective-permute-start | bytes 1179656 | tf_op jit(solution)/shard_map/ppermute | solution.py:420
  27.5 15.1 %collective-permute-start.11 = (bf16[192,512]{1,0:T(8,128)(2,1)S(1)}, bf16[192,512]{1,0:T(8,128)(2,1)S(1)}, u32[]{:S(2)}, u32[]{:S(2)}) collective-permute-start(bf16[192,512]{1,0:T(8,128)(2,1)S(1)} %bitcast.53), channel_id=1, source_target_pairs={{0,2},{1,3},{2,0},{3,1},{4,6},{5,7},{6,4},{7,5},{8,10},{9,11},{10,... | collective-permute-start | bytes 589832 | tf_op jit(solution)/shard_map/ppermute | solution.py:420
  51.7 18.4 %collective-permute-start.13 = (bf16[2,192,512]{2,1,0:T(8,128)(2,1)}, bf16[2,192,512]{2,1,0:T(8,128)(2,1)}, u32[]{:S(2)}, u32[]{:S(2)}) collective-permute-start(bf16[2,192,512]{2,1,0:T(8,128)(2,1)} %get-tuple-element.64), channel_id=1, source_target_pairs={{0,1},{1,0},{2,3},{3,2},{4,5},{5,4},{6,7},{7,6},{8,9},{9,8},{10,11... | collective-permute-start | bytes 1179656 | tf_op jit(solution)/shard_map/ppermute | solution.py:420
  52.1 10.4 %collective-permute-start.41 = (bf16[224,768]{1,0:T(8,128)(2,1)}, bf16[224,768]{1,0:T(8,128)(2,1)}, u32[]{:S(2)}, u32[]{:S(2)}) collective-permute-start(bf16[224,768]{1,0:T(8,128)(2,1)} %get-tuple-element.96), channel_id=1, source_target_pairs={{0,8},{8,0},{16,24},{24,16},{1,9},{9,1},{17,25},{25,17},{2,10},{10... | collective-permute-start | bytes 1032200 | tf_op jit(solution)/shard_map/ppermute | solution.py:420
  53.7 12.6 %collective-permute-start.35 = (bf16[224,768]{1,0:T(8,128)(2,1)}, bf16[224,768]{1,0:T(8,128)(2,1)}, u32[]{:S(2)}, u32[]{:S(2)}) collective-permute-start(bf16[224,768]{1,0:T(8,128)(2,1)} %get-tuple-element.92), channel_id=1, source_target_pairs={{0,4},{4,0},{1,5},{5,1},{2,6},{6,2},{3,7},{7,3},{8,12},{12,8},{9,1... | collective-permute-start | bytes 1032200 | tf_op jit(solution)/shard_map/ppermute | solution.py:420
  56.1 15.4 %collective-permute-start.16 = (bf16[384,512]{1,0:T(8,128)(2,1)}, bf16[384,512]{1,0:T(8,128)(2,1)}, u32[]{:S(2)}, u32[]{:S(2)}) collective-permute-start(bf16[384,512]{1,0:T(8,128)(2,1)} %add_convert_fusion.1), channel_id=1, source_target_pairs={{0,2},{1,3},{2,0},{3,1},{4,6},{5,7},{6,4},{7,5},{8,10},{9,11},{10,... | collective-permute-start | bytes 1179656 | tf_op jit(solution)/shard_map/ppermute | solution.py:420
  68.5 17.5 %collective-permute-start.36 = (bf16[112,768]{1,0:T(8,128)(2,1)S(1)}, bf16[112,768]{1,0:T(8,128)(2,1)S(1)}, u32[]{:S(2)}, u32[]{:S(2)}) collective-permute-start(bf16[112,768]{1,0:T(8,128)(2,1)S(1)} %get-tuple-element.94), channel_id=1, source_target_pairs={{0,8},{8,0},{16,24},{24,16},{1,9},{9,1},{17,25},{25,17},{2,10},{10... | collective-permute-start | bytes 516104 | tf_op jit(solution)/shard_map/ppermute | solution.py:420
  73.8 60.8 %collective-permute-start.14 = (bf16[192,512]{1,0:T(8,128)(2,1)}, bf16[192,512]{1,0:T(8,128)(2,1)}, u32[]{:S(2)}, u32[]{:S(2)}) collective-permute-start(bf16[192,512]{1,0:T(8,128)(2,1)} %fusion.9), channel_id=1, source_target_pairs={{0,2},{1,3},{2,0},{3,1},{4,6},{5,7},{6,4},{7,5},{8,10},{9,11},{10,... | collective-permute-start | bytes 589832 | tf_op jit(solution)/shard_map/ppermute | solution.py:420
  74.4 12.6 %collective-permute-start.43 = (bf16[112,768]{1,0:T(8,128)(2,1)S(1)}, bf16[112,768]{1,0:T(8,128)(2,1)S(1)}, u32[]{:S(2)}, u32[]{:S(2)}) collective-permute-start(bf16[112,768]{1,0:T(8,128)(2,1)S(1)} %add_convert_fusion.5), channel_id=1, source_target_pairs={{0,16},{8,24},{16,0},{24,8},{1,17},{9,25},{17,1},{25,9},{2,18},{10... | collective-permute-start | bytes 516104 | tf_op jit(solution)/shard_map/ppermute | solution.py:420
  85.4 12.6 %collective-permute-start.29 = (bf16[192,768]{1,0:T(8,128)(2,1)S(1)}, bf16[192,768]{1,0:T(8,128)(2,1)S(1)}, u32[]{:S(2)}, u32[]{:S(2)}) collective-permute-start(bf16[192,768]{1,0:T(8,128)(2,1)S(1)} %get-tuple-element.86), channel_id=1, source_target_pairs={{0,8},{8,0},{16,24},{24,16},{1,9},{9,1},{17,25},{25,17},{2,10},{10... | collective-permute-start | bytes 884744 | tf_op jit(solution)/shard_map/ppermute | solution.py:420
  86.0 13.5 %collective-permute-start.37 = (bf16[112,768]{1,0:T(8,128)(2,1)S(1)}, bf16[112,768]{1,0:T(8,128)(2,1)S(1)}, u32[]{:S(2)}, u32[]{:S(2)}) collective-permute-start(bf16[112,768]{1,0:T(8,128)(2,1)S(1)} %add_convert_fusion.7), channel_id=1, source_target_pairs={{0,16},{8,24},{16,0},{24,8},{1,17},{9,25},{17,1},{25,9},{2,18},{10... | collective-permute-start | bytes 516104 | tf_op jit(solution)/shard_map/ppermute | solution.py:420
  86.4 16.3 %collective-permute-start.23 = (bf16[192,768]{1,0:T(8,128)(2,1)}, bf16[192,768]{1,0:T(8,128)(2,1)S(1)}, u32[]{:S(2)}, u32[]{:S(2)}) collective-permute-start(bf16[192,768]{1,0:T(8,128)(2,1)} %get-tuple-element.82), channel_id=1, source_target_pairs={{0,4},{4,0},{1,5},{5,1},{2,6},{6,2},{3,7},{7,3},{8,12},{12,8},{9,1... | collective-permute-start | bytes 884744 | tf_op jit(solution)/shard_map/ppermute | solution.py:420
  90.1 22.1 %collective-permute-start.18 = (bf16[2,192,640]{2,1,0:T(8,128)(2,1)}, bf16[2,192,640]{2,1,0:T(8,128)(2,1)}, u32[]{:S(2)}, u32[]{:S(2)}) collective-permute-start(bf16[2,192,640]{2,1,0:T(8,128)(2,1)} %get-tuple-element.79), channel_id=1, source_target_pairs={{0,1},{1,0},{2,3},{3,2},{4,5},{5,4},{6,7},{7,6},{8,9},{9,8},{10,11... | collective-permute-start | bytes 1474568 | tf_op jit(solution)/shard_map/ppermute | solution.py:420
  101.1 26.2 %collective-permute-start.44 = (bf16[112,768]{1,0:T(8,128)(2,1)S(1)}, bf16[112,768]{1,0:T(8,128)(2,1)S(1)}, u32[]{:S(2)}, u32[]{:S(2)}) collective-permute-start(bf16[112,768]{1,0:T(8,128)(2,1)S(1)} %add_convert_fusion.4.refs_4_), channel_id=1, source_target_pairs={{0,4},{4,0},{1,5},{5,1},{2,6},{6,2},{3,7},{7,3},{8,12},{12,8},{9,1... | collective-permute-start | bytes 516104 | tf_op jit(solution)/shard_map/ppermute | solution.py:420
  102.7 33.4 %collective-permute-start.45 = (bf16[112,768]{1,0:T(8,128)(2,1)S(1)}, bf16[112,768]{1,0:T(8,128)(2,1)S(1)}, u32[]{:S(2)}, u32[]{:S(2)}) collective-permute-start(bf16[112,768]{1,0:T(8,128)(2,1)S(1)} %add_convert_fusion.4.refs_4_), channel_id=1, source_target_pairs={{0,8},{8,0},{16,24},{24,16},{1,9},{9,1},{17,25},{25,17},{2,10},{10... | collective-permute-start | bytes 516104 | tf_op jit(solution)/shard_map/ppermute | solution.py:420
  112.1 12.0 %collective-permute-start.31 = (bf16[96,768]{1,0:T(8,128)(2,1)S(1)}, bf16[96,768]{1,0:T(8,128)(2,1)S(1)}, u32[]{:S(2)}, u32[]{:S(2)}) collective-permute-start(bf16[96,768]{1,0:T(8,128)(2,1)S(1)} %add_convert_fusion.9), channel_id=1, source_target_pairs={{0,16},{8,24},{16,0},{24,8},{1,17},{9,25},{17,1},{25,9},{2,18},{10... | collective-permute-start | bytes 442376 | tf_op jit(solution)/shard_map/ppermute | solution.py:420
  112.2 15.1 %collective-permute-start.25 = (bf16[96,768]{1,0:T(8,128)(2,1)S(1)}, bf16[96,768]{1,0:T(8,128)(2,1)S(1)}, u32[]{:S(2)}, u32[]{:S(2)}) collective-permute-start(bf16[96,768]{1,0:T(8,128)(2,1)S(1)} %add_convert_fusion.11), channel_id=1, source_target_pairs={{0,16},{8,24},{16,0},{24,8},{1,17},{9,25},{17,1},{25,9},{2,18},{10... | collective-permute-start | bytes 442376 | tf_op jit(solution)/shard_map/ppermute | solution.py:420
  124.2 9.6 %collective-permute-start.19 = (bf16[192,640]{1,0:T(8,128)(2,1)S(1)}, bf16[192,640]{1,0:T(8,128)(2,1)S(1)}, u32[]{:S(2)}, u32[]{:S(2)}) collective-permute-start(bf16[192,640]{1,0:T(8,128)(2,1)S(1)} %fusion.8), channel_id=1, source_target_pairs={{0,2},{1,3},{2,0},{3,1},{4,6},{5,7},{6,4},{7,5},{8,10},{9,11},{10,... | collective-permute-start | bytes 737288 | tf_op jit(solution)/shard_map/ppermute | solution.py:420
  127.3 10.4 %collective-permute-start.39 = (bf16[112,768]{1,0:T(8,128)(2,1)S(1)}, bf16[112,768]{1,0:T(8,128)(2,1)S(1)}, u32[]{:S(2)}, u32[]{:S(2)}) collective-permute-start(bf16[112,768]{1,0:T(8,128)(2,1)S(1)} %add_convert_fusion.6.refs_0_), channel_id=1, source_target_pairs={{0,4},{4,0},{1,5},{5,1},{2,6},{6,2},{3,7},{7,3},{8,12},{12,8},{9,1... | collective-permute-start | bytes 516104 | tf_op jit(solution)/shard_map/ppermute | solution.py:420
  143.5 18.3 %collective-permute-start.33 = (bf16[96,768]{1,0:T(8,128)(2,1)S(1)}, bf16[96,768]{1,0:T(8,128)(2,1)S(1)}, u32[]{:S(2)}, u32[]{:S(2)}) collective-permute-start(bf16[96,768]{1,0:T(8,128)(2,1)S(1)} %add_convert_fusion.8.refs_4_), channel_id=1, source_target_pairs={{0,8},{8,0},{16,24},{24,16},{1,9},{9,1},{17,25},{25,17},{2,10},{10... | collective-permute-start | bytes 442376 | tf_op jit(solution)/shard_map/ppermute | solution.py:420
  144.2 17.7 %collective-permute-start.27 = (bf16[96,768]{1,0:T(8,128)(2,1)S(1)}, bf16[96,768]{1,0:T(8,128)(2,1)S(1)}, u32[]{:S(2)}, u32[]{:S(2)}) collective-permute-start(bf16[96,768]{1,0:T(8,128)(2,1)S(1)} %add_convert_fusion.10.refs_0_), channel_id=1, source_target_pairs={{0,4},{4,0},{1,5},{5,1},{2,6},{6,2},{3,7},{7,3},{8,12},{12,8},{9,1... | collective-permute-start | bytes 442376 | tf_op jit(solution)/shard_map/ppermute | solution.py:420
  145.4 16.4 %collective-permute-start.34 = (bf16[96,768]{1,0:T(8,128)(2,1)S(1)}, bf16[96,768]{1,0:T(8,128)(2,1)S(1)}, u32[]{:S(2)}, u32[]{:S(2)}) collective-permute-start(bf16[96,768]{1,0:T(8,128)(2,1)S(1)} %collective-permute-done.32.refs_5_), channel_id=1, source_target_pairs={{0,8},{8,0},{16,24},{24,16},{1,9},{9,1},{17,25},{25,17},{2,10},{10... | collective-permute-start | bytes 442376 | tf_op jit(solution)/shard_map/ppermute | solution.py:420
  147.2 14.7 %collective-permute-start.28 = (bf16[96,768]{1,0:T(8,128)(2,1)S(1)}, bf16[96,768]{1,0:T(8,128)(2,1)S(1)}, u32[]{:S(2)}, u32[]{:S(2)}) collective-permute-start(bf16[96,768]{1,0:T(8,128)(2,1)S(1)} %collective-permute-done.26.refs_1_), channel_id=1, source_target_pairs={{0,4},{4,0},{1,5},{5,1},{2,6},{6,2},{3,7},{7,3},{8,12},{12,8},{9,1... | collective-permute-start | bytes 442376 | tf_op jit(solution)/shard_map/ppermute | solution.py:420
  (68 other events, 534.8 us)

commit v3 on v2

--- a/solution.py
+++ b/solution.py
@@ -8,10 +8,12 @@
 from jax.experimental.pallas import tpu as pltpu
 from jax.sharding import PartitionSpec as P
 
+
 HEAD = 64
 HALF = 64
 TILE = 2 * HALF
 STEP = 64
+GRANT = 8 * 1024 * 1024
 F32 = jnp.float32
 BF16 = jnp.bfloat16
 
@@ -21,15 +23,21 @@
     return math.prod(shape[:-1]) * lanes * jnp.dtype(dtype).itemsize
 
 
-def call(kernel, outs, scratch, *args):
-    arrays = list(outs) + list(scratch) + [(a.shape, a.dtype) for a in args]
-    grant = sum(room(s, t) for s, t in arrays) + 4 * 1024 * 1024
-    return pl.pallas_call(
+def call(kernel, outs, scratch, *args, loads=0):
+    grant = sum(room(s, t) for s, t in scratch) + GRANT
+    extra = [pltpu.SemaphoreType.DMA((loads,))] if loads else []
+    spaces = [pltpu.VMEM] * (len(args) - loads) + [pltpu.HBM] * loads
+    run = pl.pallas_call(
         kernel,
         out_shape=tuple(jax.ShapeDtypeStruct(s, t) for s, t in outs),
-        scratch_shapes=[pltpu.VMEM(s, t) for s, t in scratch],
+        in_specs=[pl.BlockSpec(memory_space=space) for space in spaces],
+        scratch_shapes=[pltpu.VMEM(s, t) for s, t in scratch] + extra,
         compiler_params=pltpu.CompilerParams(vmem_limit_bytes=grant),
-    )(*args)
+    )
+    if loads:
+        far = [pltpu.with_memory_space_constraint(a, pltpu.HBM) for a in args[-loads:]]
+        args = args[:-loads] + tuple(far)
+    return run(*args)
 
 
 def nn(a, b):
@@ -85,20 +93,18 @@
     row_loop(rows, 16, one, 0)
 
 
-def split_shards(source, keep, send, core):
-    share = keep.shape[1]
-    for x in range(2):
-        mine = pl.multiple_of((2 * x + core) * share, share)
-        other = pl.multiple_of((2 * x + 1 - core) * share, share)
-        keep[x] = source[pl.ds(mine, share), :]
-        send[x] = source[pl.ds(other, share), :].astype(send.dtype)
-
-
 def attention_kernel(
-    p0, p1, p2, p3, h0, h1, h2, h3, gain, w, wo, cos, sin,
+    p1, p2, p3, h0, h1, h2, h3, gain, cos, sin, p0_far, w_far, wo_far,
     xall, stats, fed, q, kw, vw, totals, mixed, keep, send,
-    proj, terms,
+    proj, terms, p0, w, wo, sems,
 ):
+    copies = [
+        pltpu.make_async_copy(p0_far, p0, sems.at[0]),
+        pltpu.make_async_copy(w_far, w, sems.at[1]),
+        pltpu.make_async_copy(wo_far, wo, sems.at[2]),
+    ]
+    for copy in copies:
+        copy.start()
     width, tokens = xall.shape
     length = q.shape[1]
     columns = q.shape[0]
@@ -106,8 +112,9 @@
     core = lax.axis_index("mp") % 2
     first = lax.axis_index("seq") * length
     total = lax.axis_size("seq") * length
+    gather_rows((h0, h1, h2, h3), xall, slice(length, tokens))
+    copies[0].wait()
     gather_rows((p0, p1, p2, p3), xall, slice(0, length))
-    gather_rows((h0, h1, h2, h3), xall, slice(length, tokens))
 
     def add(r, acc):
         return acc + fold(xall[pl.ds(r, STEP), :].astype(F32))
@@ -131,6 +138,7 @@
         return carry
 
     row_loop(width, STEP, feed, 0)
+    copies[1].wait()
     proj[...] = nn(w[...], fed[...])
     half = HEAD // 2
 
@@ -166,6 +174,7 @@
         return carry
 
     lax.fori_loop(0, heads, one_head, 0)
+    copies[2].wait()
     terms[...] = tn(wo[...], mixed[...])
     split_half(terms, keep, send, core)
 
@@ -233,18 +242,15 @@
     split_half(terms, keep, send, core)
 
 
-def geglu_weights_kernel(product, lifted_grad, fed, upstream, gout, *rest, cuts):
-    outs, (terms, stack) = rest[:-2], rest[-2:]
-    core = lax.axis_index("mp") % 2
-    terms[...] = tn(gout[...], product[...])
-    split_shards(terms, outs[0], outs[1], core)
+def geglu_weights_kernel(product, lifted_grad, fed, upstream, *rest, cuts):
+    outs, stack = rest[:-1], rest[-1]
     count = lifted_grad.shape[0]
     units = product.shape[0]
     stack[0:count, :] = nt(lifted_grad[...], fed[...])
     stack[count : count + units, :] = nt(product[...], upstream[...])
     if stack.shape[0] > count + units:
         stack[count + units :, :] = jnp.zeros((stack.shape[0] - count - units, stack.shape[1]), F32)
-    emit_units(stack, outs[2:], cuts)
+    emit_units(stack, outs, cuts)
 
 
 def emit_units(stack, outs, cuts):
@@ -358,26 +364,99 @@
     emit_units(stack, outs[3:], cuts)
 
 
-def input_terms_kernel(proj_grad, w, gain, xall, stats, keep, send, sums, terms):
-    width, tokens = terms.shape
-    core = lax.axis_index("mp") % 2
-    terms[...] = tn(w[...], proj_grad[...])
+def terms_kernel(
+    proj_grad, w, gain, xall, stats, gout, product,
+    keep, send, terms,
+):
+    width, tokens = xall.shape
+    share = (keep.shape[0] - 16) // 2
+    me = lax.axis_index("mp")
+    core = me % 2
+    terms[:, 0:tokens] = tn(w[...], proj_grad[...])
     mean = stats[0:1, :]
     inverse = stats[1:2, :]
 
     def add(r, acc):
         a, b = acc
         at = pl.ds(r, STEP)
-        hat = terms[at, :] * gain[at, 0:1]
+        hat = terms[at, 0:tokens] * gain[at, 0:1]
         normed = (xall[at, :].astype(F32) - mean) * inverse
         return a + fold(hat), b + fold(hat * normed)
 
     zero = jnp.zeros((8, tokens), F32)
     a, b = row_loop(width, STEP, add, (zero, zero))
-    sums[0:1, :] = jnp.sum(a, axis=0, keepdims=True) / width
-    sums[1:2, :] = jnp.sum(b, axis=0, keepdims=True) / width
-    sums[2:8, :] = jnp.zeros((6, tokens), F32)
-    split_shards(terms, keep, send, core)
+    one = jnp.sum(a, axis=0, keepdims=True) / width
+    two = jnp.sum(b, axis=0, keepdims=True) / width
+    terms[:, tokens:] = tn(gout[...], product[...])
+    for x in range(2):
+        mine = pl.multiple_of((2 * x + core) * share, share)
+        other = pl.multiple_of((2 * x + 1 - core) * share, share)
+        at = slice(x * share, (x + 1) * share)
+        keep[at, :] = terms[pl.ds(mine, share), :]
+        send[at, :] = terms[pl.ds(other, share), :].astype(BF16)
+    rest = slice(2 * share, 2 * share + 16)
+    row = lax.broadcasted_iota(jnp.int32, (16, tokens), 0)
+    sums = jnp.where(row == 0, one, jnp.where(row == 1, two, 0.0))
+    keep[rest, 0:tokens] = sums
+    send[rest, 0:tokens] = sums.astype(BF16)
+    keep[rest, tokens:] = jnp.zeros((16, terms.shape[1] - tokens), F32)
+    send[rest, tokens:] = jnp.zeros((16, terms.shape[1] - tokens), BF16)
+
+
+def own_rows_kernel(xall, stats, out):
+    share = out.shape[0]
+    own = pl.ds(pl.multiple_of(lax.axis_index("mp") * share, share), share)
+    out[...] = (xall[own, :].astype(F32) - stats[0:1, :]) * stats[1:2, :]
+
+
+def across_kernel(keep, got, own, away):
+    share = (keep.shape[0] - 16) // 2
+    x = lax.axis_index("mp") // 2
+    for out, index in ((own, x), (away, 1 - x)):
+        at = pl.ds(pl.multiple_of(index * share, share), share)
+        out[0:share, :] = (keep[at, :] + got[at, :].astype(F32)).astype(out.dtype)
+        last = slice(2 * share, 2 * share + 16)
+        out[share : share + 16, :] = (keep[last, :] + got[last, :].astype(F32)).astype(out.dtype)
+
+
+def finish_kernel(own, got, middle, normed, gain_lanes, layer_out, main, edges, gains):
+    share, length = middle.shape
+    tokens = normed.shape[1]
+    layer_out[...] = middle[...] + own[0:share, tokens:] + got[0:share, tokens:].astype(F32)
+    main[...] = own[:, 0:length] + got[:, 0:length].astype(F32)
+    edges[...] = own[:, length:tokens] + got[:, length:tokens].astype(F32)
+    weighted = gain_lanes[...], main[0:share, :] * normed[:, 0:length]
+    last = edges[0:share, :] * normed[:, length:tokens]
+    exact = functools.partial(
+        lax.dot_general,
+        dimension_numbers=(((1,), (1,)), ((), ())),
+        precision=lax.Precision.HIGHEST,
+        preferred_element_type=F32,
+    )
+    one = exact(jnp.ones((8, length), F32), weighted[1])
+    gains[0:8, :] = one + exact(jnp.ones((8, tokens - length), F32), last)
+    gains[8:16, :] = exact(jnp.ones((8, gain_lanes.shape[1]), F32), weighted[0])
+
+
+def input_kernel(main, low, high, middle_grad, stats, normed, gain, out):
+    share, length = out.shape
+    own = pl.ds(pl.multiple_of(lax.axis_index("mp") * share, share), share)
+    pad = jnp.zeros((main.shape[0], HALF), F32)
+    ends = (
+        jnp.concatenate([low[...], pad], axis=1),
+        jnp.concatenate([pad, high[...]], axis=1),
+    )
+    for j in range(length // 128):
+        at = slice(j * 128, (j + 1) * 128)
+        both = main[:, at]
+        if j == 0:
+            both = both + ends[0]
+        if j == length // 128 - 1:
+            both = both + ends[1]
+        hat = both[0:share] * gain[own, 0:1]
+        one = both[share : share + 1]
+        two = both[share + 1 : share + 2]
+        out[:, at] = middle_grad[:, at] + stats[1:2, at] * (hat - one - normed[:, at] * two)
 
 
 def halves_kernel(keep, got, out_keep, out_send, *, axis):
@@ -395,18 +474,23 @@
     row_loop(rows, 16, one, 0)
 
 
+def join_kernel(mine, other, out, *, axis):
+    rows = mine.shape[0]
+    index = lax.axis_index(axis) % 2
+    out[pl.ds(pl.multiple_of(index * rows, 16), rows), :] = mine[...]
+    out[pl.ds(pl.multiple_of((1 - index) * rows, 16), rows), :] = other[...]
+
+
 def place_kernel(*refs, cuts, outs):
     count = len(cuts)
-    pieces, targets, stack = refs[: 4 * count], refs[4 * count : -1], refs[-1]
+    pieces, targets, stack = refs[: 2 * count], refs[2 * count : -1], refs[-1]
     start = 0
     for i, (rows, order) in enumerate(cuts):
-        size = rows // 4
-        one, two = (lax.axis_index(axis) % 2 for axis in order)
-        for k in range(4):
-            far = one if k < 2 else 1 - one
-            near = two if k % 2 == 0 else 1 - two
-            at = pl.multiple_of(start + (2 * far + near) * size, 16)
-            stack[pl.ds(at, size), :] = pieces[4 * i + k][...].astype(F32)
+        size = rows // 2
+        index = lax.axis_index(order[0]) % 2
+        for k, at in enumerate((index, 1 - index)):
+            at = pl.multiple_of(start + at * size, 16)
+            stack[pl.ds(at, size), :] = pieces[2 * i + k][...].astype(F32)
         start += rows
     for target, spans in zip(targets, outs):
         at = 0
@@ -425,17 +509,23 @@
     return shard, flip(shard, "mp", 1), across, flip(across, "mp", 1)
 
 
+def held(x, other):
+    return lax.optimization_barrier((x, other))[0]
+
+
 def sum_halves(keep, send):
     half = (keep + flip(send, "mp", 1).astype(F32)).astype(BF16)
-    total = (half.astype(F32) + flip(half, "mp", 2).astype(F32)).astype(BF16)
-    return total, flip(total, "mp", 1)
+    across = flip(half, "mp", 2)
+    total = (half.astype(F32) + across.astype(F32)).astype(BF16)
+    return total, flip(total, "mp", 1), half
 
 
 def scatter_shards(keep, send):
-    x = lax.axis_index("mp") // 2
-    half = keep + flip(send, "mp", 1).astype(F32)
-    away = jnp.where(x == 0, half[1], half[0]).astype(BF16)
-    return jnp.where(x == 0, half[0], half[1]) + flip(away, "mp", 2).astype(F32)
+    rows, lanes = keep.shape
+    rows = (rows - 16) // 2 + 16
+    got = flip(send, "mp", 1)
+    own, away = call(across_kernel, [((rows, lanes), F32), ((rows, lanes), BF16)], [], keep, got)
+    return own, flip(away, "mp", 2)
 
 
 def to_neighbours(low, high):
@@ -457,9 +547,9 @@
 def sum_blocks(x):
     if not staged():
         return lax.psum(x, ("dp", "seq"))
-    x = x + flip(x, "seq", 1)
-    x = x + flip(x, "dp", 1)
-    return x + flip(x, "dp", 2)
+    for axis, bit in (("seq", 1), ("dp", 1), ("dp", 2)):
+        x = x + flip(x, axis, bit)
+    return x
 
 
 def reduce_unit(keep, send, order):
@@ -473,20 +563,34 @@
         keep,
         got,
     )
-    part = (keep + flip(send, two, 1).astype(F32)).astype(BF16)
-    total = (part.astype(F32) + flip(part, "dp", 2).astype(F32)).astype(BF16)
+    got = flip(send, two, 1)
+    part = (keep + got.astype(F32)).astype(BF16)
+    got = flip(part, "dp", 2)
+    total = (part.astype(F32) + got.astype(F32)).astype(BF16)
     beside = flip(total, two, 1)
-    return total, beside, flip(total, one, 1), flip(beside, one, 1)
-
-
-def reduce_stack(parts, cuts, spans, width):
-    sizes = [(sum(size for _, size in span), width) for span in spans]
+    (half,) = call(
+        functools.partial(join_kernel, axis=two),
+        [((rows, width), BF16)],
+        [],
+        total,
+        beside,
+    )
+    return half, flip(half, one, 1)
+
+
+def reduce_stack(parts, cuts):
     if cuts is None:
-        total = lax.psum(parts[0], ("dp", "seq"))
-        return [jnp.concatenate([total[b : b + n] for b, n in span]) for span in spans]
+        return [lax.psum(parts[0], ("dp", "seq"))]
     pieces = []
     for i, (_, order) in enumerate(cuts):
         pieces.extend(reduce_unit(parts[2 * i], parts[2 * i + 1], order))
+    return pieces
+
+
+def place_stack(pieces, cuts, spans, width):
+    sizes = [(sum(size for _, size in span), width) for span in spans]
+    if cuts is None:
+        return [jnp.concatenate([pieces[0][b : b + n] for b, n in span]) for span in spans]
     kernel = functools.partial(place_kernel, cuts=cuts, outs=spans)
     scratch = [((sum(rows for rows, _ in cuts), width), F32)]
     return call(kernel, [(size, F32) for size in sizes], scratch, *pieces)
@@ -519,7 +623,7 @@
     tokens = length + TILE
     half = width // 2
     orders = (("seq", "dp"), ("dp", "seq"))
-    grain = 4 * 16
+    grain = 8 * 16
     x_own = hidden_in[0].T
     u_own = cotangent[0].T
     w = jnp.transpose(qkv_weight, (1, 2, 0)).reshape(3 * columns, width)
@@ -553,10 +657,17 @@
             ((half, length), F32),
             ((half, length), BF16),
         ],
-        [((3 * columns, tokens), F32), ((width, length), F32)],
-        *x_parts, *h_parts, gains, w, attention_out, cos, sin,
-    )
-    mine, other = sum_halves(keep, send)
+        [
+            ((3 * columns, tokens), F32),
+            ((width, length), F32),
+            ((share, length), BF16),
+            ((3 * columns, width), BF16),
+            ((columns, width), BF16),
+        ],
+        *x_parts[1:], *h_parts, gains, cos, sin, x_own, w, attention_out,
+        loads=3,
+    )
+    mine, other, _ = sum_halves(keep, send)
     middle_own, normed, inverse, fed_two, upstream, product, lifted_grad, keep, send = call(
         geglu_kernel,
         [
@@ -578,25 +689,23 @@
         ],
         xall, mine, other, *u_parts, gains, win, geglu_out,
     )
-    mine, other = sum_halves(keep, send)
-
+    mine, other, half_sent = sum_halves(keep, send)
+
+    (normed_own,) = call(
+        own_rows_kernel, [((share, tokens), F32)], [], xall, held(stats, half_sent)
+    )
     rows = 3 * units
-    padded = -(-rows // (2 * grain)) * (2 * grain) if staged() else rows
+    padded = -(-rows // grain) * grain if staged() else rows
     geglu_cuts = tuple((padded // 2, order) for order in orders) if staged() else None
-    shard_shapes = [((2, share, length), F32), ((2, share, length), BF16)]
-    outs = call(
+    geglu_parts = call(
         functools.partial(geglu_weights_kernel, cuts=geglu_cuts),
-        shard_shapes + unit_shapes(geglu_cuts, padded, width),
-        [((width, length), F32), ((padded, width), F32)],
-        product, lifted_grad, fed_two, upstream, geglu_out,
-    )
-    layer_out = middle_own + scatter_shards(outs[0], outs[1])
-    grad_in, grad_out = reduce_stack(
-        outs[2:], geglu_cuts, (((0, 2 * units),), ((2 * units, units),)), width
+        unit_shapes(geglu_cuts, padded, width),
+        [((padded, width), F32)],
+        held(product, half_sent), lifted_grad, fed_two, upstream,
     )
 
     back_cuts = None
-    if staged() and 2 * columns % grain == 0:
+    if staged() and 4 * columns % grain == 0:
         back_cuts = tuple((2 * columns, order) for order in orders)
     outs = call(
         functools.partial(attention_back_kernel, cuts=back_cuts),
@@ -614,41 +723,44 @@
         q, kw, vw, totals, mixed, cos, sin, fed,
     )
     middle_grad, gain_two_lanes, proj_grad = outs[:3]
-    grad_qkv, grad_attention_out = reduce_stack(
-        outs[3:],
+    pieces = reduce_stack(geglu_parts, geglu_cuts)
+    grad_in, grad_out = place_stack(
+        pieces, geglu_cuts, (((0, 2 * units),), ((2 * units, units),)), width
+    )
+    back_pieces = reduce_stack(outs[3:], back_cuts)
+
+    lanes = tokens + length
+    keep, send = call(
+        terms_kernel,
+        [((2 * share + 16, lanes), F32), ((2 * share + 16, lanes), BF16)],
+        [((width, lanes), F32)],
+        proj_grad, w, gains, xall, stats, geglu_out, product,
+    )
+    own, got = scatter_shards(keep, send)
+    layer_out, main, edges, gain_sums = call(
+        finish_kernel,
+        [
+            ((share, length), F32),
+            ((share + 16, length), F32),
+            ((share + 16, TILE), F32),
+            ((16, share), F32),
+        ],
+        [],
+        own, got, middle_own, normed_own, gain_two_lanes,
+    )
+    high_add, low_add = to_neighbours(edges[:, HALF:], edges[:, :HALF])
+    gain_sums = sum_blocks(gain_sums)
+    (grad_input,) = call(
+        input_kernel,
+        [((share, length), F32)],
+        [],
+        main, low_add, high_add, middle_grad, stats, normed_own, gains,
+    )
+    grad_qkv, grad_attention_out = place_stack(
+        held(back_pieces, (gain_sums, grad_input, layer_out)),
         back_cuts,
         (((2 * columns, 2 * columns), (0, columns)), ((columns, columns),)),
         width,
-    )
-
-    keep, send, sums = call(
-        input_terms_kernel,
-        [((2, share, tokens), F32), ((2, share, tokens), BF16), ((8, tokens), F32)],
-        [((width, tokens), F32)],
-        proj_grad, w, gains, xall, stats,
-    )
-    grad_one = scatter_shards(keep, send)
-    sums = sums + flip(sums, "mp", 1)
-    sums = sums + flip(sums, "mp", 2)
-    offset = lax.axis_index("mp") * share
-    x_all_own = lax.dynamic_slice_in_dim(xall, offset, share, 0).astype(F32)
-    normed_own = (x_all_own - stats[0:1]) * stats[1:2]
-    gain_one_grad = jnp.sum(grad_one * normed_own, axis=1)
-    gain_two_grad = jnp.sum(gain_two_lanes, axis=1)
-    gains = sum_blocks(jnp.stack([gain_one_grad, gain_two_grad]))
-    both = jnp.concatenate([grad_one, sums], axis=0)
-    high_add, low_add = to_neighbours(both[:, length + HALF :], both[:, length : length + HALF])
-    both = jnp.concatenate(
-        [
-            both[:, :HALF] + low_add,
-            both[:, HALF : length - HALF],
-            both[:, length - HALF : length] + high_add,
-        ],
-        axis=1,
-    )
-    hat = both[:share] * lax.dynamic_slice_in_dim(attention_gain, offset, share, 0)[:, None]
-    grad_input = middle_grad + stats[1:2, :length] * (
-        hat - both[share : share + 1] - normed_own[:, :length] * both[share + 1 : share + 2]
     )
     return (
         layer_out.T[None],
@@ -657,8 +769,8 @@
         grad_attention_out,
         jnp.transpose(grad_in.reshape(2, units, width), (2, 0, 1)),
         grad_out,
-        gains[0],
-        gains[1],
+        gain_sums[0],
+        gain_sums[8],
     )
 
 
@@ -683,4 +795,5 @@
         P("mp"),
         P("mp"),
     )
+
     return jax.shard_map(body, mesh=mesh, in_specs=in_specs, out_specs=out_specs, check_vma=False)

time: 164 us -> 135 us (0.82)
  local copies, waits for them, and re-layouts: 13.8 us -> 2.16 us
  other arithmetic: 13 us -> 2.26 us
  waiting for transfers between devices: 63.2 us -> 55 us
  starting transfers between devices: 40.4 us -> 43.4 us
    ppermute x50 -> x42, waiting for transfers between devices: 63.2 us -> 55 us  [flip(): return lax.ppermute(x, axis, [(i, i ^ bit) for i in range(count)])]
    unnamed x84 -> x10, local copies, waits for them, and re-layouts: 7.6 us -> 0.02 us
    convert_element_type x12 -> x10, other arithmetic: 3.66 us -> 0.49 us  [the longest x2 0.19 us: sum_halves(): total = (half.astype(F32) + across.astype(F32)).astype(BF16)]
    ppermute x50 -> x42, starting transfers between devices: 40.4 us -> 43.4 us  [flip(): return lax.ppermute(x, axis, [(i, i ^ bit) for i in range(count)])]
    slice x3 -> x1, local copies, waits for them, and re-layouts: 3.28 us -> 0.57 us  [body(): gain_sums[8]]
    broadcast_in_dim x2 -> x0, other arithmetic: 2.69 us -> none  [the longest x1 1.8 us: body(): layer_out.T[None]]
    add x8 -> x3, other arithmetic: 2.52 us -> 0.01 us  [sum_blocks(): x = x + flip(x, axis, bit)]
    pallas_call x11 -> x19, Pallas kernels: 31.9 us -> 30.8 us  [call(): return run(*args)]
  transfers between devices with their start and end apart: 50 -> 42, of which waited for: 17 -> 20; matrix products, arithmetic and copies ran while one was open for 12% -> 3% of each run, Pallas kernels for 12% -> 13%
where the time goes in v3:
time: 135 us; the launch traced here: 134 us
  waiting for transfers between devices  55 us (41%)
  starting transfers between devices  43.4 us (32%)
  Pallas kernels  30.8 us (23%)
  other arithmetic  2.26 us (2%)
  local copies, waits for them, and re-layouts  2.16 us (2%)
    ppermute x42, waiting for transfers between devices, flip(): return lax.ppermute(x, axis, [(i, i ^ bit) for i in range(count)])  55 us
    ppermute x42, starting transfers between devices, flip(): return lax.ppermute(x, axis, [(i, i ^ bit) for i in range(count)])  43.4 us
    pallas_call x19, Pallas kernels, call(): return run(*args)  30.8 us
  transfers between devices with their start and end apart: 42, of which 20 were waited for; matrix products, arithmetic and copies ran while one was open for 3% of the time, Pallas kernels for 13%

profile of v3, /device:TPU:0, one launch (start us, length us, event | category | flops | bytes accessed | tf_op | source)
XLA Modules:
  0.0 134.5 jit_solution(8813169717567380684)
XLA Ops:
  0.6 3.0 %collective-permute-start.1 = (bf16[192,512]{1,0:T(8,128)(2,1)}, bf16[192,512]{1,0:T(8,128)(2,1)S(1)}, u32[]{:S(2)}, u32[]{:S(2)}) collective-permute-start(bf16[192,512]{1,0:T(8,128)(2,1)} %bitcast.32), channel_id=1, source_target_pairs={{0,2},{1,3},{2,0},{3,1},{4,6},{5,7},{6,4},{7,5},{8,10},{9,11},{10,... | collective-permute-start | bytes 589832 | tf_op jit(solution)/shard_map/ppermute | solution.py:504
  6.2 2.6 %collective-permute-done.3 = bf16[192,64]{1,0:T(8,128)(2,1)S(1)} collective-permute-done((bf16[192,64]{1,0:T(8,128)(2,1)S(1)}, bf16[192,64]{1,0:T(8,128)(2,1)S(1)}, u32[]{:S(2)}, u32[]{:S(2)}) %collective-permute-start.3) | collective-permute-done | bytes 24608 | tf_op jit(solution)/shard_map/ppermute | solution.py:504
  14.3 8.2 %shard_map.143 = (bf16[768,640]{1,0:T(8,128)(2,1)S(1)}, f32[8,640]{1,0:T(8,128)S(1)}, bf16[768,640]{1,0:T(8,128)(2,1)S(1)}, bf16[192,512]{1,0:T(8,128)(2,1)S(1)}...) custom-call(bf16[192,512]{1,0:T(8,128)(2,1)S(1)} %collective-permute, ...), custom_call_target="tpu_custom_call" | custom-call | tf_op jit(solution)/shard_map/pallas_call | solution.py:40
  24.8 1.7 %collective-permute-start.11 = (bf16[192,512]{1,0:T(8,128)(2,1)S(1)}, bf16[192,512]{1,0:T(8,128)(2,1)S(1)}, u32[]{:S(2)}, u32[]{:S(2)}) collective-permute-start(bf16[192,512]{1,0:T(8,128)(2,1)S(1)} %bitcast.29), channel_id=1, source_target_pairs={{0,2},{1,3},{2,0},{3,1},{4,6},{5,7},{6,4},{7,5},{8,10},{9,11},{10,... | collective-permute-start | bytes 589832 | tf_op jit(solution)/shard_map/ppermute | solution.py:504
  26.6 10.0 %collective-permute-done.8 = bf16[384,512]{1,0:T(8,128)(2,1)S(1)} collective-permute-done((bf16[384,512]{1,0:T(8,128)(2,1)S(1)}, bf16[384,512]{1,0:T(8,128)(2,1)S(1)}, u32[]{:S(2)}, u32[]{:S(2)}) %collective-permute-start.8) | collective-permute-done | bytes 393248 | tf_op jit(solution)/shard_map/ppermute | solution.py:504
  37.2 2.7 %collective-permute-done.11.u2 = bf16[192,512]{1,0:T(8,128)(2,1)S(1)} collective-permute-done((bf16[192,512]{1,0:T(8,128)(2,1)S(1)}, bf16[192,512]{1,0:T(8,128)(2,1)S(1)}, u32[]{:S(2)}, u32[]{:S(2)}) %collective-permute-start.11) | collective-permute-done | bytes 196640 | tf_op jit(solution)/shard_map/ppermute | solution.py:504
  41.4 3.8 %shard_map.144 = (f32[192,512]{1,0:T(8,128)S(1)}, f32[768,512]{1,0:T(8,128)S(1)}, f32[8,512]{1,0:T(8,128)S(1)}, bf16[768,512]{1,0:T(8,128)(2,1)S(1)}, bf16[768,5...) custom-call(bf16[768,640]{1,0:T(8,128)(2,1)S(1)} %get-tuple-element., ...), custom_call_target="tpu_custom_call" | custom-call | tf_op jit(solution)/shard_map/pallas_call | solution.py:40
  48.7 1.8 %collective-permute-start.32 = (bf16[224,768]{1,0:T(8,128)(2,1)S(1)}, bf16[224,768]{1,0:T(8,128)(2,1)S(1)}, u32[]{:S(2)}, u32[]{:S(2)}) collective-permute-start(bf16[224,768]{1,0:T(8,128)(2,1)S(1)} %get-tuple-element.111), channel_id=1, source_target_pairs={{0,4},{4,0},{1,5},{5,1},{2,6},{6,2},{3,7},{7,3},{8,12},{12,8},{9,1... | collective-permute-start | bytes 1032200 | tf_op jit(solution)/shard_map/ppermute | solution.py:504
  52.1 6.5 %collective-permute-done.32.got = bf16[224,768]{1,0:T(8,128)(2,1)S(1)} collective-permute-done((bf16[224,768]{1,0:T(8,128)(2,1)S(1)}, bf16[224,768]{1,0:T(8,128)(2,1)S(1)}, u32[]{:S(2)}, u32[]{:S(2)}) %collective-permute-start.32) | collective-permute-done | bytes 344096 | tf_op jit(solution)/shard_map/ppermute | solution.py:504
  58.7 1.8 %collective-permute-start.33 = (bf16[112,768]{1,0:T(8,128)(2,1)S(1)}, bf16[112,768]{1,0:T(8,128)(2,1)S(1)}, u32[]{:S(2)}, u32[]{:S(2)}) collective-permute-start(bf16[112,768]{1,0:T(8,128)(2,1)S(1)} %get-tuple-element.113), channel_id=1, source_target_pairs={{0,8},{8,0},{16,24},{24,16},{1,9},{9,1},{17,25},{25,17},{2,10},{10... | collective-permute-start | bytes 516104 | tf_op jit(solution)/shard_map/ppermute | solution.py:504
  62.4 1.7 %collective-permute-done.33 = bf16[112,768]{1,0:T(8,128)(2,1)S(1)} collective-permute-done((bf16[112,768]{1,0:T(8,128)(2,1)S(1)}, bf16[112,768]{1,0:T(8,128)(2,1)S(1)}, u32[]{:S(2)}, u32[]{:S(2)}) %collective-permute-start.33) | collective-permute-done | bytes 172064 | tf_op jit(solution)/shard_map/ppermute | solution.py:504
  64.2 2.9 %collective-permute-start.34 = (bf16[112,768]{1,0:T(8,128)(2,1)S(1)}, bf16[112,768]{1,0:T(8,128)(2,1)S(1)}, u32[]{:S(2)}, u32[]{:S(2)}) collective-permute-start(bf16[112,768]{1,0:T(8,128)(2,1)S(1)} %add_convert_fusion.7), channel_id=1, source_target_pairs={{0,16},{8,24},{16,0},{24,8},{1,17},{9,25},{17,1},{25,9},{2,18},{10... | collective-permute-start | bytes 516104 | tf_op jit(solution)/shard_map/ppermute | solution.py:504
  67.1 1.7 %collective-permute-start.39 = (bf16[112,768]{1,0:T(8,128)(2,1)S(1)}, bf16[112,768]{1,0:T(8,128)(2,1)S(1)}, u32[]{:S(2)}, u32[]{:S(2)}) collective-permute-start(bf16[112,768]{1,0:T(8,128)(2,1)S(1)} %add_convert_fusion.5), channel_id=1, source_target_pairs={{0,16},{8,24},{16,0},{24,8},{1,17},{9,25},{17,1},{25,9},{2,18},{10... | collective-permute-start | bytes 516104 | tf_op jit(solution)/shard_map/ppermute | solution.py:504
  68.8 7.6 %shard_map.145 = (f32[192,512]{1,0:T(8,128)S(1)}, f32[192,128]{1,0:T(8,128)S(1)}, bf16[576,640]{1,0:T(8,128)(2,1)S(1)}, f32[192,768]{1,0:T(8,128)S(1)}, bf16[192...) custom-call(bf16[384,512]{1,0:T(8,128)(2,1)S(1)} %add_convert_fusion.mine, ...), custom_call_target="tpu_custom_call" | custom-call | tf_op jit(solution)/shard_map/pallas_call | solution.py:40
  78.0 3.1 %shard_map.146 = (f32[400,1152]{1,0:T(8,128)S(1)}, bf16[400,1152]{1,0:T(8,128)(2,1)S(1)}) custom-call(bf16[576,640]{1,0:T(8,128)(2,1)S(1)} %get-tuple-element.78.proj_grad, bf16[576,768]{1,0:T(8,128)(2,1)S(1)} %bitcast.27, f32[768,2]{1,0:T(8,128)S(1)} %copy.18.gain, bf16[768,640]{1,0:T(8,128)(2,1)S(1)} %get-tuple-element.64.xall, ...), custom_call_target="tpu_custom_call" | custom-call | tf_op jit(solution)/shard_map/pallas_call | solution.py:40
  85.1 3.4 %collective-permute-done.35.other = bf16[112,768]{1,0:T(8,128)(2,1)S(1)} collective-permute-done((bf16[112,768]{1,0:T(8,128)(2,1)S(1)}, bf16[112,768]{1,0:T(8,128)(2,1)S(1)}, u32[]{:S(2)}, u32[]{:S(2)}) %collective-permute-start.35) | collective-permute-done | bytes 172064 | tf_op jit(solution)/shard_map/ppermute | solution.py:504
  90.3 4.5 %collective-permute-done.24.got = bf16[192,768]{1,0:T(8,128)(2,1)S(1)} collective-permute-done((bf16[192,768]{1,0:T(8,128)(2,1)S(1)}, bf16[192,768]{1,0:T(8,128)(2,1)S(1)}, u32[]{:S(2)}, u32[]{:S(2)}) %collective-permute-start.24) | collective-permute-done | bytes 294944 | tf_op jit(solution)/shard_map/ppermute | solution.py:504
  95.7 2.3 %collective-permute-done.20 = bf16[96,768]{1,0:T(8,128)(2,1)S(1)} collective-permute-done((bf16[96,768]{1,0:T(8,128)(2,1)S(1)}, bf16[96,768]{1,0:T(8,128)(2,1)S(1)}, u32[]{:S(2)}, u32[]{:S(2)}) %collective-permute-start.20) | collective-permute-done | bytes 147488 | tf_op jit(solution)/shard_map/ppermute | solution.py:504
  104.1 2.4 %collective-permute-done.21 = bf16[96,768]{1,0:T(8,128)(2,1)S(1)} collective-permute-done((bf16[96,768]{1,0:T(8,128)(2,1)S(1)}, bf16[96,768]{1,0:T(8,128)(2,1)S(1)}, u32[]{:S(2)}, u32[]{:S(2)}) %collective-permute-start.21) | collective-permute-done | bytes 147488 | tf_op jit(solution)/shard_map/ppermute | solution.py:504
  106.6 3.4 %collective-permute-start.22 = (bf16[96,768]{1,0:T(8,128)(2,1)S(1)}, bf16[96,768]{1,0:T(8,128)(2,1)S(1)}, u32[]{:S(2)}, u32[]{:S(2)}) collective-permute-start(bf16[96,768]{1,0:T(8,128)(2,1)S(1)} %add_convert_fusion.10.mine), channel_id=1, source_target_pairs={{0,8},{8,0},{16,24},{24,16},{1,9},{9,1},{17,25},{25,17},{2,10},{10... | collective-permute-start | bytes 442376 | tf_op jit(solution)/shard_map/ppermute | solution.py:504
  110.0 3.7 %collective-permute-done.26 = bf16[96,768]{1,0:T(8,128)(2,1)S(1)} collective-permute-done((bf16[96,768]{1,0:T(8,128)(2,1)S(1)}, bf16[96,768]{1,0:T(8,128)(2,1)S(1)}, u32[]{:S(2)}, u32[]{:S(2)}) %collective-permute-start.26) | collective-permute-done | bytes 147488 | tf_op jit(solution)/shard_map/ppermute | solution.py:504
  117.3 2.2 %collective-permute-done.29 = f32[16,192]{1,0:T(8,128)S(1)} collective-permute-done((f32[16,192]{1,0:T(8,128)S(1)}, f32[16,192]{1,0:T(8,128)S(1)}, u32[]{:S(2)}, u32[]{:S(2)}) %collective-permute-start.29) | collective-permute-done | bytes 12320 | tf_op jit(solution)/shard_map/ppermute | solution.py:504
  121.0 1.8 %shard_map.161 = (f32[576,768]{1,0:T(8,128)}, f32[288,768]{1,0:T(8,128)}) custom-call(bf16[224,768]{1,0:T(8,128)(2,1)S(1)} %shard_map.158.refs_0_, bf16[224,768]{1,0:T(8,128)(2,1)S(1)} %collective-permute-done.36.refs_1_, bf16[224,768]{1,0:T(8,128)(2,1)S(1)} %shard_map.160.refs_2_, bf16[224,768]{1,0:T(8,128)(2,1)S(1)} %collective-permute-done.41.refs_3_), custom_call_target="tpu_custom_call" | custom-call | tf_op jit(solution)/shard_map/pallas_call | solution.py:40
  127.4 2.5 %collective-permute-done.31 = f32[16,192]{1,0:T(8,128)S(1)} collective-permute-done((f32[16,192]{1,0:T(8,128)S(1)}, f32[16,192]{1,0:T(8,128)S(1)}, u32[]{:S(2)}, u32[]{:S(2)}) %collective-permute-start.31) | collective-permute-done | bytes 12320 | tf_op jit(solution)/shard_map/ppermute | solution.py:504
  (117 shorter events, 48.0 us)
Async XLA Ops:
  0.6 8.7 %collective-permute-start.1 = (bf16[192,512]{1,0:T(8,128)(2,1)}, bf16[192,512]{1,0:T(8,128)(2,1)S(1)}, u32[]{:S(2)}, u32[]{:S(2)}) collective-permute-start(bf16[192,512]{1,0:T(8,128)(2,1)} %bitcast.32), channel_id=1, source_target_pairs={{0,2},{1,3},{2,0},{3,1},{4,6},{5,7},{6,4},{7,5},{8,10},{9,11},{10,... | collective-permute-start | bytes 589832 | tf_op jit(solution)/shard_map/ppermute | solution.py:504
  3.7 10.6 %collective-permute-start = (bf16[192,512]{1,0:T(8,128)(2,1)}, bf16[192,512]{1,0:T(8,128)(2,1)S(1)}, u32[]{:S(2)}, u32[]{:S(2)}) collective-permute-start(bf16[192,512]{1,0:T(8,128)(2,1)} %bitcast.33), channel_id=1, source_target_pairs={{0,1},{1,0},{2,3},{3,2},{4,5},{5,4},{6,7},{7,6},{8,9},{9,8},{10,11... | collective-permute-start | bytes 589832 | tf_op jit(solution)/shard_map/ppermute | solution.py:504
  24.5 12.1 %collective-permute-start.8 = (bf16[384,512]{1,0:T(8,128)(2,1)S(1)}, bf16[384,512]{1,0:T(8,128)(2,1)S(1)}, u32[]{:S(2)}, u32[]{:S(2)}) collective-permute-start(bf16[384,512]{1,0:T(8,128)(2,1)S(1)} %add_convert_fusion.3), channel_id=1, source_target_pairs={{0,2},{1,3},{2,0},{3,1},{4,6},{5,7},{6,4},{7,5},{8,10},{9,11},{10,... | collective-permute-start | bytes 1179656 | tf_op jit(solution)/shard_map/ppermute | solution.py:504
  24.8 15.1 %collective-permute-start.11 = (bf16[192,512]{1,0:T(8,128)(2,1)S(1)}, bf16[192,512]{1,0:T(8,128)(2,1)S(1)}, u32[]{:S(2)}, u32[]{:S(2)}) collective-permute-start(bf16[192,512]{1,0:T(8,128)(2,1)S(1)} %bitcast.29), channel_id=1, source_target_pairs={{0,2},{1,3},{2,0},{3,1},{4,6},{5,7},{6,4},{7,5},{8,10},{9,11},{10,... | collective-permute-start | bytes 589832 | tf_op jit(solution)/shard_map/ppermute | solution.py:504
  47.1 15.1 %collective-permute-start.14 = (bf16[384,512]{1,0:T(8,128)(2,1)S(1)}, bf16[384,512]{1,0:T(8,128)(2,1)S(1)}, u32[]{:S(2)}, u32[]{:S(2)}) collective-permute-start(bf16[384,512]{1,0:T(8,128)(2,1)S(1)} %add_convert_fusion.1), channel_id=1, source_target_pairs={{0,2},{1,3},{2,0},{3,1},{4,6},{5,7},{6,4},{7,5},{8,10},{9,11},{10,... | collective-permute-start | bytes 1179656 | tf_op jit(solution)/shard_map/ppermute | solution.py:504
  48.7 9.9 %collective-permute-start.32 = (bf16[224,768]{1,0:T(8,128)(2,1)S(1)}, bf16[224,768]{1,0:T(8,128)(2,1)S(1)}, u32[]{:S(2)}, u32[]{:S(2)}) collective-permute-start(bf16[224,768]{1,0:T(8,128)(2,1)S(1)} %get-tuple-element.111), channel_id=1, source_target_pairs={{0,4},{4,0},{1,5},{5,1},{2,6},{6,2},{3,7},{7,3},{8,12},{12,8},{9,1... | collective-permute-start | bytes 1032200 | tf_op jit(solution)/shard_map/ppermute | solution.py:504
  50.5 10.0 %collective-permute-start.37 = (bf16[224,768]{1,0:T(8,128)(2,1)S(1)}, bf16[224,768]{1,0:T(8,128)(2,1)S(1)}, u32[]{:S(2)}, u32[]{:S(2)}) collective-permute-start(bf16[224,768]{1,0:T(8,128)(2,1)S(1)} %get-tuple-element.115), channel_id=1, source_target_pairs={{0,8},{8,0},{16,24},{24,16},{1,9},{9,1},{17,25},{25,17},{2,10},{10... | collective-permute-start | bytes 1032200 | tf_op jit(solution)/shard_map/ppermute | solution.py:504
  62.3 6.5 %collective-permute-start.15 = (bf16[384,512]{1,0:T(8,128)(2,1)S(1)}, bf16[384,512]{1,0:T(8,128)(2,1)S(1)}, u32[]{:S(2)}, u32[]{:S(2)}) collective-permute-start(bf16[384,512]{1,0:T(8,128)(2,1)S(1)} %add_convert_fusion.mine), channel_id=1, source_target_pairs={{0,1},{1,0},{2,3},{3,2},{4,5},{5,4},{6,7},{7,6},{8,9},{9,8},{10,11... | collective-permute-start | bytes 1179656 | tf_op jit(solution)/shard_map/ppermute | solution.py:504
  64.2 17.0 %collective-permute-start.34 = (bf16[112,768]{1,0:T(8,128)(2,1)S(1)}, bf16[112,768]{1,0:T(8,128)(2,1)S(1)}, u32[]{:S(2)}, u32[]{:S(2)}) collective-permute-start(bf16[112,768]{1,0:T(8,128)(2,1)S(1)} %add_convert_fusion.7), channel_id=1, source_target_pairs={{0,16},{8,24},{16,0},{24,8},{1,17},{9,25},{17,1},{25,9},{2,18},{10... | collective-permute-start | bytes 516104 | tf_op jit(solution)/shard_map/ppermute | solution.py:504
  67.1 16.2 %collective-permute-start.39 = (bf16[112,768]{1,0:T(8,128)(2,1)S(1)}, bf16[112,768]{1,0:T(8,128)(2,1)S(1)}, u32[]{:S(2)}, u32[]{:S(2)}) collective-permute-start(bf16[112,768]{1,0:T(8,128)(2,1)S(1)} %add_convert_fusion.5), channel_id=1, source_target_pairs={{0,16},{8,24},{16,0},{24,8},{1,17},{9,25},{17,1},{25,9},{2,18},{10... | collective-permute-start | bytes 516104 | tf_op jit(solution)/shard_map/ppermute | solution.py:504
  76.4 7.5 %collective-permute-start.19 = (bf16[192,768]{1,0:T(8,128)(2,1)S(1)}, bf16[192,768]{1,0:T(8,128)(2,1)S(1)}, u32[]{:S(2)}, u32[]{:S(2)}) collective-permute-start(bf16[192,768]{1,0:T(8,128)(2,1)S(1)} %get-tuple-element.93), channel_id=1, source_target_pairs={{0,4},{4,0},{1,5},{5,1},{2,6},{6,2},{3,7},{7,3},{8,12},{12,8},{9,1... | collective-permute-start | bytes 884744 | tf_op jit(solution)/shard_map/ppermute | solution.py:504
  81.1 21.2 %collective-permute-start.16 = (bf16[400,1152]{1,0:T(8,128)(2,1)S(1)}, bf16[400,1152]{1,0:T(8,128)(2,1)S(1)}, u32[]{:S(2)}, u32[]{:S(2)}) collective-permute-start(bf16[400,1152]{1,0:T(8,128)(2,1)S(1)} %get-tuple-element.82), channel_id=1, source_target_pairs={{0,1},{1,0},{2,3},{3,2},{4,5},{5,4},{6,7},{7,6},{8,9},{9,8},{10,11... | collective-permute-start | bytes 2764808 | tf_op jit(solution)/shard_map/ppermute | solution.py:504
  81.2 7.3 %collective-permute-start.35 = (bf16[112,768]{1,0:T(8,128)(2,1)S(1)}, bf16[112,768]{1,0:T(8,128)(2,1)S(1)}, u32[]{:S(2)}, u32[]{:S(2)}) collective-permute-start(bf16[112,768]{1,0:T(8,128)(2,1)S(1)} %add_convert_fusion.6.mine), channel_id=1, source_target_pairs={{0,8},{8,0},{16,24},{24,16},{1,9},{9,1},{17,25},{25,17},{2,10},{10... | collective-permute-start | bytes 516104 | tf_op jit(solution)/shard_map/ppermute | solution.py:504
  81.7 13.1 %collective-permute-start.24 = (bf16[192,768]{1,0:T(8,128)(2,1)S(1)}, bf16[192,768]{1,0:T(8,128)(2,1)S(1)}, u32[]{:S(2)}, u32[]{:S(2)}) collective-permute-start(bf16[192,768]{1,0:T(8,128)(2,1)S(1)} %get-tuple-element.97), channel_id=1, source_target_pairs={{0,8},{8,0},{16,24},{24,16},{1,9},{9,1},{17,25},{25,17},{2,10},{10... | collective-permute-start | bytes 884744 | tf_op jit(solution)/shard_map/ppermute | solution.py:504
  84.0 14.0 %collective-permute-start.20 = (bf16[96,768]{1,0:T(8,128)(2,1)S(1)}, bf16[96,768]{1,0:T(8,128)(2,1)S(1)}, u32[]{:S(2)}, u32[]{:S(2)}) collective-permute-start(bf16[96,768]{1,0:T(8,128)(2,1)S(1)} %get-tuple-element.95), channel_id=1, source_target_pairs={{0,8},{8,0},{16,24},{24,16},{1,9},{9,1},{17,25},{25,17},{2,10},{10... | collective-permute-start | bytes 442376 | tf_op jit(solution)/shard_map/ppermute | solution.py:504
  88.5 32.5 %collective-permute-start.36 = (bf16[224,768]{1,0:T(8,128)(2,1)S(1)}, bf16[224,768]{1,0:T(8,128)(2,1)S(1)}, u32[]{:S(2)}, u32[]{:S(2)}) collective-permute-start(bf16[224,768]{1,0:T(8,128)(2,1)S(1)} %shard_map.158.refs_0_), channel_id=1, source_target_pairs={{0,4},{4,0},{1,5},{5,1},{2,6},{6,2},{3,7},{7,3},{8,12},{12,8},{9,1... | collective-permute-start | bytes 1032200 | tf_op jit(solution)/shard_map/ppermute | solution.py:504
  89.6 31.4 %collective-permute-start.41 = (bf16[224,768]{1,0:T(8,128)(2,1)S(1)}, bf16[224,768]{1,0:T(8,128)(2,1)S(1)}, u32[]{:S(2)}, u32[]{:S(2)}) collective-permute-start(bf16[224,768]{1,0:T(8,128)(2,1)S(1)} %shard_map.160.refs_2_), channel_id=1, source_target_pairs={{0,8},{8,0},{16,24},{24,16},{1,9},{9,1},{17,25},{25,17},{2,10},{10... | collective-permute-start | bytes 1032200 | tf_op jit(solution)/shard_map/ppermute | solution.py:504
  98.0 8.5 %collective-permute-start.21 = (bf16[96,768]{1,0:T(8,128)(2,1)S(1)}, bf16[96,768]{1,0:T(8,128)(2,1)S(1)}, u32[]{:S(2)}, u32[]{:S(2)}) collective-permute-start(bf16[96,768]{1,0:T(8,128)(2,1)S(1)} %add_convert_fusion.11), channel_id=1, source_target_pairs={{0,16},{8,24},{16,0},{24,8},{1,17},{9,25},{17,1},{25,9},{2,18},{10... | collective-permute-start | bytes 442376 | tf_op jit(solution)/shard_map/ppermute | solution.py:504
  100.9 12.8 %collective-permute-start.26 = (bf16[96,768]{1,0:T(8,128)(2,1)S(1)}, bf16[96,768]{1,0:T(8,128)(2,1)S(1)}, u32[]{:S(2)}, u32[]{:S(2)}) collective-permute-start(bf16[96,768]{1,0:T(8,128)(2,1)S(1)} %add_convert_fusion.9), channel_id=1, source_target_pairs={{0,16},{8,24},{16,0},{24,8},{1,17},{9,25},{17,1},{25,9},{2,18},{10... | collective-permute-start | bytes 442376 | tf_op jit(solution)/shard_map/ppermute | solution.py:504
  102.5 11.9 %collective-permute-start.17 = (bf16[208,1152]{1,0:T(8,128)(2,1)S(1)}, bf16[208,1152]{1,0:T(8,128)(2,1)S(1)}, u32[]{:S(2)}, u32[]{:S(2)}) collective-permute-start(bf16[208,1152]{1,0:T(8,128)(2,1)S(1)} %get-tuple-element.84), channel_id=1, source_target_pairs={{0,2},{1,3},{2,0},{3,1},{4,6},{5,7},{6,4},{7,5},{8,10},{9,11},{10,... | collective-permute-start | bytes 1437704 | tf_op jit(solution)/shard_map/ppermute | solution.py:504
  106.6 16.3 %collective-permute-start.22 = (bf16[96,768]{1,0:T(8,128)(2,1)S(1)}, bf16[96,768]{1,0:T(8,128)(2,1)S(1)}, u32[]{:S(2)}, u32[]{:S(2)}) collective-permute-start(bf16[96,768]{1,0:T(8,128)(2,1)S(1)} %add_convert_fusion.10.mine), channel_id=1, source_target_pairs={{0,8},{8,0},{16,24},{24,16},{1,9},{9,1},{17,25},{25,17},{2,10},{10... | collective-permute-start | bytes 442376 | tf_op jit(solution)/shard_map/ppermute | solution.py:504
  113.7 9.8 %collective-permute-start.27 = (bf16[96,768]{1,0:T(8,128)(2,1)S(1)}, bf16[96,768]{1,0:T(8,128)(2,1)S(1)}, u32[]{:S(2)}, u32[]{:S(2)}) collective-permute-start(bf16[96,768]{1,0:T(8,128)(2,1)S(1)} %add_convert_fusion.8.mine), channel_id=1, source_target_pairs={{0,4},{4,0},{1,5},{5,1},{2,6},{6,2},{3,7},{7,3},{8,12},{12,8},{9,1... | collective-permute-start | bytes 442376 | tf_op jit(solution)/shard_map/ppermute | solution.py:504
  122.9 9.8 %collective-permute-start.23 = (bf16[192,768]{1,0:T(8,128)(2,1)S(1)}, bf16[192,768]{1,0:T(8,128)(2,1)S(1)}, u32[]{:S(2)}, u32[]{:S(2)}) collective-permute-start(bf16[192,768]{1,0:T(8,128)(2,1)S(1)} %shard_map.152.refs_0_), channel_id=1, source_target_pairs={{0,4},{4,0},{1,5},{5,1},{2,6},{6,2},{3,7},{7,3},{8,12},{12,8},{9,1... | collective-permute-start | bytes 884744 | tf_op jit(solution)/shard_map/ppermute | solution.py:504
  123.5 9.2 %collective-permute-start.28 = (bf16[192,768]{1,0:T(8,128)(2,1)S(1)}, bf16[192,768]{1,0:T(8,128)(2,1)S(1)}, u32[]{:S(2)}, u32[]{:S(2)}) collective-permute-start(bf16[192,768]{1,0:T(8,128)(2,1)S(1)} %shard_map.154.refs_2_), channel_id=1, source_target_pairs={{0,8},{8,0},{16,24},{24,16},{1,9},{9,1},{17,25},{25,17},{2,10},{10... | collective-permute-start | bytes 884744 | tf_op jit(solution)/shard_map/ppermute | solution.py:504
  (23 other events, 139.1 us)

commit v4 on v3

--- a/solution.py
+++ b/solution.py
@@ -63,13 +63,23 @@
     return jnp.sum(x.reshape(x.shape[0] // 8, 8, x.shape[1]), axis=0)
 
 
-def allowed_of(first, tile, total):
+def fill_bias(bias, first, length, total):
     shape = (2 * TILE, TILE)
     key = lax.broadcasted_iota(jnp.int32, shape, 0)
-    query = lax.broadcasted_iota(jnp.int32, shape, 1)
-    gap = key - query
-    position = key + (first + tile * TILE - HALF)
-    return (gap >= 0) & (gap <= TILE) & (position >= 0) & (position < total)
+    gap = key - lax.broadcasted_iota(jnp.int32, shape, 1)
+    near = (gap >= 0) & (gap <= TILE)
+    low = key + (first - HALF) >= 0
+    high = key + (first + length - TILE - HALF) < total
+    if length == TILE:
+        low = low & high
+    for k, allowed in enumerate((near & low, near, near & high)):
+        bias[k] = jnp.where(allowed, 0.0, -1e30)
+
+
+def bias_of(bias, tile, count):
+    if tile == 0:
+        return bias[0]
+    return bias[2] if tile == count - 1 else bias[1]
 
 
 def gather_rows(pieces, target, lanes):
@@ -95,8 +105,8 @@
 
 def attention_kernel(
     p1, p2, p3, h0, h1, h2, h3, gain, cos, sin, p0_far, w_far, wo_far,
-    xall, stats, fed, q, kw, vw, totals, mixed, keep, send,
-    proj, terms, p0, w, wo, sems,
+    xall, stats, fed, q, kw, kt, vt, totals, mixed, keep, send,
+    proj, terms, p0, w, wo, bias, sems,
 ):
     copies = [
         pltpu.make_async_copy(p0_far, p0, sems.at[0]),
@@ -112,6 +122,7 @@
     core = lax.axis_index("mp") % 2
     first = lax.axis_index("seq") * length
     total = lax.axis_size("seq") * length
+    fill_bias(bias, first, length, total)
     gather_rows((h0, h1, h2, h3), xall, slice(length, tokens))
     copies[0].wait()
     gather_rows((p0, p1, p2, p3), xall, slice(0, length))
@@ -156,21 +167,25 @@
         upper, lower = rope(row, own)
         q[pl.ds(row, half), :] = upper.astype(BF16)
         q[pl.ds(row + half, half), :] = lower.astype(BF16)
-        upper, lower = rope(columns + row, every)
-        kw[pl.ds(row, half), :] = pltpu.roll(upper, HALF, 1).astype(BF16)
-        kw[pl.ds(row + half, half), :] = pltpu.roll(lower, HALF, 1).astype(BF16)
-        value = proj[pl.ds(2 * columns + row, HEAD), :]
-        vw[pl.ds(row, HEAD), :] = pltpu.roll(value, HALF, 1).astype(BF16)
-        for j in range(length // TILE):
+        keys = jnp.concatenate(rope(columns + row, every), axis=0)
+        keys = pltpu.roll(keys, HALF, 1)
+        kw[pl.ds(row, HEAD), :] = keys.astype(BF16)
+        kt[h] = keys.T.astype(BF16)
+        value = pltpu.roll(proj[pl.ds(2 * columns + row, HEAD), :], HALF, 1)
+        vt[h] = value.T.astype(BF16)
+        value = value.astype(BF16)
+        count = length // TILE
+        for j in range(count):
             wide = slice(j * TILE, (j + 2) * TILE)
             mine = slice(j * TILE, (j + 1) * TILE)
-            scores = tn(kw[pl.ds(row, HEAD), wide], q[pl.ds(row, HEAD), mine]) * HEAD**-0.5
-            scores = jnp.where(allowed_of(first, j, total), scores, -1e30)
+            scores = nn(kt[h, wide, :], q[pl.ds(row, HEAD), mine]) * HEAD**-0.5
+            scores = scores + bias_of(bias, j, count)
             top = jnp.max(scores, axis=0, keepdims=True)
-            log_total = top + jnp.log(jnp.sum(jnp.exp(scores - top), axis=0, keepdims=True))
-            weights = jnp.exp(scores - log_total).astype(BF16)
-            totals[h, 0:1, mine] = log_total
-            mixed[pl.ds(row, HEAD), mine] = nn(vw[pl.ds(row, HEAD), wide], weights).astype(BF16)
+            raised = jnp.exp(scores - top)
+            amount = jnp.sum(raised, axis=0, keepdims=True)
+            weights = (raised * (1.0 / amount)).astype(BF16)
+            totals[h, 0:1, mine] = top + jnp.log(amount)
+            mixed[pl.ds(row, HEAD), mine] = nn(value[:, wide], weights).astype(BF16)
         return carry
 
     lax.fori_loop(0, heads, one_head, 0)
@@ -179,8 +194,13 @@
     split_half(terms, keep, send, core)
 
 
+def flip_weights_kernel(*refs):
+    for source, target in zip(refs[:3], refs[3:]):
+        target[...] = source[...].T
+
+
 def geglu_kernel(
-    xall, mine, other, u0, u1, u2, u3, gain, win, gout,
+    xall, mine, other, u0, u1, u2, u3, gain, win, win_t, gout,
     middle_own, normed, inverse_out, fed, upstream, product, lifted_grad, keep, send,
     middle, lifted, grad_product, terms,
 ):
@@ -238,7 +258,7 @@
         return carry
 
     row_loop(units, 32, unit, 0)
-    terms[...] = tn(win[...], lifted_grad[...])
+    terms[...] = nn(win_t[...], lifted_grad[...])
     split_half(terms, keep, send, core)
 
 
@@ -265,10 +285,10 @@
 
 
 def attention_back_kernel(
-    mine, other, normed, inverse, gain, upstream, wo, q, kw, vw, totals, mixed, cos, sin, fed, *rest,
+    mine, other, normed, inverse, gain, upstream, wo, q, kw, kt, vt, totals, mixed, cos, sin, fed, *rest,
     cuts,
 ):
-    outs, (full, low, mixed_grad, dk, dv, stack) = rest[:-6], rest[-6:]
+    outs, (full, low, mixed_grad, dk, dv, stack, bias) = rest[:-7], rest[-7:]
     middle_grad_own, gain_grad, proj_grad = outs[:3]
     width, length = normed.shape
     columns = q.shape[0]
@@ -281,6 +301,7 @@
     first = lax.axis_index("seq") * length
     total = lax.axis_size("seq") * length
     inv = inverse[0:1, :]
+    fill_bias(bias, first, length, total)
 
     def add(r, acc):
         a, b = acc
@@ -334,13 +355,13 @@
             keys = kw[head, wide]
             query = q[head, here]
             grad = mixed_grad[head, here]
-            scores = tn(keys, query) * HEAD**-0.5
-            scores = jnp.where(allowed_of(first, j, total), scores, -1e30)
+            scores = nn(kt[h, wide, :], query) * HEAD**-0.5
+            scores = scores + bias_of(bias, j, length // TILE)
             probs = jnp.exp(scores - totals[h, 0:1, here])
             both = grad.astype(F32) * mixed[head, here].astype(F32)
             delta = jnp.sum(both, axis=0, keepdims=True)
             dv[head, wide] += nt(grad, probs.astype(BF16))
-            grad_probs = tn(vw[head, wide], grad)
+            grad_probs = nn(vt[h, wide, :], grad)
             grad_scores = (probs * (grad_probs - delta) * HEAD**-0.5).astype(BF16)
             dk[head, wide] += nt(query, grad_scores)
             dq = nn(keys, grad_scores)
@@ -372,7 +393,7 @@
     share = (keep.shape[0] - 16) // 2
     me = lax.axis_index("mp")
     core = me % 2
-    terms[:, 0:tokens] = tn(w[...], proj_grad[...])
+    terms[:, 0:tokens] = nn(w[...], proj_grad[...])
     mean = stats[0:1, :]
     inverse = stats[1:2, :]
 
@@ -387,7 +408,7 @@
     a, b = row_loop(width, STEP, add, (zero, zero))
     one = jnp.sum(a, axis=0, keepdims=True) / width
     two = jnp.sum(b, axis=0, keepdims=True) / width
-    terms[:, tokens:] = tn(gout[...], product[...])
+    terms[:, tokens:] = nn(gout[...], product[...])
     for x in range(2):
         mine = pl.multiple_of((2 * x + core) * share, share)
         other = pl.multiple_of((2 * x + 1 - core) * share, share)
@@ -434,8 +455,9 @@
         preferred_element_type=F32,
     )
     one = exact(jnp.ones((8, length), F32), weighted[1])
-    gains[0:8, :] = one + exact(jnp.ones((8, tokens - length), F32), last)
-    gains[8:16, :] = exact(jnp.ones((8, gain_lanes.shape[1]), F32), weighted[0])
+    gains[...] = jnp.zeros(gains.shape, F32)
+    gains[0:8, 0:share] = one + exact(jnp.ones((8, tokens - length), F32), last)
+    gains[8:16, 0:share] = exact(jnp.ones((8, gain_lanes.shape[1]), F32), weighted[0])
 
 
 def input_kernel(main, low, high, middle_grad, stats, normed, gain, out):
@@ -474,11 +496,19 @@
     row_loop(rows, 16, one, 0)
 
 
-def join_kernel(mine, other, out, *, axis):
-    rows = mine.shape[0]
+def part_kernel(keep, got, rest, out):
+    rows = keep.shape[0]
+    out[0:rows, :] = (keep[...] + got[...].astype(F32)).astype(BF16)
+    out[rows:, :] = rest[...].astype(BF16)
+
+
+def join_kernel(mine, other, out, *, axis, rows):
     index = lax.axis_index(axis) % 2
-    out[pl.ds(pl.multiple_of(index * rows, 16), rows), :] = mine[...]
-    out[pl.ds(pl.multiple_of((1 - index) * rows, 16), rows), :] = other[...]
+    out[pl.ds(pl.multiple_of(index * rows, 16), rows), :] = mine[0:rows, :]
+    out[pl.ds(pl.multiple_of((1 - index) * rows, 16), rows), :] = other[0:rows, :]
+    if mine.shape[0] > rows:
+        rest = mine[rows:, :].astype(F32) + other[rows:, :].astype(F32)
+        out[2 * rows :, :] = rest.astype(BF16)
 
 
 def place_kernel(*refs, cuts, outs):
@@ -490,7 +520,7 @@
         index = lax.axis_index(order[0]) % 2
         for k, at in enumerate((index, 1 - index)):
             at = pl.multiple_of(start + at * size, 16)
-            stack[pl.ds(at, size), :] = pieces[2 * i + k][...].astype(F32)
+            stack[pl.ds(at, size), :] = pieces[2 * i + k][0:size, :].astype(F32)
         start += rows
     for target, spans in zip(targets, outs):
         at = 0
@@ -506,7 +536,8 @@
 
 def gather_mp(shard):
     across = flip(shard, "mp", 2)
-    return shard, flip(shard, "mp", 1), across, flip(across, "mp", 1)
+    beside = flip(shard, "mp", 1)
+    return shard, beside, across, flip(across, "mp", 1)
 
 
 def held(x, other):
@@ -514,7 +545,8 @@
 
 
 def sum_halves(keep, send):
-    half = (keep + flip(send, "mp", 1).astype(F32)).astype(BF16)
+    got = flip(send, "mp", 1)
+    half = (keep + got.astype(F32)).astype(BF16)
     across = flip(half, "mp", 2)
     total = (half.astype(F32) + across.astype(F32)).astype(BF16)
     return total, flip(total, "mp", 1), half
@@ -544,15 +576,7 @@
     return lax.axis_size("seq") == 2 and lax.axis_size("dp") == 4
 
 
-def sum_blocks(x):
-    if not staged():
-        return lax.psum(x, ("dp", "seq"))
-    for axis, bit in (("seq", 1), ("dp", 1), ("dp", 2)):
-        x = x + flip(x, axis, bit)
-    return x
-
-
-def reduce_unit(keep, send, order):
+def reduce_unit(keep, send, order, rest=None):
     one, two = order
     rows, width = keep.shape
     got = flip(send, one, 1)
@@ -564,13 +588,17 @@
         got,
     )
     got = flip(send, two, 1)
-    part = (keep + got.astype(F32)).astype(BF16)
+    if rest is None:
+        part = (keep + got.astype(F32)).astype(BF16)
+    else:
+        shape = (keep.shape[0] + rest.shape[0], width)
+        (part,) = call(part_kernel, [(shape, BF16)], [], keep, got, rest)
     got = flip(part, "dp", 2)
     total = (part.astype(F32) + got.astype(F32)).astype(BF16)
     beside = flip(total, two, 1)
     (half,) = call(
-        functools.partial(join_kernel, axis=two),
-        [((rows, width), BF16)],
+        functools.partial(join_kernel, axis=two, rows=rows // 2),
+        [((rows + (0 if rest is None else rest.shape[0]), width), BF16)],
         [],
         total,
         beside,
@@ -578,13 +606,16 @@
     return half, flip(half, one, 1)
 
 
-def reduce_stack(parts, cuts):
+def reduce_stack(parts, cuts, rest=None):
     if cuts is None:
-        return [lax.psum(parts[0], ("dp", "seq"))]
+        return [lax.psum(parts[0], ("dp", "seq"))], rest if rest is None else lax.psum(rest, ("dp", "seq"))
     pieces = []
     for i, (_, order) in enumerate(cuts):
-        pieces.extend(reduce_unit(parts[2 * i], parts[2 * i + 1], order))
-    return pieces
+        more = rest if i == len(cuts) - 1 else None
+        pieces.extend(reduce_unit(parts[2 * i], parts[2 * i + 1], order, more))
+    if rest is not None:
+        rest = sum(p[-rest.shape[0] :].astype(F32) for p in pieces[-2:])
+    return pieces, rest
 
 
 def place_stack(pieces, cuts, spans, width):
@@ -630,8 +661,8 @@
     win = jnp.transpose(geglu_in, (1, 2, 0)).reshape(2 * units, width)
     gains = jnp.stack([attention_gain, feedforward_gain], axis=1)
 
+    after, before = to_neighbours(x_own[:, :HALF], x_own[:, length - HALF :])
     x_parts = gather_mp(x_own)
-    after, before = to_neighbours(x_own[:, :HALF], x_own[:, length - HALF :])
     halo = jnp.concatenate([after, before], axis=1)
     h_parts = gather_mp(halo)
     u_parts = gather_mp(u_own)
@@ -643,7 +674,7 @@
     angles = rates[:, None] * spot.astype(F32)[None, :]
     cos, sin = jnp.cos(angles), jnp.sin(angles)
 
-    xall, stats, fed, q, kw, vw, totals, mixed, keep, send = call(
+    xall, stats, fed, q, kw, kt, vt, totals, mixed, keep, send = call(
         attention_kernel,
         [
             ((width, tokens), BF16),
@@ -651,7 +682,8 @@
             ((width, tokens), BF16),
             ((columns, length), BF16),
             ((columns, tokens), BF16),
-            ((columns, tokens), BF16),
+            ((heads, tokens, HEAD), BF16),
+            ((heads, tokens, HEAD), BF16),
             ((heads, 8, length), F32),
             ((columns, length), BF16),
             ((half, length), F32),
@@ -663,11 +695,18 @@
             ((share, length), BF16),
             ((3 * columns, width), BF16),
             ((columns, width), BF16),
+            ((3, 2 * TILE, TILE), F32),
         ],
         *x_parts[1:], *h_parts, gains, cos, sin, x_own, w, attention_out,
         loads=3,
     )
-    mine, other, _ = sum_halves(keep, send)
+    mine, other, half_one = sum_halves(keep, send)
+    win_t, w_t, gout_t = call(
+        flip_weights_kernel,
+        [((width, 2 * units), BF16), ((width, 3 * columns), BF16), ((width, units), BF16)],
+        [],
+        held(win, half_one), w, geglu_out,
+    )
     middle_own, normed, inverse, fed_two, upstream, product, lifted_grad, keep, send = call(
         geglu_kernel,
         [
@@ -687,7 +726,7 @@
             ((units, length), F32),
             ((width, length), F32),
         ],
-        xall, mine, other, *u_parts, gains, win, geglu_out,
+        xall, mine, other, *u_parts, gains, win, win_t, geglu_out,
     )
     mine, other, half_sent = sum_halves(keep, send)
 
@@ -706,7 +745,7 @@
 
     back_cuts = None
     if staged() and 4 * columns % grain == 0:
-        back_cuts = tuple((2 * columns, order) for order in orders)
+        back_cuts = ((2 * columns, orders[0]),) * 2
     outs = call(
         functools.partial(attention_back_kernel, cuts=back_cuts),
         [((share, length), F32), ((share, 128), F32), ((3 * columns, tokens), BF16)]
@@ -718,23 +757,24 @@
             ((columns, tokens), F32),
             ((columns, tokens), F32),
             ((4 * columns, width), F32),
+            ((3, 2 * TILE, TILE), F32),
         ],
         mine, other, normed, inverse, gains, upstream, attention_out,
-        q, kw, vw, totals, mixed, cos, sin, fed,
+        q, kw, kt, vt, totals, mixed, cos, sin, fed,
     )
     middle_grad, gain_two_lanes, proj_grad = outs[:3]
-    pieces = reduce_stack(geglu_parts, geglu_cuts)
+    pieces, _ = reduce_stack(geglu_parts, geglu_cuts)
     grad_in, grad_out = place_stack(
         pieces, geglu_cuts, (((0, 2 * units),), ((2 * units, units),)), width
     )
-    back_pieces = reduce_stack(outs[3:], back_cuts)
+    back_parts = outs[3:]
 
     lanes = tokens + length
     keep, send = call(
         terms_kernel,
         [((2 * share + 16, lanes), F32), ((2 * share + 16, lanes), BF16)],
         [((width, lanes), F32)],
-        proj_grad, w, gains, xall, stats, geglu_out, product,
+        proj_grad, w_t, gains, xall, stats, gout_t, product,
     )
     own, got = scatter_shards(keep, send)
     layer_out, main, edges, gain_sums = call(
@@ -743,13 +783,13 @@
             ((share, length), F32),
             ((share + 16, length), F32),
             ((share + 16, TILE), F32),
-            ((16, share), F32),
+            ((16, width), F32),
         ],
         [],
         own, got, middle_own, normed_own, gain_two_lanes,
     )
     high_add, low_add = to_neighbours(edges[:, HALF:], edges[:, :HALF])
-    gain_sums = sum_blocks(gain_sums)
+    back_pieces, gain_sums = reduce_stack(back_parts, back_cuts, gain_sums)
     (grad_input,) = call(
         input_kernel,
         [((share, length), F32)],
@@ -757,7 +797,7 @@
         main, low_add, high_add, middle_grad, stats, normed_own, gains,
     )
     grad_qkv, grad_attention_out = place_stack(
-        held(back_pieces, (gain_sums, grad_input, layer_out)),
+        held(back_pieces, (grad_input, layer_out)),
         back_cuts,
         (((2 * columns, 2 * columns), (0, columns)), ((columns, columns),)),
         width,
@@ -769,8 +809,8 @@
         grad_attention_out,
         jnp.transpose(grad_in.reshape(2, units, width), (2, 0, 1)),
         grad_out,
-        gain_sums[0],
-        gain_sums[8],
+        gain_sums[0, :share],
+        gain_sums[8, :share],
     )
 
 

time: 135 us -> 161 us (1.19)
  waiting for transfers between devices: 55 us -> 87.3 us
  starting transfers between devices: 43.4 us -> 36.7 us
    ppermute x42 -> x39, waiting for transfers between devices: 55 us -> 87.3 us  [flip(): return lax.ppermute(x, axis, [(i, i ^ bit) for i in range(count)])]
    ppermute x42 -> x39, starting transfers between devices: 43.4 us -> 36.7 us  [flip(): return lax.ppermute(x, axis, [(i, i ^ bit) for i in range(count)])]
    pallas_call x19 -> x21, Pallas kernels: 30.8 us -> 31 us  [call(): return run(*args)]
  transfers between devices with their start and end apart: 42 -> 39, of which waited for: 20 -> 19; matrix products, arithmetic and copies ran while one was open for 3% -> 2% of each run, Pallas kernels for 13% -> 5%
where the time goes in v4:
time: 161 us; the launch traced here: 160 us
  waiting for transfers between devices  87.3 us (54%)
  starting transfers between devices  36.7 us (23%)
  Pallas kernels  31 us (19%)
  other arithmetic  2.24 us (1%)
  local copies, waits for them, and re-layouts  2.16 us (1%)
    ppermute x39, waiting for transfers between devices, flip(): return lax.ppermute(x, axis, [(i, i ^ bit) for i in range(count)])  87.3 us
    ppermute x39, starting transfers between devices, flip(): return lax.ppermute(x, axis, [(i, i ^ bit) for i in range(count)])  36.7 us
    pallas_call x21, Pallas kernels, call(): return run(*args)  31 us
  transfers between devices with their start and end apart: 39, of which 19 were waited for; matrix products, arithmetic and copies ran while one was open for 2% of the time, Pallas kernels for 5%

profile of v4, /device:TPU:0, one launch (start us, length us, event | category | flops | bytes accessed | tf_op | source)
XLA Modules:
  0.0 160.3 jit_solution(4951719544768420562)
XLA Ops:
  0.6 3.0 %collective-permute-start.1 = (bf16[192,512]{1,0:T(8,128)(2,1)}, bf16[192,512]{1,0:T(8,128)(2,1)S(1)}, u32[]{:S(2)}, u32[]{:S(2)}) collective-permute-start(bf16[192,512]{1,0:T(8,128)(2,1)} %bitcast.33), channel_id=1, source_target_pairs={{0,2},{1,3},{2,0},{3,1},{4,6},{5,7},{6,4},{7,5},{8,10},{9,11},{10,... | collective-permute-start | bytes 589832 | tf_op jit(solution)/shard_map/ppermute | solution.py:534
  6.2 2.6 %collective-permute-done.3 = bf16[192,64]{1,0:T(8,128)(2,1)S(1)} collective-permute-done((bf16[192,64]{1,0:T(8,128)(2,1)S(1)}, bf16[192,64]{1,0:T(8,128)(2,1)S(1)}, u32[]{:S(2)}, u32[]{:S(2)}) %collective-permute-start.3) | collective-permute-done | bytes 24608 | tf_op jit(solution)/shard_map/ppermute | solution.py:534
  14.3 8.1 %shard_map.143 = (bf16[768,640]{1,0:T(8,128)(2,1)S(1)}, f32[8,640]{1,0:T(8,128)S(1)}, bf16[768,640]{1,0:T(8,128)(2,1)S(1)}, bf16[192,512]{1,0:T(8,128)(2,1)S(1)}...) custom-call(bf16[192,512]{1,0:T(8,128)(2,1)S(1)} %collective-permute, ...), custom_call_target="tpu_custom_call" | custom-call | tf_op jit(solution)/shard_map/pallas_call | solution.py:40
  24.7 1.7 %collective-permute-start.11 = (bf16[192,512]{1,0:T(8,128)(2,1)S(1)}, bf16[192,512]{1,0:T(8,128)(2,1)S(1)}, u32[]{:S(2)}, u32[]{:S(2)}) collective-permute-start(bf16[192,512]{1,0:T(8,128)(2,1)S(1)} %bitcast.30), channel_id=1, source_target_pairs={{0,2},{1,3},{2,0},{3,1},{4,6},{5,7},{6,4},{7,5},{8,10},{9,11},{10,... | collective-permute-start | bytes 589832 | tf_op jit(solution)/shard_map/ppermute | solution.py:534
  26.4 10.0 %collective-permute-done.8 = bf16[384,512]{1,0:T(8,128)(2,1)S(1)} collective-permute-done((bf16[384,512]{1,0:T(8,128)(2,1)S(1)}, bf16[384,512]{1,0:T(8,128)(2,1)S(1)}, u32[]{:S(2)}, u32[]{:S(2)}) %collective-permute-start.8) | collective-permute-done | bytes 393248 | tf_op jit(solution)/shard_map/ppermute | solution.py:534
  37.1 2.7 %collective-permute-done.11.u2 = bf16[192,512]{1,0:T(8,128)(2,1)S(1)} collective-permute-done((bf16[192,512]{1,0:T(8,128)(2,1)S(1)}, bf16[192,512]{1,0:T(8,128)(2,1)S(1)}, u32[]{:S(2)}, u32[]{:S(2)}) %collective-permute-start.11) | collective-permute-done | bytes 196640 | tf_op jit(solution)/shard_map/ppermute | solution.py:534
  41.2 3.8 %shard_map.145 = (f32[192,512]{1,0:T(8,128)S(1)}, f32[768,512]{1,0:T(8,128)S(1)}, f32[8,512]{1,0:T(8,128)S(1)}, bf16[768,512]{1,0:T(8,128)(2,1)S(1)}, bf16[768,5...) custom-call(bf16[768,640]{1,0:T(8,128)(2,1)S(1)} %get-tuple-element., ...), custom_call_target="tpu_custom_call" | custom-call | tf_op jit(solution)/shard_map/pallas_call | solution.py:40
  47.3 10.8 %collective-permute-done.14 = bf16[384,512]{1,0:T(8,128)(2,1)S(1)} collective-permute-done((bf16[384,512]{1,0:T(8,128)(2,1)S(1)}, bf16[384,512]{1,0:T(8,128)(2,1)S(1)}, u32[]{:S(2)}, u32[]{:S(2)}) %collective-permute-start.14) | collective-permute-done | bytes 393248 | tf_op jit(solution)/shard_map/ppermute | solution.py:534
  58.4 1.7 %collective-permute-done.15.other = bf16[384,512]{1,0:T(8,128)(2,1)S(1)} collective-permute-done((bf16[384,512]{1,0:T(8,128)(2,1)S(1)}, bf16[384,512]{1,0:T(8,128)(2,1)S(1)}, u32[]{:S(2)}, u32[]{:S(2)}) %collective-permute-start.15) | collective-permute-done | bytes 393248 | tf_op jit(solution)/shard_map/ppermute | solution.py:534
  60.1 7.2 %shard_map.146 = (f32[192,512]{1,0:T(8,128)S(1)}, f32[192,128]{1,0:T(8,128)S(1)}, bf16[576,640]{1,0:T(8,128)(2,1)S(1)}, f32[192,768]{1,0:T(8,128)S(1)}, bf16[192...) custom-call(bf16[384,512]{1,0:T(8,128)(2,1)S(1)} %add_convert_fusion.mine, ...), custom_call_target="tpu_custom_call" | custom-call | tf_op jit(solution)/shard_map/pallas_call | solution.py:40
  67.3 3.0 %shard_map.147 = (f32[400,1152]{1,0:T(8,128)S(1)}, bf16[400,1152]{1,0:T(8,128)(2,1)S(1)}) custom-call(bf16[576,640]{1,0:T(8,128)(2,1)S(1)} %get-tuple-element.86.proj_grad, bf16[768,576]{1,0:T(8,128)(2,1)S(1)} %get-tuple-element.87.w, f32[768,2]{1,0:T(8,128)S(1)} %copy.18.gain, bf16[768,640]{1,0:T(8,128)(2,1)S(1)} %get-tuple-element.69.xall, ...), custom_call_target="tpu_custom_call" | custom-call | tf_op jit(solution)/shard_map/pallas_call | solution.py:40
  74.9 7.2 %collective-permute-done.29.got = bf16[224,768]{1,0:T(8,128)(2,1)S(1)} collective-permute-done((bf16[224,768]{1,0:T(8,128)(2,1)S(1)}, bf16[224,768]{1,0:T(8,128)(2,1)S(1)}, u32[]{:S(2)}, u32[]{:S(2)}) %collective-permute-start.29) | collective-permute-done | bytes 344096 | tf_op jit(solution)/shard_map/ppermute | solution.py:534
  82.2 1.6 %collective-permute-start.30 = (bf16[112,768]{1,0:T(8,128)(2,1)S(1)}, bf16[112,768]{1,0:T(8,128)(2,1)S(1)}, u32[]{:S(2)}, u32[]{:S(2)}) collective-permute-start(bf16[112,768]{1,0:T(8,128)(2,1)S(1)} %get-tuple-element.123), channel_id=1, source_target_pairs={{0,8},{8,0},{16,24},{24,16},{1,9},{9,1},{17,25},{25,17},{2,10},{10... | collective-permute-start | bytes 516104 | tf_op jit(solution)/shard_map/ppermute | solution.py:534
  85.6 2.4 %collective-permute-done.30 = bf16[112,768]{1,0:T(8,128)(2,1)S(1)} collective-permute-done((bf16[112,768]{1,0:T(8,128)(2,1)S(1)}, bf16[112,768]{1,0:T(8,128)(2,1)S(1)}, u32[]{:S(2)}, u32[]{:S(2)}) %collective-permute-start.30) | collective-permute-done | bytes 172064 | tf_op jit(solution)/shard_map/ppermute | solution.py:534
  88.1 2.7 %collective-permute-start.31 = (bf16[112,768]{1,0:T(8,128)(2,1)S(1)}, bf16[112,768]{1,0:T(8,128)(2,1)S(1)}, u32[]{:S(2)}, u32[]{:S(2)}) collective-permute-start(bf16[112,768]{1,0:T(8,128)(2,1)S(1)} %add_convert_fusion.7), channel_id=1, source_target_pairs={{0,16},{8,24},{16,0},{24,8},{1,17},{9,25},{17,1},{25,9},{2,18},{10... | collective-permute-start | bytes 516104 | tf_op jit(solution)/shard_map/ppermute | solution.py:534
  93.9 8.5 %collective-permute-done.31 = bf16[112,768]{1,0:T(8,128)(2,1)S(1)} collective-permute-done((bf16[112,768]{1,0:T(8,128)(2,1)S(1)}, bf16[112,768]{1,0:T(8,128)(2,1)S(1)}, u32[]{:S(2)}, u32[]{:S(2)}) %collective-permute-start.31) | collective-permute-done | bytes 172064 | tf_op jit(solution)/shard_map/ppermute | solution.py:534
  102.7 2.0 %collective-permute-start.20 = (bf16[96,768]{1,0:T(8,128)(2,1)S(1)}, bf16[96,768]{1,0:T(8,128)(2,1)S(1)}, u32[]{:S(2)}, u32[]{:S(2)}) collective-permute-start(bf16[96,768]{1,0:T(8,128)(2,1)S(1)} %get-tuple-element.105), channel_id=1, source_target_pairs={{0,8},{8,0},{16,24},{24,16},{1,9},{9,1},{17,25},{25,17},{2,10},{10... | collective-permute-start | bytes 442376 | tf_op jit(solution)/shard_map/ppermute | solution.py:534
  109.3 5.7 %collective-permute-done.25.got = bf16[96,768]{1,0:T(8,128)(2,1)S(1)} collective-permute-done((bf16[96,768]{1,0:T(8,128)(2,1)S(1)}, bf16[96,768]{1,0:T(8,128)(2,1)S(1)}, u32[]{:S(2)}, u32[]{:S(2)}) %collective-permute-start.25) | collective-permute-done | bytes 147488 | tf_op jit(solution)/shard_map/ppermute | solution.py:534
  115.1 1.6 %collective-permute-start.26 = (bf16[112,768]{1,0:T(8,128)(2,1)S(1)}, bf16[112,768]{1,0:T(8,128)(2,1)S(1)}, u32[]{:S(2)}, u32[]{:S(2)}) collective-permute-start(bf16[112,768]{1,0:T(8,128)(2,1)S(1)} %shard_map.155), channel_id=1, source_target_pairs={{0,16},{8,24},{16,0},{24,8},{1,17},{9,25},{17,1},{25,9},{2,18},{10... | collective-permute-start | bytes 516104 | tf_op jit(solution)/shard_map/ppermute | solution.py:534
  118.2 11.6 %collective-permute-done.26 = bf16[112,768]{1,0:T(8,128)(2,1)S(1)} collective-permute-done((bf16[112,768]{1,0:T(8,128)(2,1)S(1)}, bf16[112,768]{1,0:T(8,128)(2,1)S(1)}, u32[]{:S(2)}, u32[]{:S(2)}) %collective-permute-start.26) | collective-permute-done | bytes 172064 | tf_op jit(solution)/shard_map/ppermute | solution.py:534
  135.3 5.0 %collective-permute-done.22.other = bf16[96,768]{1,0:T(8,128)(2,1)S(1)} collective-permute-done((bf16[96,768]{1,0:T(8,128)(2,1)S(1)}, bf16[96,768]{1,0:T(8,128)(2,1)S(1)}, u32[]{:S(2)}, u32[]{:S(2)}) %collective-permute-start.22) | collective-permute-done | bytes 147488 | tf_op jit(solution)/shard_map/ppermute | solution.py:534
  145.5 1.8 %shard_map.163 = (f32[576,768]{1,0:T(8,128)}, f32[288,768]{1,0:T(8,128)}) custom-call(bf16[224,768]{1,0:T(8,128)(2,1)S(1)} %shard_map.160.refs_0_, bf16[224,768]{1,0:T(8,128)(2,1)S(1)} %collective-permute-done.33.refs_1_, bf16[224,768]{1,0:T(8,128)(2,1)S(1)} %shard_map.162.refs_2_, bf16[224,768]{1,0:T(8,128)(2,1)S(1)} %collective-permute-done.38.refs_3_), custom_call_target="tpu_custom_call" | custom-call | tf_op jit(solution)/shard_map/pallas_call | solution.py:40
  147.4 9.7 %collective-permute-done.18 = f32[208,64]{1,0:T(8,128)S(1)} collective-permute-done((f32[208,64]{1,0:T(8,128)S(1)}, f32[208,64]{1,0:T(8,128)S(1)}, u32[]{:S(2)}, u32[]{:S(2)}) %collective-permute-start.18) | collective-permute-done | bytes 53280 | tf_op jit(solution)/shard_map/ppermute | solution.py:534
  158.6 1.7 %shard_map.157 = (f32[576,768]{1,0:T(8,128)}, f32[192,768]{1,0:T(8,128)}) custom-call(bf16[192,768]{1,0:T(8,128)(2,1)S(1)} %shard_map.153.refs_0_, bf16[192,768]{1,0:T(8,128)(2,1)S(1)} %collective-permute-done.23.refs_1_, bf16[208,768]{1,0:T(8,128)(2,1)S(1)} %shard_map.156.refs_2_, bf16[208,768]{1,0:T(8,128)(2,1)S(1)} %collective-permute-done.28.refs_3_), custom_call_target="tpu_custom_call" | custom-call | tf_op jit(solution)/shard_map/pallas_call | solution.py:40
  (110 shorter events, 43.0 us)
Async XLA Ops:
  3.7 10.6 %collective-permute-start = (bf16[192,512]{1,0:T(8,128)(2,1)}, bf16[192,512]{1,0:T(8,128)(2,1)S(1)}, u32[]{:S(2)}, u32[]{:S(2)}) collective-permute-start(bf16[192,512]{1,0:T(8,128)(2,1)} %bitcast.34), channel_id=1, source_target_pairs={{0,1},{1,0},{2,3},{3,2},{4,5},{5,4},{6,7},{7,6},{8,9},{9,8},{10,11... | collective-permute-start | bytes 589832 | tf_op jit(solution)/shard_map/ppermute | solution.py:534
  24.3 12.1 %collective-permute-start.8 = (bf16[384,512]{1,0:T(8,128)(2,1)S(1)}, bf16[384,512]{1,0:T(8,128)(2,1)S(1)}, u32[]{:S(2)}, u32[]{:S(2)}) collective-permute-start(bf16[384,512]{1,0:T(8,128)(2,1)S(1)} %add_convert_fusion.3), channel_id=1, source_target_pairs={{0,2},{1,3},{2,0},{3,1},{4,6},{5,7},{6,4},{7,5},{8,10},{9,11},{10,... | collective-permute-start | bytes 1179656 | tf_op jit(solution)/shard_map/ppermute | solution.py:534
  24.7 15.1 %collective-permute-start.11 = (bf16[192,512]{1,0:T(8,128)(2,1)S(1)}, bf16[192,512]{1,0:T(8,128)(2,1)S(1)}, u32[]{:S(2)}, u32[]{:S(2)}) collective-permute-start(bf16[192,512]{1,0:T(8,128)(2,1)S(1)} %bitcast.30), channel_id=1, source_target_pairs={{0,2},{1,3},{2,0},{3,1},{4,6},{5,7},{6,4},{7,5},{8,10},{9,11},{10,... | collective-permute-start | bytes 589832 | tf_op jit(solution)/shard_map/ppermute | solution.py:534
  46.9 11.2 %collective-permute-start.14 = (bf16[384,512]{1,0:T(8,128)(2,1)S(1)}, bf16[384,512]{1,0:T(8,128)(2,1)S(1)}, u32[]{:S(2)}, u32[]{:S(2)}) collective-permute-start(bf16[384,512]{1,0:T(8,128)(2,1)S(1)} %add_convert_fusion.1), channel_id=1, source_target_pairs={{0,2},{1,3},{2,0},{3,1},{4,6},{5,7},{6,4},{7,5},{8,10},{9,11},{10,... | collective-permute-start | bytes 1179656 | tf_op jit(solution)/shard_map/ppermute | solution.py:534
  70.3 22.5 %collective-permute-start.16 = (bf16[400,1152]{1,0:T(8,128)(2,1)S(1)}, bf16[400,1152]{1,0:T(8,128)(2,1)S(1)}, u32[]{:S(2)}, u32[]{:S(2)}) collective-permute-start(bf16[400,1152]{1,0:T(8,128)(2,1)S(1)} %get-tuple-element.92), channel_id=1, source_target_pairs={{0,1},{1,0},{2,3},{3,2},{4,5},{5,4},{6,7},{7,6},{8,9},{9,8},{10,11... | collective-permute-start | bytes 2764808 | tf_op jit(solution)/shard_map/ppermute | solution.py:534
  71.7 10.4 %collective-permute-start.29 = (bf16[224,768]{1,0:T(8,128)(2,1)S(1)}, bf16[224,768]{1,0:T(8,128)(2,1)S(1)}, u32[]{:S(2)}, u32[]{:S(2)}) collective-permute-start(bf16[224,768]{1,0:T(8,128)(2,1)S(1)} %get-tuple-element.121), channel_id=1, source_target_pairs={{0,4},{4,0},{1,5},{5,1},{2,6},{6,2},{3,7},{7,3},{8,12},{12,8},{9,1... | collective-permute-start | bytes 1032200 | tf_op jit(solution)/shard_map/ppermute | solution.py:534
  73.3 10.6 %collective-permute-start.34 = (bf16[224,768]{1,0:T(8,128)(2,1)S(1)}, bf16[224,768]{1,0:T(8,128)(2,1)S(1)}, u32[]{:S(2)}, u32[]{:S(2)}) collective-permute-start(bf16[224,768]{1,0:T(8,128)(2,1)S(1)} %get-tuple-element.125), channel_id=1, source_target_pairs={{0,8},{8,0},{16,24},{24,16},{1,9},{9,1},{17,25},{25,17},{2,10},{10... | collective-permute-start | bytes 1032200 | tf_op jit(solution)/shard_map/ppermute | solution.py:534
  88.1 14.4 %collective-permute-start.31 = (bf16[112,768]{1,0:T(8,128)(2,1)S(1)}, bf16[112,768]{1,0:T(8,128)(2,1)S(1)}, u32[]{:S(2)}, u32[]{:S(2)}) collective-permute-start(bf16[112,768]{1,0:T(8,128)(2,1)S(1)} %add_convert_fusion.7), channel_id=1, source_target_pairs={{0,16},{8,24},{16,0},{24,8},{1,17},{9,25},{17,1},{25,9},{2,18},{10... | collective-permute-start | bytes 516104 | tf_op jit(solution)/shard_map/ppermute | solution.py:534
  90.7 11.8 %collective-permute-start.19 = (bf16[192,768]{1,0:T(8,128)(2,1)S(1)}, bf16[192,768]{1,0:T(8,128)(2,1)S(1)}, u32[]{:S(2)}, u32[]{:S(2)}) collective-permute-start(bf16[192,768]{1,0:T(8,128)(2,1)S(1)} %get-tuple-element.103), channel_id=1, source_target_pairs={{0,4},{4,0},{1,5},{5,1},{2,6},{6,2},{3,7},{7,3},{8,12},{12,8},{9,1... | collective-permute-start | bytes 884744 | tf_op jit(solution)/shard_map/ppermute | solution.py:534
  92.3 12.5 %collective-permute-start.24 = (bf16[192,768]{1,0:T(8,128)(2,1)S(1)}, bf16[192,768]{1,0:T(8,128)(2,1)S(1)}, u32[]{:S(2)}, u32[]{:S(2)}) collective-permute-start(bf16[192,768]{1,0:T(8,128)(2,1)S(1)} %get-tuple-element.107), channel_id=1, source_target_pairs={{0,4},{4,0},{1,5},{5,1},{2,6},{6,2},{3,7},{7,3},{8,12},{12,8},{9,1... | collective-permute-start | bytes 884744 | tf_op jit(solution)/shard_map/ppermute | solution.py:534
  93.0 14.9 %collective-permute-start.17 = (bf16[208,1152]{1,0:T(8,128)(2,1)S(1)}, bf16[208,1152]{1,0:T(8,128)(2,1)S(1)}, u32[]{:S(2)}, u32[]{:S(2)}) collective-permute-start(bf16[208,1152]{1,0:T(8,128)(2,1)S(1)} %get-tuple-element.94), channel_id=1, source_target_pairs={{0,2},{1,3},{2,0},{3,1},{4,6},{5,7},{6,4},{7,5},{8,10},{9,11},{10,... | collective-permute-start | bytes 1437704 | tf_op jit(solution)/shard_map/ppermute | solution.py:534
  93.7 12.6 %collective-permute-start.36 = (bf16[112,768]{1,0:T(8,128)(2,1)S(1)}, bf16[112,768]{1,0:T(8,128)(2,1)S(1)}, u32[]{:S(2)}, u32[]{:S(2)}) collective-permute-start(bf16[112,768]{1,0:T(8,128)(2,1)S(1)} %add_convert_fusion.5), channel_id=1, source_target_pairs={{0,16},{8,24},{16,0},{24,8},{1,17},{9,25},{17,1},{25,9},{2,18},{10... | collective-permute-start | bytes 516104 | tf_op jit(solution)/shard_map/ppermute | solution.py:534
  102.5 29.5 %collective-permute-start.32 = (bf16[112,768]{1,0:T(8,128)(2,1)S(1)}, bf16[112,768]{1,0:T(8,128)(2,1)S(1)}, u32[]{:S(2)}, u32[]{:S(2)}) collective-permute-start(bf16[112,768]{1,0:T(8,128)(2,1)S(1)} %add_convert_fusion.6.mine), channel_id=1, source_target_pairs={{0,8},{8,0},{16,24},{24,16},{1,9},{9,1},{17,25},{25,17},{2,10},{10... | collective-permute-start | bytes 516104 | tf_op jit(solution)/shard_map/ppermute | solution.py:534
  102.7 14.0 %collective-permute-start.20 = (bf16[96,768]{1,0:T(8,128)(2,1)S(1)}, bf16[96,768]{1,0:T(8,128)(2,1)S(1)}, u32[]{:S(2)}, u32[]{:S(2)}) collective-permute-start(bf16[96,768]{1,0:T(8,128)(2,1)S(1)} %get-tuple-element.105), channel_id=1, source_target_pairs={{0,8},{8,0},{16,24},{24,16},{1,9},{9,1},{17,25},{25,17},{2,10},{10... | collective-permute-start | bytes 442376 | tf_op jit(solution)/shard_map/ppermute | solution.py:534
  105.0 10.0 %collective-permute-start.25 = (bf16[96,768]{1,0:T(8,128)(2,1)S(1)}, bf16[96,768]{1,0:T(8,128)(2,1)S(1)}, u32[]{:S(2)}, u32[]{:S(2)}) collective-permute-start(bf16[96,768]{1,0:T(8,128)(2,1)S(1)} %get-tuple-element.109), channel_id=1, source_target_pairs={{0,8},{8,0},{16,24},{24,16},{1,9},{9,1},{17,25},{25,17},{2,10},{10... | collective-permute-start | bytes 442376 | tf_op jit(solution)/shard_map/ppermute | solution.py:534
  106.3 27.3 %collective-permute-start.37 = (bf16[112,768]{1,0:T(8,128)(2,1)S(1)}, bf16[112,768]{1,0:T(8,128)(2,1)S(1)}, u32[]{:S(2)}, u32[]{:S(2)}) collective-permute-start(bf16[112,768]{1,0:T(8,128)(2,1)S(1)} %add_convert_fusion.4.mine), channel_id=1, source_target_pairs={{0,4},{4,0},{1,5},{5,1},{2,6},{6,2},{3,7},{7,3},{8,12},{12,8},{9,1... | collective-permute-start | bytes 516104 | tf_op jit(solution)/shard_map/ppermute | solution.py:534
  115.1 14.7 %collective-permute-start.26 = (bf16[112,768]{1,0:T(8,128)(2,1)S(1)}, bf16[112,768]{1,0:T(8,128)(2,1)S(1)}, u32[]{:S(2)}, u32[]{:S(2)}) collective-permute-start(bf16[112,768]{1,0:T(8,128)(2,1)S(1)} %shard_map.155), channel_id=1, source_target_pairs={{0,16},{8,24},{16,0},{24,8},{1,17},{9,25},{17,1},{25,9},{2,18},{10... | collective-permute-start | bytes 516104 | tf_op jit(solution)/shard_map/ppermute | solution.py:534
  116.7 14.7 %collective-permute-start.21 = (bf16[96,768]{1,0:T(8,128)(2,1)S(1)}, bf16[96,768]{1,0:T(8,128)(2,1)S(1)}, u32[]{:S(2)}, u32[]{:S(2)}) collective-permute-start(bf16[96,768]{1,0:T(8,128)(2,1)S(1)} %add_convert_fusion.10), channel_id=1, source_target_pairs={{0,16},{8,24},{16,0},{24,8},{1,17},{9,25},{17,1},{25,9},{2,18},{10... | collective-permute-start | bytes 442376 | tf_op jit(solution)/shard_map/ppermute | solution.py:534
  129.8 12.1 %collective-permute-start.27 = (bf16[112,768]{1,0:T(8,128)(2,1)S(1)}, bf16[112,768]{1,0:T(8,128)(2,1)S(1)}, u32[]{:S(2)}, u32[]{:S(2)}) collective-permute-start(bf16[112,768]{1,0:T(8,128)(2,1)S(1)} %add_convert_fusion.8.mine), channel_id=1, source_target_pairs={{0,8},{8,0},{16,24},{24,16},{1,9},{9,1},{17,25},{25,17},{2,10},{10... | collective-permute-start | bytes 516104 | tf_op jit(solution)/shard_map/ppermute | solution.py:534
  132.1 12.1 %collective-permute-start.33 = (bf16[224,768]{1,0:T(8,128)(2,1)S(1)}, bf16[224,768]{1,0:T(8,128)(2,1)S(1)}, u32[]{:S(2)}, u32[]{:S(2)}) collective-permute-start(bf16[224,768]{1,0:T(8,128)(2,1)S(1)} %shard_map.160.refs_0_), channel_id=1, source_target_pairs={{0,4},{4,0},{1,5},{5,1},{2,6},{6,2},{3,7},{7,3},{8,12},{12,8},{9,1... | collective-permute-start | bytes 1032200 | tf_op jit(solution)/shard_map/ppermute | solution.py:534
  133.7 11.9 %collective-permute-start.38 = (bf16[224,768]{1,0:T(8,128)(2,1)S(1)}, bf16[224,768]{1,0:T(8,128)(2,1)S(1)}, u32[]{:S(2)}, u32[]{:S(2)}) collective-permute-start(bf16[224,768]{1,0:T(8,128)(2,1)S(1)} %shard_map.162.refs_2_), channel_id=1, source_target_pairs={{0,8},{8,0},{16,24},{24,16},{1,9},{9,1},{17,25},{25,17},{2,10},{10... | collective-permute-start | bytes 1032200 | tf_op jit(solution)/shard_map/ppermute | solution.py:534
  140.3 17.7 %collective-permute-start.23 = (bf16[192,768]{1,0:T(8,128)(2,1)S(1)}, bf16[192,768]{1,0:T(8,128)(2,1)S(1)}, u32[]{:S(2)}, u32[]{:S(2)}) collective-permute-start(bf16[192,768]{1,0:T(8,128)(2,1)S(1)} %shard_map.153.refs_0_), channel_id=1, source_target_pairs={{0,4},{4,0},{1,5},{5,1},{2,6},{6,2},{3,7},{7,3},{8,12},{12,8},{9,1... | collective-permute-start | bytes 884744 | tf_op jit(solution)/shard_map/ppermute | solution.py:534
  141.9 16.1 %collective-permute-start.28 = (bf16[208,768]{1,0:T(8,128)(2,1)S(1)}, bf16[208,768]{1,0:T(8,128)(2,1)S(1)}, u32[]{:S(2)}, u32[]{:S(2)}) collective-permute-start(bf16[208,768]{1,0:T(8,128)(2,1)S(1)} %shard_map.156.refs_2_), channel_id=1, source_target_pairs={{0,4},{4,0},{1,5},{5,1},{2,6},{6,2},{3,7},{7,3},{8,12},{12,8},{9,1... | collective-permute-start | bytes 958472 | tf_op jit(solution)/shard_map/ppermute | solution.py:534
  142.6 14.4 %collective-permute-start.18 = (f32[208,64]{1,0:T(8,128)S(1)}, f32[208,64]{1,0:T(8,128)S(1)}, u32[]{:S(2)}, u32[]{:S(2)}) collective-permute-start(f32[208,64]{1,0:T(8,128)S(1)} %slice_select_fusion), channel_id=1, source_target_pairs={{0,4},{4,0},{1,5},{5,1},{2,6},{6,2},{3,7},{7,3},{8,12},{12,8},{9,1... | collective-permute-start | bytes 159752 | tf_op jit(solution)/shard_map/ppermute | solution.py:534
  (20 other events, 142.9 us)

commit v5 on v4

--- a/solution.py
+++ b/solution.py
@@ -161,7 +161,7 @@
         return a * c - b * s, b * c + a * s
 
     def one_head(h, carry):
-        row = pl.multiple_of(h * HEAD, HEAD)
+        row = h * HEAD
         own = slice(0, length)
         every = slice(0, tokens)
         upper, lower = rope(row, own)
@@ -188,7 +188,8 @@
             mixed[pl.ds(row, HEAD), mine] = nn(value[:, wide], weights).astype(BF16)
         return carry
 
-    lax.fori_loop(0, heads, one_head, 0)
+    for h in range(heads):
+        one_head(h, 0)
     copies[2].wait()
     terms[...] = tn(wo[...], mixed[...])
     split_half(terms, keep, send, core)
@@ -347,7 +348,7 @@
         return a * c + b * s, b * c - a * s
 
     def one_head(h, carry):
-        row = pl.multiple_of(h * HEAD, HEAD)
+        row = h * HEAD
         head = pl.ds(row, HEAD)
         for j in range(length // TILE):
             wide = slice(j * TILE, (j + 2) * TILE)
@@ -371,14 +372,15 @@
         proj_grad[head, length:tokens] = jnp.zeros((HEAD, tokens - length), BF16)
         keys_grad = pltpu.roll(dk[head, :], tokens - HALF, 1)
         upper, lower = unrope(keys_grad[:half], keys_grad[half:], every)
-        at = pl.multiple_of(columns + row, HEAD)
+        at = columns + row
         proj_grad[pl.ds(at, half), :] = upper.astype(BF16)
         proj_grad[pl.ds(at + half, half), :] = lower.astype(BF16)
-        at = pl.multiple_of(2 * columns + row, HEAD)
+        at = 2 * columns + row
         proj_grad[pl.ds(at, HEAD), :] = pltpu.roll(dv[head, :], tokens - HALF, 1).astype(BF16)
         return carry
 
-    lax.fori_loop(0, heads, one_head, 0)
+    for h in range(heads):
+        one_head(h, 0)
     stack[0:columns, :] = nt(proj_grad[2 * columns : 3 * columns, :], fed[...])
     stack[columns : 2 * columns, :] = nt(mixed[...], low[...])
     stack[2 * columns : 4 * columns, :] = nt(proj_grad[0 : 2 * columns, :], fed[...])

time: 161 us -> 160 us (level)
  no operation moved by 1% of the time
where the time goes in v5:
time: 160 us; the launch traced here: 159 us
  waiting for transfers between devices  87.3 us (55%)
  starting transfers between devices  36.7 us (23%)
  Pallas kernels  29.8 us (19%)
  other arithmetic  2.24 us (1%)
  local copies, waits for them, and re-layouts  2.16 us (1%)
    ppermute x39, waiting for transfers between devices, flip(): return lax.ppermute(x, axis, [(i, i ^ bit) for i in range(count)])  87.3 us
    ppermute x39, starting transfers between devices, flip(): return lax.ppermute(x, axis, [(i, i ^ bit) for i in range(count)])  36.7 us
    pallas_call x21, Pallas kernels, call(): return run(*args)  29.8 us
  transfers between devices with their start and end apart: 39, of which 19 were waited for; matrix products, arithmetic and copies ran while one was open for 2% of the time, Pallas kernels for 5%

profile of v5, /device:TPU:0, one launch (start us, length us, event | category | flops | bytes accessed | tf_op | source)
XLA Modules:
  0.0 159.2 jit_solution(8990037199015422316)
XLA Ops:
  0.6 3.0 %collective-permute-start.1 = (bf16[192,512]{1,0:T(8,128)(2,1)}, bf16[192,512]{1,0:T(8,128)(2,1)S(1)}, u32[]{:S(2)}, u32[]{:S(2)}) collective-permute-start(bf16[192,512]{1,0:T(8,128)(2,1)} %bitcast.33), channel_id=1, source_target_pairs={{0,2},{1,3},{2,0},{3,1},{4,6},{5,7},{6,4},{7,5},{8,10},{9,11},{10,... | collective-permute-start | bytes 589832 | tf_op jit(solution)/shard_map/ppermute | solution.py:536
  6.2 2.6 %collective-permute-done.3 = bf16[192,64]{1,0:T(8,128)(2,1)S(1)} collective-permute-done((bf16[192,64]{1,0:T(8,128)(2,1)S(1)}, bf16[192,64]{1,0:T(8,128)(2,1)S(1)}, u32[]{:S(2)}, u32[]{:S(2)}) %collective-permute-start.3) | collective-permute-done | bytes 24608 | tf_op jit(solution)/shard_map/ppermute | solution.py:536
  14.3 7.4 %shard_map.143 = (bf16[768,640]{1,0:T(8,128)(2,1)S(1)}, f32[8,640]{1,0:T(8,128)S(1)}, bf16[768,640]{1,0:T(8,128)(2,1)S(1)}, bf16[192,512]{1,0:T(8,128)(2,1)S(1)}...) custom-call(bf16[192,512]{1,0:T(8,128)(2,1)S(1)} %collective-permute, ...), custom_call_target="tpu_custom_call" | custom-call | tf_op jit(solution)/shard_map/pallas_call | solution.py:40
  24.1 1.7 %collective-permute-start.11 = (bf16[192,512]{1,0:T(8,128)(2,1)S(1)}, bf16[192,512]{1,0:T(8,128)(2,1)S(1)}, u32[]{:S(2)}, u32[]{:S(2)}) collective-permute-start(bf16[192,512]{1,0:T(8,128)(2,1)S(1)} %bitcast.30), channel_id=1, source_target_pairs={{0,2},{1,3},{2,0},{3,1},{4,6},{5,7},{6,4},{7,5},{8,10},{9,11},{10,... | collective-permute-start | bytes 589832 | tf_op jit(solution)/shard_map/ppermute | solution.py:536
  25.8 10.0 %collective-permute-done.8 = bf16[384,512]{1,0:T(8,128)(2,1)S(1)} collective-permute-done((bf16[384,512]{1,0:T(8,128)(2,1)S(1)}, bf16[384,512]{1,0:T(8,128)(2,1)S(1)}, u32[]{:S(2)}, u32[]{:S(2)}) %collective-permute-start.8) | collective-permute-done | bytes 393248 | tf_op jit(solution)/shard_map/ppermute | solution.py:536
  36.4 2.7 %collective-permute-done.11.u2 = bf16[192,512]{1,0:T(8,128)(2,1)S(1)} collective-permute-done((bf16[192,512]{1,0:T(8,128)(2,1)S(1)}, bf16[192,512]{1,0:T(8,128)(2,1)S(1)}, u32[]{:S(2)}, u32[]{:S(2)}) %collective-permute-start.11) | collective-permute-done | bytes 196640 | tf_op jit(solution)/shard_map/ppermute | solution.py:536
  40.6 3.8 %shard_map.145 = (f32[192,512]{1,0:T(8,128)S(1)}, f32[768,512]{1,0:T(8,128)S(1)}, f32[8,512]{1,0:T(8,128)S(1)}, bf16[768,512]{1,0:T(8,128)(2,1)S(1)}, bf16[768,5...) custom-call(bf16[768,640]{1,0:T(8,128)(2,1)S(1)} %get-tuple-element., ...), custom_call_target="tpu_custom_call" | custom-call | tf_op jit(solution)/shard_map/pallas_call | solution.py:40
  46.7 10.9 %collective-permute-done.14 = bf16[384,512]{1,0:T(8,128)(2,1)S(1)} collective-permute-done((bf16[384,512]{1,0:T(8,128)(2,1)S(1)}, bf16[384,512]{1,0:T(8,128)(2,1)S(1)}, u32[]{:S(2)}, u32[]{:S(2)}) %collective-permute-start.14) | collective-permute-done | bytes 393248 | tf_op jit(solution)/shard_map/ppermute | solution.py:536
  57.7 1.7 %collective-permute-done.15.other = bf16[384,512]{1,0:T(8,128)(2,1)S(1)} collective-permute-done((bf16[384,512]{1,0:T(8,128)(2,1)S(1)}, bf16[384,512]{1,0:T(8,128)(2,1)S(1)}, u32[]{:S(2)}, u32[]{:S(2)}) %collective-permute-start.15) | collective-permute-done | bytes 393248 | tf_op jit(solution)/shard_map/ppermute | solution.py:536
  59.4 6.7 %shard_map.146 = (f32[192,512]{1,0:T(8,128)S(1)}, f32[192,128]{1,0:T(8,128)S(1)}, bf16[576,640]{1,0:T(8,128)(2,1)S(1)}, f32[192,768]{1,0:T(8,128)S(1)}, bf16[192...) custom-call(bf16[384,512]{1,0:T(8,128)(2,1)S(1)} %add_convert_fusion.mine, ...), custom_call_target="tpu_custom_call" | custom-call | tf_op jit(solution)/shard_map/pallas_call | solution.py:40
  66.1 3.0 %shard_map.147 = (f32[400,1152]{1,0:T(8,128)S(1)}, bf16[400,1152]{1,0:T(8,128)(2,1)S(1)}) custom-call(bf16[576,640]{1,0:T(8,128)(2,1)S(1)} %get-tuple-element.86.proj_grad, bf16[768,576]{1,0:T(8,128)(2,1)S(1)} %get-tuple-element.87.w, f32[768,2]{1,0:T(8,128)S(1)} %copy.18.gain, bf16[768,640]{1,0:T(8,128)(2,1)S(1)} %get-tuple-element.69.xall, ...), custom_call_target="tpu_custom_call" | custom-call | tf_op jit(solution)/shard_map/pallas_call | solution.py:40
  73.7 7.2 %collective-permute-done.29.got = bf16[224,768]{1,0:T(8,128)(2,1)S(1)} collective-permute-done((bf16[224,768]{1,0:T(8,128)(2,1)S(1)}, bf16[224,768]{1,0:T(8,128)(2,1)S(1)}, u32[]{:S(2)}, u32[]{:S(2)}) %collective-permute-start.29) | collective-permute-done | bytes 344096 | tf_op jit(solution)/shard_map/ppermute | solution.py:536
  81.0 1.6 %collective-permute-start.30 = (bf16[112,768]{1,0:T(8,128)(2,1)S(1)}, bf16[112,768]{1,0:T(8,128)(2,1)S(1)}, u32[]{:S(2)}, u32[]{:S(2)}) collective-permute-start(bf16[112,768]{1,0:T(8,128)(2,1)S(1)} %get-tuple-element.123), channel_id=1, source_target_pairs={{0,8},{8,0},{16,24},{24,16},{1,9},{9,1},{17,25},{25,17},{2,10},{10... | collective-permute-start | bytes 516104 | tf_op jit(solution)/shard_map/ppermute | solution.py:536
  84.6 2.3 %collective-permute-done.30 = bf16[112,768]{1,0:T(8,128)(2,1)S(1)} collective-permute-done((bf16[112,768]{1,0:T(8,128)(2,1)S(1)}, bf16[112,768]{1,0:T(8,128)(2,1)S(1)}, u32[]{:S(2)}, u32[]{:S(2)}) %collective-permute-start.30) | collective-permute-done | bytes 172064 | tf_op jit(solution)/shard_map/ppermute | solution.py:536
  86.9 2.7 %collective-permute-start.31 = (bf16[112,768]{1,0:T(8,128)(2,1)S(1)}, bf16[112,768]{1,0:T(8,128)(2,1)S(1)}, u32[]{:S(2)}, u32[]{:S(2)}) collective-permute-start(bf16[112,768]{1,0:T(8,128)(2,1)S(1)} %add_convert_fusion.7), channel_id=1, source_target_pairs={{0,16},{8,24},{16,0},{24,8},{1,17},{9,25},{17,1},{25,9},{2,18},{10... | collective-permute-start | bytes 516104 | tf_op jit(solution)/shard_map/ppermute | solution.py:536
  92.8 8.6 %collective-permute-done.31 = bf16[112,768]{1,0:T(8,128)(2,1)S(1)} collective-permute-done((bf16[112,768]{1,0:T(8,128)(2,1)S(1)}, bf16[112,768]{1,0:T(8,128)(2,1)S(1)}, u32[]{:S(2)}, u32[]{:S(2)}) %collective-permute-start.31) | collective-permute-done | bytes 172064 | tf_op jit(solution)/shard_map/ppermute | solution.py:536
  101.6 2.0 %collective-permute-start.20 = (bf16[96,768]{1,0:T(8,128)(2,1)S(1)}, bf16[96,768]{1,0:T(8,128)(2,1)S(1)}, u32[]{:S(2)}, u32[]{:S(2)}) collective-permute-start(bf16[96,768]{1,0:T(8,128)(2,1)S(1)} %get-tuple-element.105), channel_id=1, source_target_pairs={{0,8},{8,0},{16,24},{24,16},{1,9},{9,1},{17,25},{25,17},{2,10},{10... | collective-permute-start | bytes 442376 | tf_op jit(solution)/shard_map/ppermute | solution.py:536
  108.0 5.9 %collective-permute-done.25.got = bf16[96,768]{1,0:T(8,128)(2,1)S(1)} collective-permute-done((bf16[96,768]{1,0:T(8,128)(2,1)S(1)}, bf16[96,768]{1,0:T(8,128)(2,1)S(1)}, u32[]{:S(2)}, u32[]{:S(2)}) %collective-permute-start.25) | collective-permute-done | bytes 147488 | tf_op jit(solution)/shard_map/ppermute | solution.py:536
  113.9 1.7 %collective-permute-start.26 = (bf16[112,768]{1,0:T(8,128)(2,1)S(1)}, bf16[112,768]{1,0:T(8,128)(2,1)S(1)}, u32[]{:S(2)}, u32[]{:S(2)}) collective-permute-start(bf16[112,768]{1,0:T(8,128)(2,1)S(1)} %shard_map.155), channel_id=1, source_target_pairs={{0,16},{8,24},{16,0},{24,8},{1,17},{9,25},{17,1},{25,9},{2,18},{10... | collective-permute-start | bytes 516104 | tf_op jit(solution)/shard_map/ppermute | solution.py:536
  117.0 11.6 %collective-permute-done.26 = bf16[112,768]{1,0:T(8,128)(2,1)S(1)} collective-permute-done((bf16[112,768]{1,0:T(8,128)(2,1)S(1)}, bf16[112,768]{1,0:T(8,128)(2,1)S(1)}, u32[]{:S(2)}, u32[]{:S(2)}) %collective-permute-start.26) | collective-permute-done | bytes 172064 | tf_op jit(solution)/shard_map/ppermute | solution.py:536
  134.2 5.0 %collective-permute-done.22.other = bf16[96,768]{1,0:T(8,128)(2,1)S(1)} collective-permute-done((bf16[96,768]{1,0:T(8,128)(2,1)S(1)}, bf16[96,768]{1,0:T(8,128)(2,1)S(1)}, u32[]{:S(2)}, u32[]{:S(2)}) %collective-permute-start.22) | collective-permute-done | bytes 147488 | tf_op jit(solution)/shard_map/ppermute | solution.py:536
  144.4 1.8 %shard_map.163 = (f32[576,768]{1,0:T(8,128)}, f32[288,768]{1,0:T(8,128)}) custom-call(bf16[224,768]{1,0:T(8,128)(2,1)S(1)} %shard_map.160.refs_0_, bf16[224,768]{1,0:T(8,128)(2,1)S(1)} %collective-permute-done.33.refs_1_, bf16[224,768]{1,0:T(8,128)(2,1)S(1)} %shard_map.162.refs_2_, bf16[224,768]{1,0:T(8,128)(2,1)S(1)} %collective-permute-done.38.refs_3_), custom_call_target="tpu_custom_call" | custom-call | tf_op jit(solution)/shard_map/pallas_call | solution.py:40
  146.3 9.7 %collective-permute-done.18 = f32[208,64]{1,0:T(8,128)S(1)} collective-permute-done((f32[208,64]{1,0:T(8,128)S(1)}, f32[208,64]{1,0:T(8,128)S(1)}, u32[]{:S(2)}, u32[]{:S(2)}) %collective-permute-start.18) | collective-permute-done | bytes 53280 | tf_op jit(solution)/shard_map/ppermute | solution.py:536
  157.5 1.7 %shard_map.157 = (f32[576,768]{1,0:T(8,128)}, f32[192,768]{1,0:T(8,128)}) custom-call(bf16[192,768]{1,0:T(8,128)(2,1)S(1)} %shard_map.153.refs_0_, bf16[192,768]{1,0:T(8,128)(2,1)S(1)} %collective-permute-done.23.refs_1_, bf16[208,768]{1,0:T(8,128)(2,1)S(1)} %shard_map.156.refs_2_, bf16[208,768]{1,0:T(8,128)(2,1)S(1)} %collective-permute-done.28.refs_3_), custom_call_target="tpu_custom_call" | custom-call | tf_op jit(solution)/shard_map/pallas_call | solution.py:40
  (110 shorter events, 43.0 us)
Async XLA Ops:
  3.7 10.6 %collective-permute-start = (bf16[192,512]{1,0:T(8,128)(2,1)}, bf16[192,512]{1,0:T(8,128)(2,1)S(1)}, u32[]{:S(2)}, u32[]{:S(2)}) collective-permute-start(bf16[192,512]{1,0:T(8,128)(2,1)} %bitcast.34), channel_id=1, source_target_pairs={{0,1},{1,0},{2,3},{3,2},{4,5},{5,4},{6,7},{7,6},{8,9},{9,8},{10,11... | collective-permute-start | bytes 589832 | tf_op jit(solution)/shard_map/ppermute | solution.py:536
  23.7 12.1 %collective-permute-start.8 = (bf16[384,512]{1,0:T(8,128)(2,1)S(1)}, bf16[384,512]{1,0:T(8,128)(2,1)S(1)}, u32[]{:S(2)}, u32[]{:S(2)}) collective-permute-start(bf16[384,512]{1,0:T(8,128)(2,1)S(1)} %add_convert_fusion.3), channel_id=1, source_target_pairs={{0,2},{1,3},{2,0},{3,1},{4,6},{5,7},{6,4},{7,5},{8,10},{9,11},{10,... | collective-permute-start | bytes 1179656 | tf_op jit(solution)/shard_map/ppermute | solution.py:536
  24.1 15.1 %collective-permute-start.11 = (bf16[192,512]{1,0:T(8,128)(2,1)S(1)}, bf16[192,512]{1,0:T(8,128)(2,1)S(1)}, u32[]{:S(2)}, u32[]{:S(2)}) collective-permute-start(bf16[192,512]{1,0:T(8,128)(2,1)S(1)} %bitcast.30), channel_id=1, source_target_pairs={{0,2},{1,3},{2,0},{3,1},{4,6},{5,7},{6,4},{7,5},{8,10},{9,11},{10,... | collective-permute-start | bytes 589832 | tf_op jit(solution)/shard_map/ppermute | solution.py:536
  46.3 11.2 %collective-permute-start.14 = (bf16[384,512]{1,0:T(8,128)(2,1)S(1)}, bf16[384,512]{1,0:T(8,128)(2,1)S(1)}, u32[]{:S(2)}, u32[]{:S(2)}) collective-permute-start(bf16[384,512]{1,0:T(8,128)(2,1)S(1)} %add_convert_fusion.1), channel_id=1, source_target_pairs={{0,2},{1,3},{2,0},{3,1},{4,6},{5,7},{6,4},{7,5},{8,10},{9,11},{10,... | collective-permute-start | bytes 1179656 | tf_op jit(solution)/shard_map/ppermute | solution.py:536
  69.1 22.5 %collective-permute-start.16 = (bf16[400,1152]{1,0:T(8,128)(2,1)S(1)}, bf16[400,1152]{1,0:T(8,128)(2,1)S(1)}, u32[]{:S(2)}, u32[]{:S(2)}) collective-permute-start(bf16[400,1152]{1,0:T(8,128)(2,1)S(1)} %get-tuple-element.92), channel_id=1, source_target_pairs={{0,1},{1,0},{2,3},{3,2},{4,5},{5,4},{6,7},{7,6},{8,9},{9,8},{10,11... | collective-permute-start | bytes 2764808 | tf_op jit(solution)/shard_map/ppermute | solution.py:536
  70.5 10.4 %collective-permute-start.29 = (bf16[224,768]{1,0:T(8,128)(2,1)S(1)}, bf16[224,768]{1,0:T(8,128)(2,1)S(1)}, u32[]{:S(2)}, u32[]{:S(2)}) collective-permute-start(bf16[224,768]{1,0:T(8,128)(2,1)S(1)} %get-tuple-element.121), channel_id=1, source_target_pairs={{0,4},{4,0},{1,5},{5,1},{2,6},{6,2},{3,7},{7,3},{8,12},{12,8},{9,1... | collective-permute-start | bytes 1032200 | tf_op jit(solution)/shard_map/ppermute | solution.py:536
  72.1 10.7 %collective-permute-start.34 = (bf16[224,768]{1,0:T(8,128)(2,1)S(1)}, bf16[224,768]{1,0:T(8,128)(2,1)S(1)}, u32[]{:S(2)}, u32[]{:S(2)}) collective-permute-start(bf16[224,768]{1,0:T(8,128)(2,1)S(1)} %get-tuple-element.125), channel_id=1, source_target_pairs={{0,8},{8,0},{16,24},{24,16},{1,9},{9,1},{17,25},{25,17},{2,10},{10... | collective-permute-start | bytes 1032200 | tf_op jit(solution)/shard_map/ppermute | solution.py:536
  86.9 14.4 %collective-permute-start.31 = (bf16[112,768]{1,0:T(8,128)(2,1)S(1)}, bf16[112,768]{1,0:T(8,128)(2,1)S(1)}, u32[]{:S(2)}, u32[]{:S(2)}) collective-permute-start(bf16[112,768]{1,0:T(8,128)(2,1)S(1)} %add_convert_fusion.7), channel_id=1, source_target_pairs={{0,16},{8,24},{16,0},{24,8},{1,17},{9,25},{17,1},{25,9},{2,18},{10... | collective-permute-start | bytes 516104 | tf_op jit(solution)/shard_map/ppermute | solution.py:536
  89.6 11.9 %collective-permute-start.19 = (bf16[192,768]{1,0:T(8,128)(2,1)S(1)}, bf16[192,768]{1,0:T(8,128)(2,1)S(1)}, u32[]{:S(2)}, u32[]{:S(2)}) collective-permute-start(bf16[192,768]{1,0:T(8,128)(2,1)S(1)} %get-tuple-element.103), channel_id=1, source_target_pairs={{0,4},{4,0},{1,5},{5,1},{2,6},{6,2},{3,7},{7,3},{8,12},{12,8},{9,1... | collective-permute-start | bytes 884744 | tf_op jit(solution)/shard_map/ppermute | solution.py:536
  91.1 12.5 %collective-permute-start.24 = (bf16[192,768]{1,0:T(8,128)(2,1)S(1)}, bf16[192,768]{1,0:T(8,128)(2,1)S(1)}, u32[]{:S(2)}, u32[]{:S(2)}) collective-permute-start(bf16[192,768]{1,0:T(8,128)(2,1)S(1)} %get-tuple-element.107), channel_id=1, source_target_pairs={{0,4},{4,0},{1,5},{5,1},{2,6},{6,2},{3,7},{7,3},{8,12},{12,8},{9,1... | collective-permute-start | bytes 884744 | tf_op jit(solution)/shard_map/ppermute | solution.py:536
  91.9 14.7 %collective-permute-start.17 = (bf16[208,1152]{1,0:T(8,128)(2,1)S(1)}, bf16[208,1152]{1,0:T(8,128)(2,1)S(1)}, u32[]{:S(2)}, u32[]{:S(2)}) collective-permute-start(bf16[208,1152]{1,0:T(8,128)(2,1)S(1)} %get-tuple-element.94), channel_id=1, source_target_pairs={{0,2},{1,3},{2,0},{3,1},{4,6},{5,7},{6,4},{7,5},{8,10},{9,11},{10,... | collective-permute-start | bytes 1437704 | tf_op jit(solution)/shard_map/ppermute | solution.py:536
  92.5 12.4 %collective-permute-start.36 = (bf16[112,768]{1,0:T(8,128)(2,1)S(1)}, bf16[112,768]{1,0:T(8,128)(2,1)S(1)}, u32[]{:S(2)}, u32[]{:S(2)}) collective-permute-start(bf16[112,768]{1,0:T(8,128)(2,1)S(1)} %add_convert_fusion.5), channel_id=1, source_target_pairs={{0,16},{8,24},{16,0},{24,8},{1,17},{9,25},{17,1},{25,9},{2,18},{10... | collective-permute-start | bytes 516104 | tf_op jit(solution)/shard_map/ppermute | solution.py:536
  101.4 29.5 %collective-permute-start.32 = (bf16[112,768]{1,0:T(8,128)(2,1)S(1)}, bf16[112,768]{1,0:T(8,128)(2,1)S(1)}, u32[]{:S(2)}, u32[]{:S(2)}) collective-permute-start(bf16[112,768]{1,0:T(8,128)(2,1)S(1)} %add_convert_fusion.6.mine), channel_id=1, source_target_pairs={{0,8},{8,0},{16,24},{24,16},{1,9},{9,1},{17,25},{25,17},{2,10},{10... | collective-permute-start | bytes 516104 | tf_op jit(solution)/shard_map/ppermute | solution.py:536
  101.6 14.0 %collective-permute-start.20 = (bf16[96,768]{1,0:T(8,128)(2,1)S(1)}, bf16[96,768]{1,0:T(8,128)(2,1)S(1)}, u32[]{:S(2)}, u32[]{:S(2)}) collective-permute-start(bf16[96,768]{1,0:T(8,128)(2,1)S(1)} %get-tuple-element.105), channel_id=1, source_target_pairs={{0,8},{8,0},{16,24},{24,16},{1,9},{9,1},{17,25},{25,17},{2,10},{10... | collective-permute-start | bytes 442376 | tf_op jit(solution)/shard_map/ppermute | solution.py:536
  103.7 10.2 %collective-permute-start.25 = (bf16[96,768]{1,0:T(8,128)(2,1)S(1)}, bf16[96,768]{1,0:T(8,128)(2,1)S(1)}, u32[]{:S(2)}, u32[]{:S(2)}) collective-permute-start(bf16[96,768]{1,0:T(8,128)(2,1)S(1)} %get-tuple-element.109), channel_id=1, source_target_pairs={{0,8},{8,0},{16,24},{24,16},{1,9},{9,1},{17,25},{25,17},{2,10},{10... | collective-permute-start | bytes 442376 | tf_op jit(solution)/shard_map/ppermute | solution.py:536
  105.0 27.6 %collective-permute-start.37 = (bf16[112,768]{1,0:T(8,128)(2,1)S(1)}, bf16[112,768]{1,0:T(8,128)(2,1)S(1)}, u32[]{:S(2)}, u32[]{:S(2)}) collective-permute-start(bf16[112,768]{1,0:T(8,128)(2,1)S(1)} %add_convert_fusion.4.mine), channel_id=1, source_target_pairs={{0,4},{4,0},{1,5},{5,1},{2,6},{6,2},{3,7},{7,3},{8,12},{12,8},{9,1... | collective-permute-start | bytes 516104 | tf_op jit(solution)/shard_map/ppermute | solution.py:536
  113.9 14.7 %collective-permute-start.26 = (bf16[112,768]{1,0:T(8,128)(2,1)S(1)}, bf16[112,768]{1,0:T(8,128)(2,1)S(1)}, u32[]{:S(2)}, u32[]{:S(2)}) collective-permute-start(bf16[112,768]{1,0:T(8,128)(2,1)S(1)} %shard_map.155), channel_id=1, source_target_pairs={{0,16},{8,24},{16,0},{24,8},{1,17},{9,25},{17,1},{25,9},{2,18},{10... | collective-permute-start | bytes 516104 | tf_op jit(solution)/shard_map/ppermute | solution.py:536
  115.6 14.7 %collective-permute-start.21 = (bf16[96,768]{1,0:T(8,128)(2,1)S(1)}, bf16[96,768]{1,0:T(8,128)(2,1)S(1)}, u32[]{:S(2)}, u32[]{:S(2)}) collective-permute-start(bf16[96,768]{1,0:T(8,128)(2,1)S(1)} %add_convert_fusion.10), channel_id=1, source_target_pairs={{0,16},{8,24},{16,0},{24,8},{1,17},{9,25},{17,1},{25,9},{2,18},{10... | collective-permute-start | bytes 442376 | tf_op jit(solution)/shard_map/ppermute | solution.py:536
  128.7 12.1 %collective-permute-start.27 = (bf16[112,768]{1,0:T(8,128)(2,1)S(1)}, bf16[112,768]{1,0:T(8,128)(2,1)S(1)}, u32[]{:S(2)}, u32[]{:S(2)}) collective-permute-start(bf16[112,768]{1,0:T(8,128)(2,1)S(1)} %add_convert_fusion.8.mine), channel_id=1, source_target_pairs={{0,8},{8,0},{16,24},{24,16},{1,9},{9,1},{17,25},{25,17},{2,10},{10... | collective-permute-start | bytes 516104 | tf_op jit(solution)/shard_map/ppermute | solution.py:536
  130.9 12.2 %collective-permute-start.33 = (bf16[224,768]{1,0:T(8,128)(2,1)S(1)}, bf16[224,768]{1,0:T(8,128)(2,1)S(1)}, u32[]{:S(2)}, u32[]{:S(2)}) collective-permute-start(bf16[224,768]{1,0:T(8,128)(2,1)S(1)} %shard_map.160.refs_0_), channel_id=1, source_target_pairs={{0,4},{4,0},{1,5},{5,1},{2,6},{6,2},{3,7},{7,3},{8,12},{12,8},{9,1... | collective-permute-start | bytes 1032200 | tf_op jit(solution)/shard_map/ppermute | solution.py:536
  132.6 11.8 %collective-permute-start.38 = (bf16[224,768]{1,0:T(8,128)(2,1)S(1)}, bf16[224,768]{1,0:T(8,128)(2,1)S(1)}, u32[]{:S(2)}, u32[]{:S(2)}) collective-permute-start(bf16[224,768]{1,0:T(8,128)(2,1)S(1)} %shard_map.162.refs_2_), channel_id=1, source_target_pairs={{0,8},{8,0},{16,24},{24,16},{1,9},{9,1},{17,25},{25,17},{2,10},{10... | collective-permute-start | bytes 1032200 | tf_op jit(solution)/shard_map/ppermute | solution.py:536
  139.2 17.8 %collective-permute-start.23 = (bf16[192,768]{1,0:T(8,128)(2,1)S(1)}, bf16[192,768]{1,0:T(8,128)(2,1)S(1)}, u32[]{:S(2)}, u32[]{:S(2)}) collective-permute-start(bf16[192,768]{1,0:T(8,128)(2,1)S(1)} %shard_map.153.refs_0_), channel_id=1, source_target_pairs={{0,4},{4,0},{1,5},{5,1},{2,6},{6,2},{3,7},{7,3},{8,12},{12,8},{9,1... | collective-permute-start | bytes 884744 | tf_op jit(solution)/shard_map/ppermute | solution.py:536
  140.9 16.1 %collective-permute-start.28 = (bf16[208,768]{1,0:T(8,128)(2,1)S(1)}, bf16[208,768]{1,0:T(8,128)(2,1)S(1)}, u32[]{:S(2)}, u32[]{:S(2)}) collective-permute-start(bf16[208,768]{1,0:T(8,128)(2,1)S(1)} %shard_map.156.refs_2_), channel_id=1, source_target_pairs={{0,4},{4,0},{1,5},{5,1},{2,6},{6,2},{3,7},{7,3},{8,12},{12,8},{9,1... | collective-permute-start | bytes 958472 | tf_op jit(solution)/shard_map/ppermute | solution.py:536
  141.5 14.5 %collective-permute-start.18 = (f32[208,64]{1,0:T(8,128)S(1)}, f32[208,64]{1,0:T(8,128)S(1)}, u32[]{:S(2)}, u32[]{:S(2)}) collective-permute-start(f32[208,64]{1,0:T(8,128)S(1)} %slice_select_fusion), channel_id=1, source_target_pairs={{0,4},{4,0},{1,5},{5,1},{2,6},{6,2},{3,7},{7,3},{8,12},{12,8},{9,1... | collective-permute-start | bytes 159752 | tf_op jit(solution)/shard_map/ppermute | solution.py:536
  (20 other events, 142.1 us)

commit v6 on v5

--- a/solution.py
+++ b/solution.py
@@ -57,6 +57,10 @@
         return fn(pl.multiple_of(i * step, step), carry)
 
     return lax.fori_loop(0, rows // step, one, init)
+
+
+def step_of(rows):
+    return next(step for step in (64, 48, 32, 16) if rows % step == 0)
 
 
 def fold(x):
@@ -92,15 +96,16 @@
 
 def split_half(source, keep, send, index):
     rows = keep.shape[0]
+    step = step_of(rows)
 
     def one(r, carry):
         mine = pl.multiple_of(index * rows + r, 16)
         other = pl.multiple_of((1 - index) * rows + r, 16)
-        keep[pl.ds(r, 16), :] = source[pl.ds(mine, 16), :]
-        send[pl.ds(r, 16), :] = source[pl.ds(other, 16), :].astype(send.dtype)
+        keep[pl.ds(r, step), :] = source[pl.ds(mine, step), :]
+        send[pl.ds(r, step), :] = source[pl.ds(other, step), :].astype(send.dtype)
         return carry
 
-    row_loop(rows, 16, one, 0)
+    row_loop(rows, step, one, 0)
 
 
 def attention_kernel(
@@ -515,20 +520,30 @@
 
 def place_kernel(*refs, cuts, outs):
     count = len(cuts)
-    pieces, targets, stack = refs[: 2 * count], refs[2 * count : -1], refs[-1]
+    pieces, targets = refs[: 2 * count], refs[2 * count :]
+
+    def copy(piece, begin, size):
+        for target, spans in zip(targets, outs):
+            at = 0
+            for low, rows in spans:
+                start, stop = max(begin, low), min(begin + size, low + rows)
+                if start < stop:
+                    rows_here = piece[start - begin : stop - begin, :].astype(F32)
+                    target[at + start - low : at + stop - low, :] = rows_here
+                at += rows
+
     start = 0
     for i, (rows, order) in enumerate(cuts):
         size = rows // 2
         index = lax.axis_index(order[0]) % 2
-        for k, at in enumerate((index, 1 - index)):
-            at = pl.multiple_of(start + at * size, 16)
-            stack[pl.ds(at, size), :] = pieces[2 * i + k][0:size, :].astype(F32)
+        for value in range(2):
+
+            @pl.when(index == value)
+            def _(mine=start + value * size, other=start + (1 - value) * size, i=i, size=size):
+                copy(pieces[2 * i], mine, size)
+                copy(pieces[2 * i + 1], other, size)
+
         start += rows
-    for target, spans in zip(targets, outs):
-        at = 0
-        for begin, size in spans:
-            target[at : at + size, :] = stack[begin : begin + size, :]
-            at += size
 
 
 def flip(x, axis, bit):
@@ -625,8 +640,26 @@
     if cuts is None:
         return [jnp.concatenate([pieces[0][b : b + n] for b, n in span]) for span in spans]
     kernel = functools.partial(place_kernel, cuts=cuts, outs=spans)
-    scratch = [((sum(rows for rows, _ in cuts), width), F32)]
-    return call(kernel, [(size, F32) for size in sizes], scratch, *pieces)
+    return call(kernel, [(size, F32) for size in sizes], [], *pieces)
+
+
+def gather_edges(shard):
+    low, high = shard[:, :HALF], shard[:, -HALF:]
+    if lax.axis_size("seq") != 2:
+        after, before = to_neighbours(low, high)
+        return gather_mp(jnp.concatenate([after, before], axis=1))
+    last = lax.axis_index("seq") == 1
+    edge = jnp.where(last, low, high)
+    near = flip(edge, "seq", 1)
+    count = lax.axis_size("mp")
+    pairs = [(i, (i + count) % (2 * count) ^ 2) for i in range(2 * count)]
+    far = lax.ppermute(edge, ("seq", "mp"), pairs)
+    own, across = (
+        jnp.concatenate([jnp.where(last, 0, got), jnp.where(last, got, 0)], axis=1)
+        for got in (near, far)
+    )
+    beside = flip(own, "mp", 1)
+    return own, beside, across, flip(across, "mp", 1)
 
 
 def unit_shapes(cuts, rows, width):
@@ -663,10 +696,8 @@
     win = jnp.transpose(geglu_in, (1, 2, 0)).reshape(2 * units, width)
     gains = jnp.stack([attention_gain, feedforward_gain], axis=1)
 
-    after, before = to_neighbours(x_own[:, :HALF], x_own[:, length - HALF :])
+    h_parts = gather_edges(x_own)
     x_parts = gather_mp(x_own)
-    halo = jnp.concatenate([after, before], axis=1)
-    h_parts = gather_mp(halo)
     u_parts = gather_mp(u_own)
 
     base = (lax.axis_index("seq") * length).astype(jnp.int32)

time: 160 us -> 159 us (level)
    ppermute x0 -> x1, starting transfers between devices: none -> 3.99 us  [gather_edges(): far = lax.ppermute(edge, ('seq', 'mp'), pairs)]
    ppermute x39 -> x38, starting transfers between devices: 36.7 us -> 34 us  [flip(): return lax.ppermute(x, axis, [(i, i ^ bit) for i in range(count)])]
    ppermute x39 -> x38, waiting for transfers between devices: 87.3 us -> 86 us  [flip(): return lax.ppermute(x, axis, [(i, i ^ bit) for i in range(count)])]
  transfers between devices with their start and end apart: 39 -> 39, of which waited for: 19 -> 19; matrix products, arithmetic and copies ran while one was open for 2% -> 2% of each run, Pallas kernels for 5% -> 4%
where the time goes in v6:
time: 159 us; the launch traced here: 158 us
  waiting for transfers between devices  86 us (54%)
  starting transfers between devices  37.9 us (24%)
  Pallas kernels  29.1 us (18%)
  other arithmetic  2.34 us (1%)
  local copies, waits for them, and re-layouts  2.16 us (1%)
    ppermute x38, waiting for transfers between devices, flip(): return lax.ppermute(x, axis, [(i, i ^ bit) for i in range(count)])  86 us
    ppermute x38, starting transfers between devices, flip(): return lax.ppermute(x, axis, [(i, i ^ bit) for i in range(count)])  34 us
    pallas_call x21, Pallas kernels, call(): return run(*args)  29.1 us
    ppermute x1, starting transfers between devices, gather_edges(): far = lax.ppermute(edge, ('seq', 'mp'), pairs)  3.99 us
  transfers between devices with their start and end apart: 39, of which 19 were waited for; matrix products, arithmetic and copies ran while one was open for 2% of the time, Pallas kernels for 4%

profile of v6, /device:TPU:0, one launch (start us, length us, event | category | flops | bytes accessed | tf_op | source)
XLA Modules:
  0.0 158.5 jit_solution(7366560991467721634)
XLA Ops:
  1.6 4.0 %collective-permute-start.5 = (bf16[192,64]{1,0:T(8,128)(2,1)S(1)}, bf16[192,64]{1,0:T(8,128)(2,1)S(1)}, u32[]{:S(2)}, u32[]{:S(2)}) collective-permute-start(bf16[192,64]{1,0:T(8,128)(2,1)S(1)} %slice_select_fusion.1), channel_id=1, source_target_pairs={{0,6},{1,7},{2,4},{3,5},{4,2},{5,3},{6,0},{7,1},{8,14},{9,15},{10,... | collective-permute-start | bytes 73736 | tf_op jit(solution)/shard_map/ppermute | solution.py:656
  9.6 2.7 %collective-permute-done.1.p2 = bf16[192,512]{1,0:T(8,128)(2,1)S(1)} collective-permute-done((bf16[192,512]{1,0:T(8,128)(2,1)}, bf16[192,512]{1,0:T(8,128)(2,1)S(1)}, u32[]{:S(2)}, u32[]{:S(2)}) %collective-permute-start.1) | collective-permute-done | bytes 196640 | tf_op jit(solution)/shard_map/ppermute | solution.py:551
  13.9 7.3 %shard_map.143 = (bf16[768,640]{1,0:T(8,128)(2,1)S(1)}, f32[8,640]{1,0:T(8,128)S(1)}, bf16[768,640]{1,0:T(8,128)(2,1)S(1)}, bf16[192,512]{1,0:T(8,128)(2,1)S(1)}...) custom-call(bf16[192,512]{1,0:T(8,128)(2,1)S(1)} %collective-permute, ...), custom_call_target="tpu_custom_call" | custom-call | tf_op jit(solution)/shard_map/pallas_call | solution.py:40
  25.2 10.0 %collective-permute-done.8 = bf16[384,512]{1,0:T(8,128)(2,1)S(1)} collective-permute-done((bf16[384,512]{1,0:T(8,128)(2,1)S(1)}, bf16[384,512]{1,0:T(8,128)(2,1)S(1)}, u32[]{:S(2)}, u32[]{:S(2)}) %collective-permute-start.8) | collective-permute-done | bytes 393248 | tf_op jit(solution)/shard_map/ppermute | solution.py:551
  35.9 2.9 %collective-permute-done.11.u2 = bf16[192,512]{1,0:T(8,128)(2,1)S(1)} collective-permute-done((bf16[192,512]{1,0:T(8,128)(2,1)S(1)}, bf16[192,512]{1,0:T(8,128)(2,1)S(1)}, u32[]{:S(2)}, u32[]{:S(2)}) %collective-permute-start.11) | collective-permute-done | bytes 196640 | tf_op jit(solution)/shard_map/ppermute | solution.py:551
  40.2 3.7 %shard_map.145 = (f32[192,512]{1,0:T(8,128)S(1)}, f32[768,512]{1,0:T(8,128)S(1)}, f32[8,512]{1,0:T(8,128)S(1)}, bf16[768,512]{1,0:T(8,128)(2,1)S(1)}, bf16[768,5...) custom-call(bf16[768,640]{1,0:T(8,128)(2,1)S(1)} %get-tuple-element., ...), custom_call_target="tpu_custom_call" | custom-call | tf_op jit(solution)/shard_map/pallas_call | solution.py:40
  44.2 1.6 collective-permute-done.13
  46.8 10.2 %collective-permute-done.14 = bf16[384,512]{1,0:T(8,128)(2,1)S(1)} collective-permute-done((bf16[384,512]{1,0:T(8,128)(2,1)S(1)}, bf16[384,512]{1,0:T(8,128)(2,1)S(1)}, u32[]{:S(2)}, u32[]{:S(2)}) %collective-permute-start.14) | collective-permute-done | bytes 393248 | tf_op jit(solution)/shard_map/ppermute | solution.py:551
  57.3 1.7 %collective-permute-done.15.other = bf16[384,512]{1,0:T(8,128)(2,1)S(1)} collective-permute-done((bf16[384,512]{1,0:T(8,128)(2,1)S(1)}, bf16[384,512]{1,0:T(8,128)(2,1)S(1)}, u32[]{:S(2)}, u32[]{:S(2)}) %collective-permute-start.15) | collective-permute-done | bytes 393248 | tf_op jit(solution)/shard_map/ppermute | solution.py:551
  59.0 6.6 %shard_map.146 = (f32[192,512]{1,0:T(8,128)S(1)}, f32[192,128]{1,0:T(8,128)S(1)}, bf16[576,640]{1,0:T(8,128)(2,1)S(1)}, f32[192,768]{1,0:T(8,128)S(1)}, bf16[192...) custom-call(bf16[384,512]{1,0:T(8,128)(2,1)S(1)} %add_convert_fusion.mine, ...), custom_call_target="tpu_custom_call" | custom-call | tf_op jit(solution)/shard_map/pallas_call | solution.py:40
  65.6 3.0 %shard_map.147 = (f32[400,1152]{1,0:T(8,128)S(1)}, bf16[400,1152]{1,0:T(8,128)(2,1)S(1)}) custom-call(bf16[576,640]{1,0:T(8,128)(2,1)S(1)} %get-tuple-element.86.proj_grad, bf16[768,576]{1,0:T(8,128)(2,1)S(1)} %get-tuple-element.87.w, f32[768,2]{1,0:T(8,128)S(1)} %copy.18.gain, bf16[768,640]{1,0:T(8,128)(2,1)S(1)} %get-tuple-element.69.xall, ...), custom_call_target="tpu_custom_call" | custom-call | tf_op jit(solution)/shard_map/pallas_call | solution.py:40
  73.1 7.3 %collective-permute-done.29.got = bf16[224,768]{1,0:T(8,128)(2,1)S(1)} collective-permute-done((bf16[224,768]{1,0:T(8,128)(2,1)S(1)}, bf16[224,768]{1,0:T(8,128)(2,1)S(1)}, u32[]{:S(2)}, u32[]{:S(2)}) %collective-permute-start.29) | collective-permute-done | bytes 344096 | tf_op jit(solution)/shard_map/ppermute | solution.py:551
  80.5 1.6 %collective-permute-start.30 = (bf16[112,768]{1,0:T(8,128)(2,1)S(1)}, bf16[112,768]{1,0:T(8,128)(2,1)S(1)}, u32[]{:S(2)}, u32[]{:S(2)}) collective-permute-start(bf16[112,768]{1,0:T(8,128)(2,1)S(1)} %get-tuple-element.123), channel_id=1, source_target_pairs={{0,8},{8,0},{16,24},{24,16},{1,9},{9,1},{17,25},{25,17},{2,10},{10... | collective-permute-start | bytes 516104 | tf_op jit(solution)/shard_map/ppermute | solution.py:551
  84.0 2.3 %collective-permute-done.30 = bf16[112,768]{1,0:T(8,128)(2,1)S(1)} collective-permute-done((bf16[112,768]{1,0:T(8,128)(2,1)S(1)}, bf16[112,768]{1,0:T(8,128)(2,1)S(1)}, u32[]{:S(2)}, u32[]{:S(2)}) %collective-permute-start.30) | collective-permute-done | bytes 172064 | tf_op jit(solution)/shard_map/ppermute | solution.py:551
  86.4 2.7 %collective-permute-start.31 = (bf16[112,768]{1,0:T(8,128)(2,1)S(1)}, bf16[112,768]{1,0:T(8,128)(2,1)S(1)}, u32[]{:S(2)}, u32[]{:S(2)}) collective-permute-start(bf16[112,768]{1,0:T(8,128)(2,1)S(1)} %add_convert_fusion.7), channel_id=1, source_target_pairs={{0,16},{8,24},{16,0},{24,8},{1,17},{9,25},{17,1},{25,9},{2,18},{10... | collective-permute-start | bytes 516104 | tf_op jit(solution)/shard_map/ppermute | solution.py:551
  92.7 8.0 %collective-permute-done.31 = bf16[112,768]{1,0:T(8,128)(2,1)S(1)} collective-permute-done((bf16[112,768]{1,0:T(8,128)(2,1)S(1)}, bf16[112,768]{1,0:T(8,128)(2,1)S(1)}, u32[]{:S(2)}, u32[]{:S(2)}) %collective-permute-start.31) | collective-permute-done | bytes 172064 | tf_op jit(solution)/shard_map/ppermute | solution.py:551
  101.0 2.0 %collective-permute-start.20 = (bf16[96,768]{1,0:T(8,128)(2,1)S(1)}, bf16[96,768]{1,0:T(8,128)(2,1)S(1)}, u32[]{:S(2)}, u32[]{:S(2)}) collective-permute-start(bf16[96,768]{1,0:T(8,128)(2,1)S(1)} %get-tuple-element.105), channel_id=1, source_target_pairs={{0,8},{8,0},{16,24},{24,16},{1,9},{9,1},{17,25},{25,17},{2,10},{10... | collective-permute-start | bytes 442376 | tf_op jit(solution)/shard_map/ppermute | solution.py:551
  107.4 6.0 %collective-permute-done.25.got = bf16[96,768]{1,0:T(8,128)(2,1)S(1)} collective-permute-done((bf16[96,768]{1,0:T(8,128)(2,1)S(1)}, bf16[96,768]{1,0:T(8,128)(2,1)S(1)}, u32[]{:S(2)}, u32[]{:S(2)}) %collective-permute-start.25) | collective-permute-done | bytes 147488 | tf_op jit(solution)/shard_map/ppermute | solution.py:551
  113.4 1.6 %collective-permute-start.26 = (bf16[112,768]{1,0:T(8,128)(2,1)S(1)}, bf16[112,768]{1,0:T(8,128)(2,1)S(1)}, u32[]{:S(2)}, u32[]{:S(2)}) collective-permute-start(bf16[112,768]{1,0:T(8,128)(2,1)S(1)} %shard_map.155), channel_id=1, source_target_pairs={{0,16},{8,24},{16,0},{24,8},{1,17},{9,25},{17,1},{25,9},{2,18},{10... | collective-permute-start | bytes 516104 | tf_op jit(solution)/shard_map/ppermute | solution.py:551
  116.5 11.6 %collective-permute-done.26 = bf16[112,768]{1,0:T(8,128)(2,1)S(1)} collective-permute-done((bf16[112,768]{1,0:T(8,128)(2,1)S(1)}, bf16[112,768]{1,0:T(8,128)(2,1)S(1)}, u32[]{:S(2)}, u32[]{:S(2)}) %collective-permute-start.26) | collective-permute-done | bytes 172064 | tf_op jit(solution)/shard_map/ppermute | solution.py:551
  131.9 1.6 %collective-permute-start.38 = (bf16[224,768]{1,0:T(8,128)(2,1)S(1)}, bf16[224,768]{1,0:T(8,128)(2,1)S(1)}, u32[]{:S(2)}, u32[]{:S(2)}) collective-permute-start(bf16[224,768]{1,0:T(8,128)(2,1)S(1)} %shard_map.162.refs_2_), channel_id=1, source_target_pairs={{0,8},{8,0},{16,24},{24,16},{1,9},{9,1},{17,25},{25,17},{2,10},{10... | collective-permute-start | bytes 1032200 | tf_op jit(solution)/shard_map/ppermute | solution.py:551
  133.5 5.1 %collective-permute-done.22.other = bf16[96,768]{1,0:T(8,128)(2,1)S(1)} collective-permute-done((bf16[96,768]{1,0:T(8,128)(2,1)S(1)}, bf16[96,768]{1,0:T(8,128)(2,1)S(1)}, u32[]{:S(2)}, u32[]{:S(2)}) %collective-permute-start.22) | collective-permute-done | bytes 147488 | tf_op jit(solution)/shard_map/ppermute | solution.py:551
  143.9 1.7 %shard_map.163 = (f32[576,768]{1,0:T(8,128)}, f32[288,768]{1,0:T(8,128)}) custom-call(bf16[224,768]{1,0:T(8,128)(2,1)S(1)} %shard_map.160.refs_0_, bf16[224,768]{1,0:T(8,128)(2,1)S(1)} %collective-permute-done.33.refs_1_, bf16[224,768]{1,0:T(8,128)(2,1)S(1)} %shard_map.162.refs_2_, bf16[224,768]{1,0:T(8,128)(2,1)S(1)} %collective-permute-done.38.refs_3_), custom_call_target="tpu_custom_call" | custom-call | tf_op jit(solution)/shard_map/pallas_call | solution.py:40
  145.6 9.7 %collective-permute-done.18 = f32[208,64]{1,0:T(8,128)S(1)} collective-permute-done((f32[208,64]{1,0:T(8,128)S(1)}, f32[208,64]{1,0:T(8,128)S(1)}, u32[]{:S(2)}, u32[]{:S(2)}) %collective-permute-start.18) | collective-permute-done | bytes 53280 | tf_op jit(solution)/shard_map/ppermute | solution.py:551
  (112 shorter events, 42.6 us)
Async XLA Ops:
  23.1 12.1 %collective-permute-start.8 = (bf16[384,512]{1,0:T(8,128)(2,1)S(1)}, bf16[384,512]{1,0:T(8,128)(2,1)S(1)}, u32[]{:S(2)}, u32[]{:S(2)}) collective-permute-start(bf16[384,512]{1,0:T(8,128)(2,1)S(1)} %add_convert_fusion.3), channel_id=1, source_target_pairs={{0,2},{1,3},{2,0},{3,1},{4,6},{5,7},{6,4},{7,5},{8,10},{9,11},{10,... | collective-permute-start | bytes 1179656 | tf_op jit(solution)/shard_map/ppermute | solution.py:551
  24.1 14.7 %collective-permute-start.11 = (bf16[192,512]{1,0:T(8,128)(2,1)S(1)}, bf16[192,512]{1,0:T(8,128)(2,1)S(1)}, u32[]{:S(2)}, u32[]{:S(2)}) collective-permute-start(bf16[192,512]{1,0:T(8,128)(2,1)S(1)} %bitcast.30), channel_id=1, source_target_pairs={{0,2},{1,3},{2,0},{3,1},{4,6},{5,7},{6,4},{7,5},{8,10},{9,11},{10,... | collective-permute-start | bytes 589832 | tf_op jit(solution)/shard_map/ppermute | solution.py:551
  45.9 11.2 %collective-permute-start.14 = (bf16[384,512]{1,0:T(8,128)(2,1)S(1)}, bf16[384,512]{1,0:T(8,128)(2,1)S(1)}, u32[]{:S(2)}, u32[]{:S(2)}) collective-permute-start(bf16[384,512]{1,0:T(8,128)(2,1)S(1)} %add_convert_fusion.1), channel_id=1, source_target_pairs={{0,2},{1,3},{2,0},{3,1},{4,6},{5,7},{6,4},{7,5},{8,10},{9,11},{10,... | collective-permute-start | bytes 1179656 | tf_op jit(solution)/shard_map/ppermute | solution.py:551
  68.6 22.4 %collective-permute-start.16 = (bf16[400,1152]{1,0:T(8,128)(2,1)S(1)}, bf16[400,1152]{1,0:T(8,128)(2,1)S(1)}, u32[]{:S(2)}, u32[]{:S(2)}) collective-permute-start(bf16[400,1152]{1,0:T(8,128)(2,1)S(1)} %get-tuple-element.92), channel_id=1, source_target_pairs={{0,1},{1,0},{2,3},{3,2},{4,5},{5,4},{6,7},{7,6},{8,9},{9,8},{10,11... | collective-permute-start | bytes 2764808 | tf_op jit(solution)/shard_map/ppermute | solution.py:551
  69.9 10.4 %collective-permute-start.29 = (bf16[224,768]{1,0:T(8,128)(2,1)S(1)}, bf16[224,768]{1,0:T(8,128)(2,1)S(1)}, u32[]{:S(2)}, u32[]{:S(2)}) collective-permute-start(bf16[224,768]{1,0:T(8,128)(2,1)S(1)} %get-tuple-element.121), channel_id=1, source_target_pairs={{0,4},{4,0},{1,5},{5,1},{2,6},{6,2},{3,7},{7,3},{8,12},{12,8},{9,1... | collective-permute-start | bytes 1032200 | tf_op jit(solution)/shard_map/ppermute | solution.py:551
  71.5 10.6 %collective-permute-start.34 = (bf16[224,768]{1,0:T(8,128)(2,1)S(1)}, bf16[224,768]{1,0:T(8,128)(2,1)S(1)}, u32[]{:S(2)}, u32[]{:S(2)}) collective-permute-start(bf16[224,768]{1,0:T(8,128)(2,1)S(1)} %get-tuple-element.125), channel_id=1, source_target_pairs={{0,8},{8,0},{16,24},{24,16},{1,9},{9,1},{17,25},{25,17},{2,10},{10... | collective-permute-start | bytes 1032200 | tf_op jit(solution)/shard_map/ppermute | solution.py:551
  82.4 9.9 %collective-permute-start.35 = (bf16[112,768]{1,0:T(8,128)(2,1)S(1)}, bf16[112,768]{1,0:T(8,128)(2,1)S(1)}, u32[]{:S(2)}, u32[]{:S(2)}) collective-permute-start(bf16[112,768]{1,0:T(8,128)(2,1)S(1)} %get-tuple-element.127), channel_id=1, source_target_pairs={{0,4},{4,0},{1,5},{5,1},{2,6},{6,2},{3,7},{7,3},{8,12},{12,8},{9,1... | collective-permute-start | bytes 516104 | tf_op jit(solution)/shard_map/ppermute | solution.py:551
  86.4 14.3 %collective-permute-start.31 = (bf16[112,768]{1,0:T(8,128)(2,1)S(1)}, bf16[112,768]{1,0:T(8,128)(2,1)S(1)}, u32[]{:S(2)}, u32[]{:S(2)}) collective-permute-start(bf16[112,768]{1,0:T(8,128)(2,1)S(1)} %add_convert_fusion.7), channel_id=1, source_target_pairs={{0,16},{8,24},{16,0},{24,8},{1,17},{9,25},{17,1},{25,9},{2,18},{10... | collective-permute-start | bytes 516104 | tf_op jit(solution)/shard_map/ppermute | solution.py:551
  89.0 11.9 %collective-permute-start.19 = (bf16[192,768]{1,0:T(8,128)(2,1)S(1)}, bf16[192,768]{1,0:T(8,128)(2,1)S(1)}, u32[]{:S(2)}, u32[]{:S(2)}) collective-permute-start(bf16[192,768]{1,0:T(8,128)(2,1)S(1)} %get-tuple-element.103), channel_id=1, source_target_pairs={{0,4},{4,0},{1,5},{5,1},{2,6},{6,2},{3,7},{7,3},{8,12},{12,8},{9,1... | collective-permute-start | bytes 884744 | tf_op jit(solution)/shard_map/ppermute | solution.py:551
  90.5 12.5 %collective-permute-start.24 = (bf16[192,768]{1,0:T(8,128)(2,1)S(1)}, bf16[192,768]{1,0:T(8,128)(2,1)S(1)}, u32[]{:S(2)}, u32[]{:S(2)}) collective-permute-start(bf16[192,768]{1,0:T(8,128)(2,1)S(1)} %get-tuple-element.107), channel_id=1, source_target_pairs={{0,4},{4,0},{1,5},{5,1},{2,6},{6,2},{3,7},{7,3},{8,12},{12,8},{9,1... | collective-permute-start | bytes 884744 | tf_op jit(solution)/shard_map/ppermute | solution.py:551
  91.3 14.6 %collective-permute-start.17 = (bf16[208,1152]{1,0:T(8,128)(2,1)S(1)}, bf16[208,1152]{1,0:T(8,128)(2,1)S(1)}, u32[]{:S(2)}, u32[]{:S(2)}) collective-permute-start(bf16[208,1152]{1,0:T(8,128)(2,1)S(1)} %get-tuple-element.94), channel_id=1, source_target_pairs={{0,2},{1,3},{2,0},{3,1},{4,6},{5,7},{6,4},{7,5},{8,10},{9,11},{10,... | collective-permute-start | bytes 1437704 | tf_op jit(solution)/shard_map/ppermute | solution.py:551
  92.4 11.9 %collective-permute-start.36 = (bf16[112,768]{1,0:T(8,128)(2,1)S(1)}, bf16[112,768]{1,0:T(8,128)(2,1)S(1)}, u32[]{:S(2)}, u32[]{:S(2)}) collective-permute-start(bf16[112,768]{1,0:T(8,128)(2,1)S(1)} %add_convert_fusion.5), channel_id=1, source_target_pairs={{0,16},{8,24},{16,0},{24,8},{1,17},{9,25},{17,1},{25,9},{2,18},{10... | collective-permute-start | bytes 516104 | tf_op jit(solution)/shard_map/ppermute | solution.py:551
  100.7 29.6 %collective-permute-start.32 = (bf16[112,768]{1,0:T(8,128)(2,1)S(1)}, bf16[112,768]{1,0:T(8,128)(2,1)S(1)}, u32[]{:S(2)}, u32[]{:S(2)}) collective-permute-start(bf16[112,768]{1,0:T(8,128)(2,1)S(1)} %add_convert_fusion.6.mine), channel_id=1, source_target_pairs={{0,8},{8,0},{16,24},{24,16},{1,9},{9,1},{17,25},{25,17},{2,10},{10... | collective-permute-start | bytes 516104 | tf_op jit(solution)/shard_map/ppermute | solution.py:551
  101.0 14.0 %collective-permute-start.20 = (bf16[96,768]{1,0:T(8,128)(2,1)S(1)}, bf16[96,768]{1,0:T(8,128)(2,1)S(1)}, u32[]{:S(2)}, u32[]{:S(2)}) collective-permute-start(bf16[96,768]{1,0:T(8,128)(2,1)S(1)} %get-tuple-element.105), channel_id=1, source_target_pairs={{0,8},{8,0},{16,24},{24,16},{1,9},{9,1},{17,25},{25,17},{2,10},{10... | collective-permute-start | bytes 442376 | tf_op jit(solution)/shard_map/ppermute | solution.py:551
  103.1 10.3 %collective-permute-start.25 = (bf16[96,768]{1,0:T(8,128)(2,1)S(1)}, bf16[96,768]{1,0:T(8,128)(2,1)S(1)}, u32[]{:S(2)}, u32[]{:S(2)}) collective-permute-start(bf16[96,768]{1,0:T(8,128)(2,1)S(1)} %get-tuple-element.109), channel_id=1, source_target_pairs={{0,8},{8,0},{16,24},{24,16},{1,9},{9,1},{17,25},{25,17},{2,10},{10... | collective-permute-start | bytes 442376 | tf_op jit(solution)/shard_map/ppermute | solution.py:551
  104.4 27.5 %collective-permute-start.37 = (bf16[112,768]{1,0:T(8,128)(2,1)S(1)}, bf16[112,768]{1,0:T(8,128)(2,1)S(1)}, u32[]{:S(2)}, u32[]{:S(2)}) collective-permute-start(bf16[112,768]{1,0:T(8,128)(2,1)S(1)} %add_convert_fusion.4.mine), channel_id=1, source_target_pairs={{0,4},{4,0},{1,5},{5,1},{2,6},{6,2},{3,7},{7,3},{8,12},{12,8},{9,1... | collective-permute-start | bytes 516104 | tf_op jit(solution)/shard_map/ppermute | solution.py:551
  113.4 14.7 %collective-permute-start.26 = (bf16[112,768]{1,0:T(8,128)(2,1)S(1)}, bf16[112,768]{1,0:T(8,128)(2,1)S(1)}, u32[]{:S(2)}, u32[]{:S(2)}) collective-permute-start(bf16[112,768]{1,0:T(8,128)(2,1)S(1)} %shard_map.155), channel_id=1, source_target_pairs={{0,16},{8,24},{16,0},{24,8},{1,17},{9,25},{17,1},{25,9},{2,18},{10... | collective-permute-start | bytes 516104 | tf_op jit(solution)/shard_map/ppermute | solution.py:551
  115.1 14.8 %collective-permute-start.21 = (bf16[96,768]{1,0:T(8,128)(2,1)S(1)}, bf16[96,768]{1,0:T(8,128)(2,1)S(1)}, u32[]{:S(2)}, u32[]{:S(2)}) collective-permute-start(bf16[96,768]{1,0:T(8,128)(2,1)S(1)} %add_convert_fusion.10), channel_id=1, source_target_pairs={{0,16},{8,24},{16,0},{24,8},{1,17},{9,25},{17,1},{25,9},{2,18},{10... | collective-permute-start | bytes 442376 | tf_op jit(solution)/shard_map/ppermute | solution.py:551
  128.2 12.0 %collective-permute-start.27 = (bf16[112,768]{1,0:T(8,128)(2,1)S(1)}, bf16[112,768]{1,0:T(8,128)(2,1)S(1)}, u32[]{:S(2)}, u32[]{:S(2)}) collective-permute-start(bf16[112,768]{1,0:T(8,128)(2,1)S(1)} %add_convert_fusion.8.mine), channel_id=1, source_target_pairs={{0,8},{8,0},{16,24},{24,16},{1,9},{9,1},{17,25},{25,17},{2,10},{10... | collective-permute-start | bytes 516104 | tf_op jit(solution)/shard_map/ppermute | solution.py:551
  130.4 12.0 %collective-permute-start.33 = (bf16[224,768]{1,0:T(8,128)(2,1)S(1)}, bf16[224,768]{1,0:T(8,128)(2,1)S(1)}, u32[]{:S(2)}, u32[]{:S(2)}) collective-permute-start(bf16[224,768]{1,0:T(8,128)(2,1)S(1)} %shard_map.160.refs_0_), channel_id=1, source_target_pairs={{0,4},{4,0},{1,5},{5,1},{2,6},{6,2},{3,7},{7,3},{8,12},{12,8},{9,1... | collective-permute-start | bytes 1032200 | tf_op jit(solution)/shard_map/ppermute | solution.py:551
  131.9 12.0 %collective-permute-start.38 = (bf16[224,768]{1,0:T(8,128)(2,1)S(1)}, bf16[224,768]{1,0:T(8,128)(2,1)S(1)}, u32[]{:S(2)}, u32[]{:S(2)}) collective-permute-start(bf16[224,768]{1,0:T(8,128)(2,1)S(1)} %shard_map.162.refs_2_), channel_id=1, source_target_pairs={{0,8},{8,0},{16,24},{24,16},{1,9},{9,1},{17,25},{25,17},{2,10},{10... | collective-permute-start | bytes 1032200 | tf_op jit(solution)/shard_map/ppermute | solution.py:551
  138.7 17.6 %collective-permute-start.23 = (bf16[192,768]{1,0:T(8,128)(2,1)S(1)}, bf16[192,768]{1,0:T(8,128)(2,1)S(1)}, u32[]{:S(2)}, u32[]{:S(2)}) collective-permute-start(bf16[192,768]{1,0:T(8,128)(2,1)S(1)} %shard_map.153.refs_0_), channel_id=1, source_target_pairs={{0,4},{4,0},{1,5},{5,1},{2,6},{6,2},{3,7},{7,3},{8,12},{12,8},{9,1... | collective-permute-start | bytes 884744 | tf_op jit(solution)/shard_map/ppermute | solution.py:551
  140.2 16.1 %collective-permute-start.28 = (bf16[208,768]{1,0:T(8,128)(2,1)S(1)}, bf16[208,768]{1,0:T(8,128)(2,1)S(1)}, u32[]{:S(2)}, u32[]{:S(2)}) collective-permute-start(bf16[208,768]{1,0:T(8,128)(2,1)S(1)} %shard_map.156.refs_2_), channel_id=1, source_target_pairs={{0,4},{4,0},{1,5},{5,1},{2,6},{6,2},{3,7},{7,3},{8,12},{12,8},{9,1... | collective-permute-start | bytes 958472 | tf_op jit(solution)/shard_map/ppermute | solution.py:551
  141.0 14.4 %collective-permute-start.18 = (f32[208,64]{1,0:T(8,128)S(1)}, f32[208,64]{1,0:T(8,128)S(1)}, u32[]{:S(2)}, u32[]{:S(2)}) collective-permute-start(f32[208,64]{1,0:T(8,128)S(1)} %slice_select_fusion), channel_id=1, source_target_pairs={{0,4},{4,0},{1,5},{5,1},{2,6},{6,2},{3,7},{7,3},{8,12},{12,8},{9,1... | collective-permute-start | bytes 159752 | tf_op jit(solution)/shard_map/ppermute | solution.py:551
  (20 other events, 141.4 us)

commit v7 on v6

--- a/solution.py
+++ b/solution.py
@@ -455,16 +455,15 @@
     edges[...] = own[:, length:tokens] + got[:, length:tokens].astype(F32)
     weighted = gain_lanes[...], main[0:share, :] * normed[:, 0:length]
     last = edges[0:share, :] * normed[:, length:tokens]
-    exact = functools.partial(
+    rows_of = functools.partial(
         lax.dot_general,
         dimension_numbers=(((1,), (1,)), ((), ())),
-        precision=lax.Precision.HIGHEST,
         preferred_element_type=F32,
     )
-    one = exact(jnp.ones((8, length), F32), weighted[1])
+    one = rows_of(jnp.ones((8, length), F32), weighted[1])
     gains[...] = jnp.zeros(gains.shape, F32)
-    gains[0:8, 0:share] = one + exact(jnp.ones((8, tokens - length), F32), last)
-    gains[8:16, 0:share] = exact(jnp.ones((8, gain_lanes.shape[1]), F32), weighted[0])
+    gains[0:8, 0:share] = one + rows_of(jnp.ones((8, tokens - length), F32), last)
+    gains[8:16, 0:share] = rows_of(jnp.ones((8, gain_lanes.shape[1]), F32), weighted[0])
 
 
 def input_kernel(main, low, high, middle_grad, stats, normed, gain, out):

time: 159 us -> 159 us (level)
  no operation moved by 1% of the time
where the time goes in v7:
time: 159 us; the launch traced here: 158 us
  waiting for transfers between devices  86.4 us (54%)
  starting transfers between devices  37.9 us (24%)
  Pallas kernels  28.7 us (18%)
  other arithmetic  2.34 us (1%)
  local copies, waits for them, and re-layouts  2.16 us (1%)
    ppermute x38, waiting for transfers between devices, flip(): return lax.ppermute(x, axis, [(i, i ^ bit) for i in range(count)])  86.4 us
    ppermute x38, starting transfers between devices, flip(): return lax.ppermute(x, axis, [(i, i ^ bit) for i in range(count)])  34 us
    pallas_call x21, Pallas kernels, call(): return run(*args)  28.7 us
    ppermute x1, starting transfers between devices, gather_edges(): far = lax.ppermute(edge, ('seq', 'mp'), pairs)  3.99 us
  transfers between devices with their start and end apart: 39, of which 19 were waited for; matrix products, arithmetic and copies ran while one was open for 2% of the time, Pallas kernels for 4%

profile of v7, /device:TPU:0, one launch (start us, length us, event | category | flops | bytes accessed | tf_op | source)
XLA Modules:
  0.0 158.5 jit_solution(15966689709846986215)
XLA Ops:
  1.6 4.0 %collective-permute-start.5 = (bf16[192,64]{1,0:T(8,128)(2,1)S(1)}, bf16[192,64]{1,0:T(8,128)(2,1)S(1)}, u32[]{:S(2)}, u32[]{:S(2)}) collective-permute-start(bf16[192,64]{1,0:T(8,128)(2,1)S(1)} %slice_select_fusion.1), channel_id=1, source_target_pairs={{0,6},{1,7},{2,4},{3,5},{4,2},{5,3},{6,0},{7,1},{8,14},{9,15},{10,... | collective-permute-start | bytes 73736 | tf_op jit(solution)/shard_map/ppermute | solution.py:655
  9.6 2.7 %collective-permute-done.1.p2 = bf16[192,512]{1,0:T(8,128)(2,1)S(1)} collective-permute-done((bf16[192,512]{1,0:T(8,128)(2,1)}, bf16[192,512]{1,0:T(8,128)(2,1)S(1)}, u32[]{:S(2)}, u32[]{:S(2)}) %collective-permute-start.1) | collective-permute-done | bytes 196640 | tf_op jit(solution)/shard_map/ppermute | solution.py:550
  13.9 7.3 %shard_map.143 = (bf16[768,640]{1,0:T(8,128)(2,1)S(1)}, f32[8,640]{1,0:T(8,128)S(1)}, bf16[768,640]{1,0:T(8,128)(2,1)S(1)}, bf16[192,512]{1,0:T(8,128)(2,1)S(1)}...) custom-call(bf16[192,512]{1,0:T(8,128)(2,1)S(1)} %collective-permute, ...), custom_call_target="tpu_custom_call" | custom-call | tf_op jit(solution)/shard_map/pallas_call | solution.py:40
  25.2 10.0 %collective-permute-done.8 = bf16[384,512]{1,0:T(8,128)(2,1)S(1)} collective-permute-done((bf16[384,512]{1,0:T(8,128)(2,1)S(1)}, bf16[384,512]{1,0:T(8,128)(2,1)S(1)}, u32[]{:S(2)}, u32[]{:S(2)}) %collective-permute-start.8) | collective-permute-done | bytes 393248 | tf_op jit(solution)/shard_map/ppermute | solution.py:550
  35.9 2.9 %collective-permute-done.11.u2 = bf16[192,512]{1,0:T(8,128)(2,1)S(1)} collective-permute-done((bf16[192,512]{1,0:T(8,128)(2,1)S(1)}, bf16[192,512]{1,0:T(8,128)(2,1)S(1)}, u32[]{:S(2)}, u32[]{:S(2)}) %collective-permute-start.11) | collective-permute-done | bytes 196640 | tf_op jit(solution)/shard_map/ppermute | solution.py:550
  40.2 3.7 %shard_map.145 = (f32[192,512]{1,0:T(8,128)S(1)}, f32[768,512]{1,0:T(8,128)S(1)}, f32[8,512]{1,0:T(8,128)S(1)}, bf16[768,512]{1,0:T(8,128)(2,1)S(1)}, bf16[768,5...) custom-call(bf16[768,640]{1,0:T(8,128)(2,1)S(1)} %get-tuple-element., ...), custom_call_target="tpu_custom_call" | custom-call | tf_op jit(solution)/shard_map/pallas_call | solution.py:40
  44.2 1.6 collective-permute-done.13
  46.8 10.2 %collective-permute-done.14 = bf16[384,512]{1,0:T(8,128)(2,1)S(1)} collective-permute-done((bf16[384,512]{1,0:T(8,128)(2,1)S(1)}, bf16[384,512]{1,0:T(8,128)(2,1)S(1)}, u32[]{:S(2)}, u32[]{:S(2)}) %collective-permute-start.14) | collective-permute-done | bytes 393248 | tf_op jit(solution)/shard_map/ppermute | solution.py:550
  57.3 1.7 %collective-permute-done.15.other = bf16[384,512]{1,0:T(8,128)(2,1)S(1)} collective-permute-done((bf16[384,512]{1,0:T(8,128)(2,1)S(1)}, bf16[384,512]{1,0:T(8,128)(2,1)S(1)}, u32[]{:S(2)}, u32[]{:S(2)}) %collective-permute-start.15) | collective-permute-done | bytes 393248 | tf_op jit(solution)/shard_map/ppermute | solution.py:550
  59.0 6.6 %shard_map.146 = (f32[192,512]{1,0:T(8,128)S(1)}, f32[192,128]{1,0:T(8,128)S(1)}, bf16[576,640]{1,0:T(8,128)(2,1)S(1)}, f32[192,768]{1,0:T(8,128)S(1)}, bf16[192...) custom-call(bf16[384,512]{1,0:T(8,128)(2,1)S(1)} %add_convert_fusion.mine, ...), custom_call_target="tpu_custom_call" | custom-call | tf_op jit(solution)/shard_map/pallas_call | solution.py:40
  65.6 3.0 %shard_map.147 = (f32[400,1152]{1,0:T(8,128)S(1)}, bf16[400,1152]{1,0:T(8,128)(2,1)S(1)}) custom-call(bf16[576,640]{1,0:T(8,128)(2,1)S(1)} %get-tuple-element.86.proj_grad, bf16[768,576]{1,0:T(8,128)(2,1)S(1)} %get-tuple-element.87.w, f32[768,2]{1,0:T(8,128)S(1)} %copy.18.gain, bf16[768,640]{1,0:T(8,128)(2,1)S(1)} %get-tuple-element.69.xall, ...), custom_call_target="tpu_custom_call" | custom-call | tf_op jit(solution)/shard_map/pallas_call | solution.py:40
  73.1 7.3 %collective-permute-done.29.got = bf16[224,768]{1,0:T(8,128)(2,1)S(1)} collective-permute-done((bf16[224,768]{1,0:T(8,128)(2,1)S(1)}, bf16[224,768]{1,0:T(8,128)(2,1)S(1)}, u32[]{:S(2)}, u32[]{:S(2)}) %collective-permute-start.29) | collective-permute-done | bytes 344096 | tf_op jit(solution)/shard_map/ppermute | solution.py:550
  80.5 1.6 %collective-permute-start.30 = (bf16[112,768]{1,0:T(8,128)(2,1)S(1)}, bf16[112,768]{1,0:T(8,128)(2,1)S(1)}, u32[]{:S(2)}, u32[]{:S(2)}) collective-permute-start(bf16[112,768]{1,0:T(8,128)(2,1)S(1)} %get-tuple-element.123), channel_id=1, source_target_pairs={{0,8},{8,0},{16,24},{24,16},{1,9},{9,1},{17,25},{25,17},{2,10},{10... | collective-permute-start | bytes 516104 | tf_op jit(solution)/shard_map/ppermute | solution.py:550
  84.0 2.3 %collective-permute-done.30 = bf16[112,768]{1,0:T(8,128)(2,1)S(1)} collective-permute-done((bf16[112,768]{1,0:T(8,128)(2,1)S(1)}, bf16[112,768]{1,0:T(8,128)(2,1)S(1)}, u32[]{:S(2)}, u32[]{:S(2)}) %collective-permute-start.30) | collective-permute-done | bytes 172064 | tf_op jit(solution)/shard_map/ppermute | solution.py:550
  86.4 2.7 %collective-permute-start.31 = (bf16[112,768]{1,0:T(8,128)(2,1)S(1)}, bf16[112,768]{1,0:T(8,128)(2,1)S(1)}, u32[]{:S(2)}, u32[]{:S(2)}) collective-permute-start(bf16[112,768]{1,0:T(8,128)(2,1)S(1)} %add_convert_fusion.7), channel_id=1, source_target_pairs={{0,16},{8,24},{16,0},{24,8},{1,17},{9,25},{17,1},{25,9},{2,18},{10... | collective-permute-start | bytes 516104 | tf_op jit(solution)/shard_map/ppermute | solution.py:550
  92.7 8.0 %collective-permute-done.31 = bf16[112,768]{1,0:T(8,128)(2,1)S(1)} collective-permute-done((bf16[112,768]{1,0:T(8,128)(2,1)S(1)}, bf16[112,768]{1,0:T(8,128)(2,1)S(1)}, u32[]{:S(2)}, u32[]{:S(2)}) %collective-permute-start.31) | collective-permute-done | bytes 172064 | tf_op jit(solution)/shard_map/ppermute | solution.py:550
  101.0 2.0 %collective-permute-start.20 = (bf16[96,768]{1,0:T(8,128)(2,1)S(1)}, bf16[96,768]{1,0:T(8,128)(2,1)S(1)}, u32[]{:S(2)}, u32[]{:S(2)}) collective-permute-start(bf16[96,768]{1,0:T(8,128)(2,1)S(1)} %get-tuple-element.105), channel_id=1, source_target_pairs={{0,8},{8,0},{16,24},{24,16},{1,9},{9,1},{17,25},{25,17},{2,10},{10... | collective-permute-start | bytes 442376 | tf_op jit(solution)/shard_map/ppermute | solution.py:550
  106.9 6.4 %collective-permute-done.25.got = bf16[96,768]{1,0:T(8,128)(2,1)S(1)} collective-permute-done((bf16[96,768]{1,0:T(8,128)(2,1)S(1)}, bf16[96,768]{1,0:T(8,128)(2,1)S(1)}, u32[]{:S(2)}, u32[]{:S(2)}) %collective-permute-start.25) | collective-permute-done | bytes 147488 | tf_op jit(solution)/shard_map/ppermute | solution.py:550
  113.4 1.6 %collective-permute-start.26 = (bf16[112,768]{1,0:T(8,128)(2,1)S(1)}, bf16[112,768]{1,0:T(8,128)(2,1)S(1)}, u32[]{:S(2)}, u32[]{:S(2)}) collective-permute-start(bf16[112,768]{1,0:T(8,128)(2,1)S(1)} %shard_map.155), channel_id=1, source_target_pairs={{0,16},{8,24},{16,0},{24,8},{1,17},{9,25},{17,1},{25,9},{2,18},{10... | collective-permute-start | bytes 516104 | tf_op jit(solution)/shard_map/ppermute | solution.py:550
  116.5 11.6 %collective-permute-done.26 = bf16[112,768]{1,0:T(8,128)(2,1)S(1)} collective-permute-done((bf16[112,768]{1,0:T(8,128)(2,1)S(1)}, bf16[112,768]{1,0:T(8,128)(2,1)S(1)}, u32[]{:S(2)}, u32[]{:S(2)}) %collective-permute-start.26) | collective-permute-done | bytes 172064 | tf_op jit(solution)/shard_map/ppermute | solution.py:550
  131.9 1.6 %collective-permute-start.38 = (bf16[224,768]{1,0:T(8,128)(2,1)S(1)}, bf16[224,768]{1,0:T(8,128)(2,1)S(1)}, u32[]{:S(2)}, u32[]{:S(2)}) collective-permute-start(bf16[224,768]{1,0:T(8,128)(2,1)S(1)} %shard_map.162.refs_2_), channel_id=1, source_target_pairs={{0,8},{8,0},{16,24},{24,16},{1,9},{9,1},{17,25},{25,17},{2,10},{10... | collective-permute-start | bytes 1032200 | tf_op jit(solution)/shard_map/ppermute | solution.py:550
  133.5 5.1 %collective-permute-done.22.other = bf16[96,768]{1,0:T(8,128)(2,1)S(1)} collective-permute-done((bf16[96,768]{1,0:T(8,128)(2,1)S(1)}, bf16[96,768]{1,0:T(8,128)(2,1)S(1)}, u32[]{:S(2)}, u32[]{:S(2)}) %collective-permute-start.22) | collective-permute-done | bytes 147488 | tf_op jit(solution)/shard_map/ppermute | solution.py:550
  143.9 1.7 %shard_map.163 = (f32[576,768]{1,0:T(8,128)}, f32[288,768]{1,0:T(8,128)}) custom-call(bf16[224,768]{1,0:T(8,128)(2,1)S(1)} %shard_map.160.refs_0_, bf16[224,768]{1,0:T(8,128)(2,1)S(1)} %collective-permute-done.33.refs_1_, bf16[224,768]{1,0:T(8,128)(2,1)S(1)} %shard_map.162.refs_2_, bf16[224,768]{1,0:T(8,128)(2,1)S(1)} %collective-permute-done.38.refs_3_), custom_call_target="tpu_custom_call" | custom-call | tf_op jit(solution)/shard_map/pallas_call | solution.py:40
  145.6 9.7 %collective-permute-done.18 = f32[208,64]{1,0:T(8,128)S(1)} collective-permute-done((f32[208,64]{1,0:T(8,128)S(1)}, f32[208,64]{1,0:T(8,128)S(1)}, u32[]{:S(2)}, u32[]{:S(2)}) %collective-permute-start.18) | collective-permute-done | bytes 53280 | tf_op jit(solution)/shard_map/ppermute | solution.py:550
  (112 shorter events, 42.2 us)
Async XLA Ops:
  23.1 12.1 %collective-permute-start.8 = (bf16[384,512]{1,0:T(8,128)(2,1)S(1)}, bf16[384,512]{1,0:T(8,128)(2,1)S(1)}, u32[]{:S(2)}, u32[]{:S(2)}) collective-permute-start(bf16[384,512]{1,0:T(8,128)(2,1)S(1)} %add_convert_fusion.3), channel_id=1, source_target_pairs={{0,2},{1,3},{2,0},{3,1},{4,6},{5,7},{6,4},{7,5},{8,10},{9,11},{10,... | collective-permute-start | bytes 1179656 | tf_op jit(solution)/shard_map/ppermute | solution.py:550
  24.1 14.7 %collective-permute-start.11 = (bf16[192,512]{1,0:T(8,128)(2,1)S(1)}, bf16[192,512]{1,0:T(8,128)(2,1)S(1)}, u32[]{:S(2)}, u32[]{:S(2)}) collective-permute-start(bf16[192,512]{1,0:T(8,128)(2,1)S(1)} %bitcast.30), channel_id=1, source_target_pairs={{0,2},{1,3},{2,0},{3,1},{4,6},{5,7},{6,4},{7,5},{8,10},{9,11},{10,... | collective-permute-start | bytes 589832 | tf_op jit(solution)/shard_map/ppermute | solution.py:550
  45.9 11.2 %collective-permute-start.14 = (bf16[384,512]{1,0:T(8,128)(2,1)S(1)}, bf16[384,512]{1,0:T(8,128)(2,1)S(1)}, u32[]{:S(2)}, u32[]{:S(2)}) collective-permute-start(bf16[384,512]{1,0:T(8,128)(2,1)S(1)} %add_convert_fusion.1), channel_id=1, source_target_pairs={{0,2},{1,3},{2,0},{3,1},{4,6},{5,7},{6,4},{7,5},{8,10},{9,11},{10,... | collective-permute-start | bytes 1179656 | tf_op jit(solution)/shard_map/ppermute | solution.py:550
  68.6 22.4 %collective-permute-start.16 = (bf16[400,1152]{1,0:T(8,128)(2,1)S(1)}, bf16[400,1152]{1,0:T(8,128)(2,1)S(1)}, u32[]{:S(2)}, u32[]{:S(2)}) collective-permute-start(bf16[400,1152]{1,0:T(8,128)(2,1)S(1)} %get-tuple-element.92), channel_id=1, source_target_pairs={{0,1},{1,0},{2,3},{3,2},{4,5},{5,4},{6,7},{7,6},{8,9},{9,8},{10,11... | collective-permute-start | bytes 2764808 | tf_op jit(solution)/shard_map/ppermute | solution.py:550
  69.9 10.4 %collective-permute-start.29 = (bf16[224,768]{1,0:T(8,128)(2,1)S(1)}, bf16[224,768]{1,0:T(8,128)(2,1)S(1)}, u32[]{:S(2)}, u32[]{:S(2)}) collective-permute-start(bf16[224,768]{1,0:T(8,128)(2,1)S(1)} %get-tuple-element.121), channel_id=1, source_target_pairs={{0,4},{4,0},{1,5},{5,1},{2,6},{6,2},{3,7},{7,3},{8,12},{12,8},{9,1... | collective-permute-start | bytes 1032200 | tf_op jit(solution)/shard_map/ppermute | solution.py:550
  71.5 10.6 %collective-permute-start.34 = (bf16[224,768]{1,0:T(8,128)(2,1)S(1)}, bf16[224,768]{1,0:T(8,128)(2,1)S(1)}, u32[]{:S(2)}, u32[]{:S(2)}) collective-permute-start(bf16[224,768]{1,0:T(8,128)(2,1)S(1)} %get-tuple-element.125), channel_id=1, source_target_pairs={{0,8},{8,0},{16,24},{24,16},{1,9},{9,1},{17,25},{25,17},{2,10},{10... | collective-permute-start | bytes 1032200 | tf_op jit(solution)/shard_map/ppermute | solution.py:550
  82.4 9.9 %collective-permute-start.35 = (bf16[112,768]{1,0:T(8,128)(2,1)S(1)}, bf16[112,768]{1,0:T(8,128)(2,1)S(1)}, u32[]{:S(2)}, u32[]{:S(2)}) collective-permute-start(bf16[112,768]{1,0:T(8,128)(2,1)S(1)} %get-tuple-element.127), channel_id=1, source_target_pairs={{0,4},{4,0},{1,5},{5,1},{2,6},{6,2},{3,7},{7,3},{8,12},{12,8},{9,1... | collective-permute-start | bytes 516104 | tf_op jit(solution)/shard_map/ppermute | solution.py:550
  86.4 14.3 %collective-permute-start.31 = (bf16[112,768]{1,0:T(8,128)(2,1)S(1)}, bf16[112,768]{1,0:T(8,128)(2,1)S(1)}, u32[]{:S(2)}, u32[]{:S(2)}) collective-permute-start(bf16[112,768]{1,0:T(8,128)(2,1)S(1)} %add_convert_fusion.7), channel_id=1, source_target_pairs={{0,16},{8,24},{16,0},{24,8},{1,17},{9,25},{17,1},{25,9},{2,18},{10... | collective-permute-start | bytes 516104 | tf_op jit(solution)/shard_map/ppermute | solution.py:550
  89.0 11.9 %collective-permute-start.19 = (bf16[192,768]{1,0:T(8,128)(2,1)S(1)}, bf16[192,768]{1,0:T(8,128)(2,1)S(1)}, u32[]{:S(2)}, u32[]{:S(2)}) collective-permute-start(bf16[192,768]{1,0:T(8,128)(2,1)S(1)} %get-tuple-element.103), channel_id=1, source_target_pairs={{0,4},{4,0},{1,5},{5,1},{2,6},{6,2},{3,7},{7,3},{8,12},{12,8},{9,1... | collective-permute-start | bytes 884744 | tf_op jit(solution)/shard_map/ppermute | solution.py:550
  90.5 12.5 %collective-permute-start.24 = (bf16[192,768]{1,0:T(8,128)(2,1)S(1)}, bf16[192,768]{1,0:T(8,128)(2,1)S(1)}, u32[]{:S(2)}, u32[]{:S(2)}) collective-permute-start(bf16[192,768]{1,0:T(8,128)(2,1)S(1)} %get-tuple-element.107), channel_id=1, source_target_pairs={{0,4},{4,0},{1,5},{5,1},{2,6},{6,2},{3,7},{7,3},{8,12},{12,8},{9,1... | collective-permute-start | bytes 884744 | tf_op jit(solution)/shard_map/ppermute | solution.py:550
  91.3 14.6 %collective-permute-start.17 = (bf16[208,1152]{1,0:T(8,128)(2,1)S(1)}, bf16[208,1152]{1,0:T(8,128)(2,1)S(1)}, u32[]{:S(2)}, u32[]{:S(2)}) collective-permute-start(bf16[208,1152]{1,0:T(8,128)(2,1)S(1)} %get-tuple-element.94), channel_id=1, source_target_pairs={{0,2},{1,3},{2,0},{3,1},{4,6},{5,7},{6,4},{7,5},{8,10},{9,11},{10,... | collective-permute-start | bytes 1437704 | tf_op jit(solution)/shard_map/ppermute | solution.py:550
  92.4 11.9 %collective-permute-start.36 = (bf16[112,768]{1,0:T(8,128)(2,1)S(1)}, bf16[112,768]{1,0:T(8,128)(2,1)S(1)}, u32[]{:S(2)}, u32[]{:S(2)}) collective-permute-start(bf16[112,768]{1,0:T(8,128)(2,1)S(1)} %add_convert_fusion.5), channel_id=1, source_target_pairs={{0,16},{8,24},{16,0},{24,8},{1,17},{9,25},{17,1},{25,9},{2,18},{10... | collective-permute-start | bytes 516104 | tf_op jit(solution)/shard_map/ppermute | solution.py:550
  100.7 29.6 %collective-permute-start.32 = (bf16[112,768]{1,0:T(8,128)(2,1)S(1)}, bf16[112,768]{1,0:T(8,128)(2,1)S(1)}, u32[]{:S(2)}, u32[]{:S(2)}) collective-permute-start(bf16[112,768]{1,0:T(8,128)(2,1)S(1)} %add_convert_fusion.6.mine), channel_id=1, source_target_pairs={{0,8},{8,0},{16,24},{24,16},{1,9},{9,1},{17,25},{25,17},{2,10},{10... | collective-permute-start | bytes 516104 | tf_op jit(solution)/shard_map/ppermute | solution.py:550
  101.0 14.0 %collective-permute-start.20 = (bf16[96,768]{1,0:T(8,128)(2,1)S(1)}, bf16[96,768]{1,0:T(8,128)(2,1)S(1)}, u32[]{:S(2)}, u32[]{:S(2)}) collective-permute-start(bf16[96,768]{1,0:T(8,128)(2,1)S(1)} %get-tuple-element.105), channel_id=1, source_target_pairs={{0,8},{8,0},{16,24},{24,16},{1,9},{9,1},{17,25},{25,17},{2,10},{10... | collective-permute-start | bytes 442376 | tf_op jit(solution)/shard_map/ppermute | solution.py:550
  103.1 10.3 %collective-permute-start.25 = (bf16[96,768]{1,0:T(8,128)(2,1)S(1)}, bf16[96,768]{1,0:T(8,128)(2,1)S(1)}, u32[]{:S(2)}, u32[]{:S(2)}) collective-permute-start(bf16[96,768]{1,0:T(8,128)(2,1)S(1)} %get-tuple-element.109), channel_id=1, source_target_pairs={{0,8},{8,0},{16,24},{24,16},{1,9},{9,1},{17,25},{25,17},{2,10},{10... | collective-permute-start | bytes 442376 | tf_op jit(solution)/shard_map/ppermute | solution.py:550
  104.4 27.5 %collective-permute-start.37 = (bf16[112,768]{1,0:T(8,128)(2,1)S(1)}, bf16[112,768]{1,0:T(8,128)(2,1)S(1)}, u32[]{:S(2)}, u32[]{:S(2)}) collective-permute-start(bf16[112,768]{1,0:T(8,128)(2,1)S(1)} %add_convert_fusion.4.mine), channel_id=1, source_target_pairs={{0,4},{4,0},{1,5},{5,1},{2,6},{6,2},{3,7},{7,3},{8,12},{12,8},{9,1... | collective-permute-start | bytes 516104 | tf_op jit(solution)/shard_map/ppermute | solution.py:550
  113.4 14.7 %collective-permute-start.26 = (bf16[112,768]{1,0:T(8,128)(2,1)S(1)}, bf16[112,768]{1,0:T(8,128)(2,1)S(1)}, u32[]{:S(2)}, u32[]{:S(2)}) collective-permute-start(bf16[112,768]{1,0:T(8,128)(2,1)S(1)} %shard_map.155), channel_id=1, source_target_pairs={{0,16},{8,24},{16,0},{24,8},{1,17},{9,25},{17,1},{25,9},{2,18},{10... | collective-permute-start | bytes 516104 | tf_op jit(solution)/shard_map/ppermute | solution.py:550
  115.1 14.8 %collective-permute-start.21 = (bf16[96,768]{1,0:T(8,128)(2,1)S(1)}, bf16[96,768]{1,0:T(8,128)(2,1)S(1)}, u32[]{:S(2)}, u32[]{:S(2)}) collective-permute-start(bf16[96,768]{1,0:T(8,128)(2,1)S(1)} %add_convert_fusion.10), channel_id=1, source_target_pairs={{0,16},{8,24},{16,0},{24,8},{1,17},{9,25},{17,1},{25,9},{2,18},{10... | collective-permute-start | bytes 442376 | tf_op jit(solution)/shard_map/ppermute | solution.py:550
  128.2 12.0 %collective-permute-start.27 = (bf16[112,768]{1,0:T(8,128)(2,1)S(1)}, bf16[112,768]{1,0:T(8,128)(2,1)S(1)}, u32[]{:S(2)}, u32[]{:S(2)}) collective-permute-start(bf16[112,768]{1,0:T(8,128)(2,1)S(1)} %add_convert_fusion.8.mine), channel_id=1, source_target_pairs={{0,8},{8,0},{16,24},{24,16},{1,9},{9,1},{17,25},{25,17},{2,10},{10... | collective-permute-start | bytes 516104 | tf_op jit(solution)/shard_map/ppermute | solution.py:550
  130.4 12.0 %collective-permute-start.33 = (bf16[224,768]{1,0:T(8,128)(2,1)S(1)}, bf16[224,768]{1,0:T(8,128)(2,1)S(1)}, u32[]{:S(2)}, u32[]{:S(2)}) collective-permute-start(bf16[224,768]{1,0:T(8,128)(2,1)S(1)} %shard_map.160.refs_0_), channel_id=1, source_target_pairs={{0,4},{4,0},{1,5},{5,1},{2,6},{6,2},{3,7},{7,3},{8,12},{12,8},{9,1... | collective-permute-start | bytes 1032200 | tf_op jit(solution)/shard_map/ppermute | solution.py:550
  131.9 12.0 %collective-permute-start.38 = (bf16[224,768]{1,0:T(8,128)(2,1)S(1)}, bf16[224,768]{1,0:T(8,128)(2,1)S(1)}, u32[]{:S(2)}, u32[]{:S(2)}) collective-permute-start(bf16[224,768]{1,0:T(8,128)(2,1)S(1)} %shard_map.162.refs_2_), channel_id=1, source_target_pairs={{0,8},{8,0},{16,24},{24,16},{1,9},{9,1},{17,25},{25,17},{2,10},{10... | collective-permute-start | bytes 1032200 | tf_op jit(solution)/shard_map/ppermute | solution.py:550
  138.7 17.6 %collective-permute-start.23 = (bf16[192,768]{1,0:T(8,128)(2,1)S(1)}, bf16[192,768]{1,0:T(8,128)(2,1)S(1)}, u32[]{:S(2)}, u32[]{:S(2)}) collective-permute-start(bf16[192,768]{1,0:T(8,128)(2,1)S(1)} %shard_map.153.refs_0_), channel_id=1, source_target_pairs={{0,4},{4,0},{1,5},{5,1},{2,6},{6,2},{3,7},{7,3},{8,12},{12,8},{9,1... | collective-permute-start | bytes 884744 | tf_op jit(solution)/shard_map/ppermute | solution.py:550
  140.2 16.1 %collective-permute-start.28 = (bf16[208,768]{1,0:T(8,128)(2,1)S(1)}, bf16[208,768]{1,0:T(8,128)(2,1)S(1)}, u32[]{:S(2)}, u32[]{:S(2)}) collective-permute-start(bf16[208,768]{1,0:T(8,128)(2,1)S(1)} %shard_map.156.refs_2_), channel_id=1, source_target_pairs={{0,4},{4,0},{1,5},{5,1},{2,6},{6,2},{3,7},{7,3},{8,12},{12,8},{9,1... | collective-permute-start | bytes 958472 | tf_op jit(solution)/shard_map/ppermute | solution.py:550
  141.0 14.4 %collective-permute-start.18 = (f32[208,64]{1,0:T(8,128)S(1)}, f32[208,64]{1,0:T(8,128)S(1)}, u32[]{:S(2)}, u32[]{:S(2)}) collective-permute-start(f32[208,64]{1,0:T(8,128)S(1)} %slice_select_fusion), channel_id=1, source_target_pairs={{0,4},{4,0},{1,5},{5,1},{2,6},{6,2},{3,7},{7,3},{8,12},{12,8},{9,1... | collective-permute-start | bytes 159752 | tf_op jit(solution)/shard_map/ppermute | solution.py:550
  (20 other events, 141.4 us)
